TPU v7x, 32 devices: a whole 2x2x4 slice. The times are simulated.
32 devices in a mesh: row: 8 (over y, x, core), col: 4 (over z).
Axes of the slice: x: 2, y: 2, z: 4, core: 2. Of those that a mesh axis runs over, the one named last changes fastest.
Arguments:
- diag_blocks: float32 [16, 512, 512], P('row', None, 'col'), as said below
- near_blocks: float32 [16, 4, 512, 512], P('row', None, None, 'col'), may hold values from -0.1 to 0.1, as said below
- cluster_bases: float32 [16, 512, 512], P('row', 'col'), as said below
- near_ids: int32 [16, 4], P('row'), may hold values from 0 to 15, as said below
- near_count: int32 [16], P('row'), may hold values from 1 to 4
- parent_bases: float32 [8, 512, 512], P('row'), as said below
Outputs:
- leaf_diag: float32 [16, 256, 256], P('row', None, 'col')
- leaf_near: float32 [16, 4, 256, 256], P('row', None, None, 'col')
- parent_diag: float32 [8, 256, 256], P('row', None, 'col')
Inputs may be any that keep to these rules, and one draw needn't show every extreme that they name: `near_ids`: slot 0 of cluster i names its sibling: i + 2 when i // 2 is even, else i - 2. The other slots may name any cluster. For sibling clusters a and b = a + 2 (a // 2 even), near_blocks[b, 0] is the transpose of near_blocks[a, 0]. `diag_blocks`: Symmetric. `cluster_bases`: the identity plus a small full-rank perturbation. `parent_bases`: the identity plus a small full-rank perturbation.
All inputs are finite; a program needn't handle non-finite values.
Results may differ from a plain program's by a relative error of at most 0.0003.
Values sent between devices are 32-bit elements; how exact they have to be, the bound alone decides.
No kernel may reach another device: no remote copies, remote signals or barrier semaphores. Data moves between devices by JAX's collectives and lax.ppermute only.
A program may use at most 128 MiB of HBM per device.

v0:
```python
import jax
import jax.numpy as jnp
from jax import lax
from jax.experimental import pallas as pl
from jax.experimental.pallas import tpu as pltpu
from jax.sharding import PartitionSpec as P


K = 256
PANEL = 8


highest = lax.Precision.HIGHEST


def dot(a, b, left=1, right=0):
    dims = (((left,), (right,)), ((), ()))
    return lax.dot_general(a, b, dims, precision=highest, preferred_element_type=jnp.float32)


def dot3(a, b):
    a_high, b_high = a.astype(jnp.bfloat16), b.astype(jnp.bfloat16)
    a_low = (a - a_high.astype(jnp.float32)).astype(jnp.bfloat16)
    b_low = (b - b_high.astype(jnp.float32)).astype(jnp.bfloat16)

    def product(x, y):
        return jnp.dot(x, y, preferred_element_type=jnp.float32)

    return product(a_high, b_high) + (product(a_high, b_low) + product(a_low, b_high))


def sweep(block):
    size = len(block)
    e = [[block[min(i, j)][max(i, j)] for j in range(size)] for i in range(size)]
    for k in range(size):
        inv = 1.0 / e[k][k]
        t = [e[k][j] * inv for j in range(size)]
        for i in range(size):
            for j in range(i, size):
                if i != k and j != k:
                    e[i][j] = e[i][j] - e[i][k] * t[j]
                    e[j][i] = e[i][j]
        for j in range(size):
            if j != k:
                e[k][j] = e[j][k] = t[j]
        e[k][k] = -inv
    return e


def panel_step(a, lane, sub):
    n = a.shape[0]
    cols = [jnp.broadcast_to(a[:, s : s + 1], (n, n)) for s in range(PANEL)]
    block = [[jnp.broadcast_to(cols[j][i : i + 1], (PANEL, n)) if i <= j else None for j in range(PANEL)] for i in range(PANEL)]
    negated = sweep(block)
    result = jnp.where(lane < PANEL, jnp.where(lane == sub, 1.0, 0.0), a)
    rows = [jnp.broadcast_to(result[t : t + 1], (PANEL, n)) for t in range(PANEL)]
    for s in range(PANEL):
        terms = [negated[s][t] * rows[t] for t in range(PANEL)]
        while len(terms) > 1:
            terms = [terms[i] + terms[i + 1] for i in range(0, len(terms), 2)]
        spread = jnp.concatenate([terms[0]] * (n // PANEL), axis=0)
        top = jnp.where(sub[:PANEL] == s, cols[s][:PANEL] - 1.0, cols[s][:PANEL])
        result = result + jnp.concatenate([top, cols[s][PANEL:]], axis=0) * spread
    return result


def inverse(a):
    n = a.shape[0]
    lane = lax.broadcasted_iota(jnp.int32, (n, n), 1)
    sub = lax.broadcasted_iota(jnp.int32, (n, n), 0)

    def body(_, mat):
        mat = panel_step(mat, lane, sub)
        return pltpu.roll(jnp.concatenate([mat[PANEL:], mat[:PANEL]], axis=0), n - PANEL, 1)

    return lax.fori_loop(0, n // PANEL, body, a)


def solve(corner, right):
    half = corner.shape[0] // 2
    cross, turned = corner[:half, half:], corner[half:, :half]
    first = inverse(corner[:half, :half])
    link, link_turned = dot(first, cross), dot(turned, first)
    second = inverse(corner[half:, half:] - dot(turned, link))
    low = dot(second, right[half:] - dot(link_turned, right[:half]))
    up = dot(first, right[:half]) - dot(link, low)
    return jnp.concatenate([up, low], axis=0)


def eliminate(dense, redundant):
    rr = dense[:redundant, :redundant]
    solved = solve((rr + rr.T) * 0.5, dense[:redundant, redundant:])
    return solved, dense[redundant:, redundant:] - dot(dense[redundant:, :redundant], solved)


def wide(ref, start, count):
    return jnp.concatenate([ref[start + i] for i in range(count)], axis=1)


def leaf_kernel(place, own, near, far2, far3, w_ref, schur_ref):
    z = place[1]
    inner = z & 1
    edge = own.shape[1]
    redundant = 4 * edge - w_ref.shape[1]
    pairs = [jnp.concatenate([own[z ^ m], near[z ^ m]], axis=1) for m in range(4)]
    corner = jnp.concatenate(pairs[:2], axis=0)
    side = jnp.concatenate(pairs[2:], axis=0)
    far = [jnp.concatenate([far2[i], far3[i]], axis=1) for i in (inner, 1 - inner)]
    far = jnp.concatenate(far, axis=0)
    bases = [wide(own, 4, 4), wide(near, 4, 4), wide(far2, 2, 4), wide(far3, 2, 4)]
    u = jnp.concatenate(bases, axis=0)
    ut = u.T
    ut_near, ut_far = ut[:, : 2 * edge], ut[:, 2 * edge :]
    yt_near = dot(ut_near, corner) + dot(ut_far, side)
    yt_far = dot(ut_near, side, 1, 1) + dot(ut_far, far)
    dense = dot(jnp.concatenate([yt_near, yt_far], axis=1), u)
    solved, schur = eliminate(dense, redundant)
    schur_ref[...] = schur
    wt = ut[redundant:] - dot(solved.T, ut[:redundant])
    for m in range(4):
        w_ref[z ^ m] = wt[:, m * edge : (m + 1) * edge]


def pack_kernel(place, diag, bases, full, half, shard):
    edge = bases.shape[1]
    mine = place[1] >> 1
    other = 1 - mine
    for i in range(4):
        lanes = slice(i * edge, (i + 1) * edge)
        full[i] = diag[mine, lanes, :]
        full[4 + i] = bases[mine, :, lanes]
        half[2 + i] = bases[other, :, lanes]
    for i in range(2):
        half[i] = diag[other, pl.ds(pl.multiple_of((2 * mine + i) * edge, edge), edge), :]
    for c in range(bases.shape[0]):
        shard[c] = bases[c, :, bases.shape[2] - shard.shape[2] :]


def skeleton_kernel(place, own, near, far2, far3, out):
    for j, ref in enumerate((own, near, far2, far3)):
        out[j] = wide(ref, ref.shape[0] - 2, 2)


def name_kernel(place, ids, low, high, mine_ref, other_ref):
    row, mine = place[0], place[1] >> 1
    clusters, slots = ids.shape
    for which, out in ((mine, mine_ref), (1 - mine, other_ref)):
        for k in range(1, slots):
            name = ids[which, k]
            apart = lax.div(name, clusters) ^ row
            spot = (apart >> 1) * clusters + lax.rem(name, clusters)
            out[k - 1] = jnp.where((apart & 1) > 0, high[spot], low[spot])


def coupling(w_ref, blocks, bases):
    w = jnp.concatenate([w_ref[b] for b in range(4)], axis=1)
    return dot3(w, dot3(jnp.concatenate(blocks, axis=1), jnp.concatenate(bases, axis=0)))


def tall(ref, start):
    return jnp.concatenate([ref[start + i] for i in range(4)], axis=0)


def deal(z, flipped, index, parts):
    quarter = parts[0].shape[1]
    for j, part in enumerate(parts):
        part[index] = flipped[index, pl.ds(pl.multiple_of((z ^ j) * quarter, quarter), quarter), :]


def near_first_kernel(place, count, w_ref, bases, n0, n1, n2, n3, schur, pair, flipped):
    result = coupling(w_ref, [tall(n, 0) for n in (n0, n1, n2, n3)], [bases[j ^ 1] for j in range(4)])
    result = jnp.where(count[place[1] >> 1] > 0, result, 0.0)
    pair[0] = schur[...]
    pair[1] = result
    flipped[...] = result.T


def near_rest_kernel(place, count, w_ref, schur, first, parent, *refs):
    z = place[1]
    blocks, named, parts, flipped = refs[:4], refs[4:8], refs[8:12], refs[12]
    total = named[0].shape[0]
    flipped[0] = schur[...]
    flipped[1] = first[...]
    for k in range(total):
        result = coupling(w_ref, [tall(n, 4 * k) for n in blocks], [s[k] for s in named])
        flipped[k + 2] = jnp.where(count[z >> 1] > k + 1, result, 0.0).T
    flipped[total + 2] = parent[...]
    for i in range(total + 3):
        deal(z, flipped, i, parts)


def finish_kernel(place, *refs):
    row, z = place[0], place[1]
    parts, (diag, near, final) = refs[:4], refs[4:]
    owner = (z & 1) == (row & 1)
    swap = z >> 1
    last = parts[0].shape[0] - 1

    def sides(i):
        return jnp.where(owner, parts[0][i], parts[1][i]), parts[2][i] + parts[3][i]

    for i in range(last):
        for side, value in zip((swap, 1 - swap), sides(i)):
            if i == 0:
                diag[side] = value
            else:
                near[side, i - 1] = value
    here, there = sides(last)
    final[0] = jnp.where(swap == (row & 1), here, there)


def parent_kernel(place, own, arrived, vt_ref, v_ref, flipped_ref):
    size = own.shape[1]
    swap = (place[0] & 1) > 0

    def choose(a, b, index):
        return jnp.where(swap, b[index], a[index])

    top = jnp.concatenate([choose(own, arrived, 0), choose(own, arrived, 1)], axis=1)
    low = jnp.concatenate([choose(arrived, own, 1), choose(arrived, own, 0)], axis=1)
    merged = jnp.concatenate([top, low], axis=0)
    dense = dot(dot(vt_ref[...], merged), v_ref[...])
    flipped_ref[...] = eliminate(dense, size)[1].T


def call(kernel, outs, scalars, arrays, us=2, scratch=()):
    vmem = pl.BlockSpec(memory_space=pltpu.VMEM)
    specs = [pl.BlockSpec(memory_space=pltpu.SMEM)] * len(scalars) + [vmem] * len(arrays)
    shapes = [jax.ShapeDtypeStruct(shape, jnp.float32) for shape in outs]
    cost = pl.CostEstimate(flops=us * 10**9, bytes_accessed=us * 10**6, transcendentals=0)
    return pl.pallas_call(
        kernel,
        out_shape=shapes,
        in_specs=specs,
        out_specs=[vmem] * len(outs),
        scratch_shapes=[pltpu.VMEM(shape, jnp.float32) for shape in scratch],
        cost_estimate=cost,
    )(*scalars, *arrays)


def pick(array, index):
    return lax.dynamic_index_in_dim(array, index, 0, keepdims=False)


def after(values, ready):
    return lax.optimization_barrier((values, ready))[0]


def levels(diag_blocks, near_blocks, cluster_bases, near_ids, near_count, parent_bases):
    clusters, edge, _ = cluster_bases.shape
    slots = near_blocks.shape[1]
    skeleton = K
    n_row, n_col = lax.axis_size("row"), lax.axis_size("col")
    assert n_col == 2 * clusters == 4 and n_row & (n_row - 1) == 0
    quarter = skeleton // n_col
    row, column = lax.axis_index("row"), lax.axis_index("col")
    place = jnp.stack([row, column]).astype(jnp.int32)
    mine, other = column // 2, 1 - column // 2
    both = ("row", "col")
    owned = [(r, z) for r in range(n_row) for z in range(n_col) if z % 2 == r % 2]
    heads = [(r, (n_col - 1) * (r % 2)) for r in range(n_row)]

    def to_owner(x, j):
        return lax.ppermute(x, both, [(r * n_col + (z ^ j), r * n_col + z) for r, z in owned])

    def from_owner(x, j):
        return lax.ppermute(x, both, [(r * n_col + z, r * n_col + (z ^ j)) for r, z in owned])

    def from_sibling(x, places):
        return lax.ppermute(x, both, [((r ^ 1) * n_col + (z ^ 1), r * n_col + z) for r, z in places])

    def across(x, bit):
        return lax.ppermute(x, "row", [(r, r ^ bit) for r in range(n_row)])

    def gather(x, y):
        got = [x]
        for j, payload in enumerate((x, y, y), 1):
            got.append(to_owner(payload, j))
        return got

    def scatter(parts):
        return [parts[0]] + [from_owner(parts[j], j) for j in range(1, 4)]

    full, half, table = call(
        pack_kernel,
        [(8, edge, edge), (6, edge, edge), (clusters, edge, skeleton)],
        [place],
        [diag_blocks, cluster_bases],
    )
    leaf = gather(full, half)

    bits = [1 << t for t in range(1, n_row.bit_length() - 1)]
    for bit in bits:
        table = jnp.concatenate([table, across(table, bit)], axis=0)

    near = near_blocks.reshape(clusters, slots * 4, edge, edge)
    n_mine, n_other = pick(near, mine), pick(near, other)
    ready = after((n_mine[:4], n_other[:4], n_mine[4:], n_other[4:]), leaf[1:])
    n_early, n_late = gather(*ready[:2]), gather(*ready[2:])
    (skeletons,) = call(skeleton_kernel, [(4, edge, skeleton)], [place], leaf)
    sibling = from_sibling(skeletons, owned)

    w, schur = call(
        leaf_kernel, [(4, skeleton, edge), (skeleton, skeleton)], [place], leaf, 22
    )

    pair, first = call(
        near_first_kernel,
        [(2, skeleton, skeleton), (skeleton, skeleton)],
        [place, near_count],
        [w, sibling, *n_early, schur],
        4,
    )
    arrived = from_sibling(pair, heads)

    table = after(table, w)
    s_mine, s_other = call(
        name_kernel,
        [(slots - 1, edge, skeleton)] * 2,
        [place, near_ids],
        [table, across(table, 1)],
    )
    named = gather(*after((s_mine, s_other), pair))

    v = parent_bases[0]
    (parent,) = call(
        parent_kernel, [(skeleton, skeleton)], [place], [pair, arrived, v.T, v], 22
    )
    total = slots + 2
    results = call(
        near_rest_kernel,
        [(total, quarter, skeleton)] * 4,
        [place, near_count],
        [w, schur, first, parent, *n_late, *named],
        7,
        [(total, skeleton, skeleton)],
    )
    turned = call(
        finish_kernel,
        [(clusters, quarter, skeleton), (clusters, slots, quarter, skeleton), (1, quarter, skeleton)],
        [place],
        scatter(results),
    )
    return tuple(jnp.swapaxes(x, -1, -2) for x in turned)


def solution(mesh):
    return jax.shard_map(
        levels,
        mesh=mesh,
        in_specs=(
            P("row", None, "col"),
            P("row", None, None, "col"),
            P("row", "col", None),
            P("row", None),
            P("row"),
            P("row", None, None),
        ),
        out_specs=(P("row", None, "col"), P("row", None, None, "col"), P("row", None, "col")),
        check_vma=False,
    )
```

profile of v0, /device:TPU:0, one launch (start us, length us, event | category | flops | bytes accessed | tf_op | source)
XLA Modules:
  0.0 171.5 jit_solution(17469230032026589701)
XLA Ops:
  0.6 0.6 pad_add_fusion.place
  1.2 2.4 %shard_map.85 = (f32[8,128,128]{2,1,0:T(8,128)}, f32[6,128,128]{2,1,0:T(8,128)}, f32[2,128,256]{2,1,0:T(8,128)}) custom-call(s32[2]{0:T(128)} %pad_add_fusion.place, f32[2,512,128]{2,1,0:T(8,128)} %diag.1, f32[2,128,512]{2,1,0:T(8,128)} %bases.1), custom_call_target="tpu_custom_call" | custom-call | flops 2000000000 | bytes 2000000 | tf_op jit(solution)/shard_map/pallas_call | solution.py:231
  3.6 1.4 collective-permute-start
  5.1 1.3 collective-permute-start.2
  6.4 6.0 %collective-permute-start.1 = (f32[6,128,128]{2,1,0:T(8,128)}, f32[6,128,128]{2,1,0:T(8,128)}, u32[]{:S(2)}, u32[]{:S(2)}) collective-permute-start(f32[6,128,128]{2,1,0:T(8,128)} %get-tuple-element.27), channel_id=1, source_target_pairs={{2,0},{0,2},{7,5},{5,7},{10,8},{8,10},{15,13},{13,15},{18,16},{16,... | collective-permute-start | bytes 1179656 | tf_op jit(solution)/shard_map/ppermute | solution.py:264
  12.3 1.6 collective-permute-start.11
  13.9 1.2 dynamic-slice_bitcast_fusion
  15.1 6.3 %collective-permute-done.11 = f32[2,128,256]{2,1,0:T(8,128)S(1)} collective-permute-done((f32[2,128,256]{2,1,0:T(8,128)}, f32[2,128,256]{2,1,0:T(8,128)S(1)}, u32[]{:S(2)}, u32[]{:S(2)}) %collective-permute-start.11) | collective-permute-done | bytes 262176 | tf_op jit(solution)/shard_map/ppermute | solution.py:273
  21.5 1.6 collective-permute-start.12
  23.1 4.0 %collective-permute-done.2.far3 = f32[6,128,128]{2,1,0:T(8,128)S(1)} collective-permute-done((f32[6,128,128]{2,1,0:T(8,128)}, f32[6,128,128]{2,1,0:T(8,128)S(1)}, u32[]{:S(2)}, u32[]{:S(2)}) %collective-permute-start.2) | collective-permute-done | bytes 393248 | tf_op jit(solution)/shard_map/ppermute | solution.py:264
  27.1 3.9 %collective-permute-done.1.far2 = f32[6,128,128]{2,1,0:T(8,128)} collective-permute-done((f32[6,128,128]{2,1,0:T(8,128)}, f32[6,128,128]{2,1,0:T(8,128)}, u32[]{:S(2)}, u32[]{:S(2)}) %collective-permute-start.1) | collective-permute-done | bytes 393248 | tf_op jit(solution)/shard_map/ppermute | solution.py:264
  31.0 0.0 collective-permute-done.near
  31.0 2.3 %shard_map.87 = f32[4,128,256]{2,1,0:T(8,128)} custom-call(s32[2]{0:T(128)} %pad_add_fusion.place, f32[8,128,128]{2,1,0:T(8,128)} %get-tuple-element.26.own, f32[8,128,128]{2,1,0:T(8,128)} %collective-permute-done.near, f32[6,128,128]{2,1,0:T(8,128)} %collective-permute-done.1.far2, f32[6,128,128]{2,1,0:T(8,128)} %copy-done.9), custom_call_target="tpu_custom_call" | custom-call | flops 2000000000 | bytes 2000000 | tf_op jit(solution)/shard_map/pallas_call | solution.py:231
  33.2 2.9 %collective-permute-start.3 = (f32[4,128,256]{2,1,0:T(8,128)}, f32[4,128,256]{2,1,0:T(8,128)}, u32[]{:S(2)}, u32[]{:S(2)}) collective-permute-start(f32[4,128,256]{2,1,0:T(8,128)} %shard_map.87), channel_id=1, source_target_pairs={{5,0},{7,2},{0,5},{2,7},{13,8},{15,10},{8,13},{10,15},{21,16},{23,... | collective-permute-start | bytes 1572872 | tf_op jit(solution)/shard_map/ppermute | solution.py:270
  36.1 19.7 %shard_map.86 = (f32[4,256,128]{2,1,0:T(8,128)}, f32[256,256]{1,0:T(8,128)}) custom-call(s32[2]{0:T(128)} %pad_add_fusion.place, f32[8,128,128]{2,1,0:T(8,128)} %get-tuple-element.26.own, f32[8,128,128]{2,1,0:T(8,128)} %collective-permute-done.near, f32[6,128,128]{2,1,0:T(8,128)} %collective-permute-done.1.far2, f32[6,128,128]{2,1,0:T(8,128)} %copy-done.9), custom_call_target="tpu_custom_call" | custom-call | flops 22000001024 | bytes 22000000 | tf_op jit(solution)/shard_map/pallas_call | solution.py:231
  55.8 0.0 collective-permute-done.12
  55.8 1.2 pad_maximum_fusion.low
  57.0 0.1 collective-permute-start.13
  57.2 1.3 collective-permute-start.4
  58.5 1.3 collective-permute-start.6
  59.8 2.6 %collective-permute-start.5 = (f32[4,128,128]{2,1,0:T(8,128)S(1)}, f32[4,128,128]{2,1,0:T(8,128)S(1)}, u32[]{:S(2)}, u32[]{:S(2)}) collective-permute-start(f32[4,128,128]{2,1,0:T(8,128)S(1)} %get-tuple-element.31), channel_id=1, source_target_pairs={{2,0},{0,2},{7,5},{5,7},{10,8},{8,10},{15,13},{13,15},{18,16},{16,... | collective-permute-start | bytes 786440 | tf_op jit(solution)/shard_map/ppermute | solution.py:264
  62.4 3.0 %collective-permute-done.4.n1 = f32[4,128,128]{2,1,0:T(8,128)S(1)} collective-permute-done((f32[4,128,128]{2,1,0:T(8,128)S(1)}, f32[4,128,128]{2,1,0:T(8,128)S(1)}, u32[]{:S(2)}, u32[]{:S(2)}) %collective-permute-start.4) | collective-permute-done | bytes 262176 | tf_op jit(solution)/shard_map/ppermute | solution.py:264
  65.4 1.3 collective-permute-start.8
  66.7 4.7 %collective-permute-done.6.n3 = f32[4,128,128]{2,1,0:T(8,128)S(1)} collective-permute-done((f32[4,128,128]{2,1,0:T(8,128)S(1)}, f32[4,128,128]{2,1,0:T(8,128)S(1)}, u32[]{:S(2)}, u32[]{:S(2)}) %collective-permute-start.6) | collective-permute-done | bytes 262176 | tf_op jit(solution)/shard_map/ppermute | solution.py:264
  71.4 3.5 %collective-permute-done.5.n2 = f32[4,128,128]{2,1,0:T(8,128)S(1)} collective-permute-done((f32[4,128,128]{2,1,0:T(8,128)S(1)}, f32[4,128,128]{2,1,0:T(8,128)S(1)}, u32[]{:S(2)}, u32[]{:S(2)}) %collective-permute-start.5) | collective-permute-done | bytes 262176 | tf_op jit(solution)/shard_map/ppermute | solution.py:264
  75.0 0.7 copy-done.18
  75.6 3.8 %shard_map.88 = (f32[2,256,256]{2,1,0:T(8,128)}, f32[256,256]{1,0:T(8,128)}) custom-call(s32[2]{0:T(128)} %pad_add_fusion.place, s32[2]{0:T(128)} %count.3, f32[4,256,128]{2,1,0:T(8,128)} %get-tuple-element.28.w_ref, f32[4,128,256]{2,1,0:T(8,128)} %collective-permute-done.3.bases, f32[4,128,128]{2,1,0:T(8,128)} %copy-done.6, f32[4,128,128]{2,1,0:T(8,128)} %copy-done.16, ...), custom_call_target="tpu_custom_call" | custom-call | flops 4000000000 | bytes 4000000 | tf_op jit(solution)/shard_map/pallas_call | solution.py:231
  79.4 1.4 collective-permute-start.7
  80.8 1.3 copy.9.vt_ref
  82.1 1.3 collective-permute-start.10
  83.4 4.7 %collective-permute-start.9 = (f32[12,128,128]{2,1,0:T(8,128)S(1)}, f32[12,128,128]{2,1,0:T(8,128)}, u32[]{:S(2)}, u32[]{:S(2)}) collective-permute-start(f32[12,128,128]{2,1,0:T(8,128)S(1)} %copy-done.5), channel_id=1, source_target_pairs={{2,0},{0,2},{7,5},{5,7},{10,8},{8,10},{15,13},{13,15},{18,16},{16,... | collective-permute-start | bytes 2359304 | tf_op jit(solution)/shard_map/ppermute | solution.py:264
  88.2 2.5 %shard_map.90 = (f32[3,128,256]{2,1,0:T(8,128)}, f32[3,128,256]{2,1,0:T(8,128)}) custom-call(s32[2]{0:T(128)} %pad_add_fusion.place, s32[2,4]{1,0:T(2,128)} %ids.1, f32[8,128,256]{2,1,0:T(8,128)} %copy-done.2, f32[8,128,256]{2,1,0:T(8,128)} %collective-permute-done.13.high), custom_call_target="tpu_custom_call" | custom-call | flops 2000000000 | bytes 2000000 | tf_op jit(solution)/shard_map/pallas_call | solution.py:231
  90.7 1.3 collective-permute-start.16
  92.0 2.0 %collective-permute-start.15 = (f32[3,128,256]{2,1,0:T(8,128)}, f32[3,128,256]{2,1,0:T(8,128)S(1)}, u32[]{:S(2)}, u32[]{:S(2)}) collective-permute-start(f32[3,128,256]{2,1,0:T(8,128)} %get-tuple-element.41), channel_id=1, source_target_pairs={{2,0},{0,2},{7,5},{5,7},{10,8},{8,10},{15,13},{13,15},{18,16},{16,... | collective-permute-start | bytes 1179656 | tf_op jit(solution)/shard_map/ppermute | solution.py:264
  94.0 1.5 collective-permute-start.14
  95.5 19.6 %shard_map.89.parent = f32[256,256]{1,0:T(8,128)} custom-call(s32[2]{0:T(128)} %pad_add_fusion.place, f32[2,256,256]{2,1,0:T(8,128)} %get-tuple-element.33.own, f32[2,256,256]{2,1,0:T(8,128)} %copy-done.8, f32[512,512]{1,0:T(8,128)} %copy.9.vt_ref, f32[512,512]{1,0:T(8,128)} %bitcast.19), custom_call_target="tpu_custom_call" | custom-call | flops 22000001024 | bytes 22000000 | tf_op jit(solution)/shard_map/pallas_call | solution.py:231
  115.2 16.5 %collective-permute-done.9.refs_2_ = f32[12,128,128]{2,1,0:T(8,128)} collective-permute-done((f32[12,128,128]{2,1,0:T(8,128)S(1)}, f32[12,128,128]{2,1,0:T(8,128)}, u32[]{:S(2)}, u32[]{:S(2)}) %collective-permute-start.9) | collective-permute-done | bytes 786464 | tf_op jit(solution)/shard_map/ppermute | solution.py:264
  131.7 7.7 %collective-permute-done.15.refs_6_ = f32[3,128,256]{2,1,0:T(8,128)S(1)} collective-permute-done((f32[3,128,256]{2,1,0:T(8,128)}, f32[3,128,256]{2,1,0:T(8,128)S(1)}, u32[]{:S(2)}, u32[]{:S(2)}) %collective-permute-start.15) | collective-permute-done | bytes 393248 | tf_op jit(solution)/shard_map/ppermute | solution.py:264
  139.4 0.7 copy-done.11
  140.2 7.7 %shard_map.91 = (f32[6,64,256]{2,1,0:T(8,128)}, f32[6,64,256]{2,1,0:T(8,128)}, f32[6,64,256]{2,1,0:T(8,128)}, f32[6,64,256]{2,1,0:T(8,128)}) custom-call(s32[2]{0:T(128)} %pad_add_fusion.place, s32[2]{0:T(128)} %count.3, f32[4,256,128]{2,1,0:T(8,128)} %get-tuple-element.28.w_ref, f32[256,256]{1,0:T(8,128)} %get-tuple-element.29.schur, ...), custom_call_target="tpu_custom_call" | custom-call | flops 7000000000 | bytes 7000000 | tf_op jit(solution)/shard_map/pallas_call | solution.py:231
  147.9 1.3 collective-permute-start.17
  149.2 2.7 %collective-permute-start.18 = (f32[6,64,256]{2,1,0:T(8,128)}, f32[6,64,256]{2,1,0:T(8,128)S(1)}, u32[]{:S(2)}, u32[]{:S(2)}) collective-permute-start(f32[6,64,256]{2,1,0:T(8,128)} %get-tuple-element.44), channel_id=1, source_target_pairs={{0,2},{2,0},{5,7},{7,5},{8,10},{10,8},{13,15},{15,13},{16,18},{18,... | collective-permute-start | bytes 1179656 | tf_op jit(solution)/shard_map/ppermute | solution.py:267
  151.9 1.3 collective-permute-start.19
  153.2 1.5 collective-permute-done.17.refs_1_
  154.7 13.6 %collective-permute-done.18.refs_2_ = f32[6,64,256]{2,1,0:T(8,128)S(1)} collective-permute-done((f32[6,64,256]{2,1,0:T(8,128)}, f32[6,64,256]{2,1,0:T(8,128)S(1)}, u32[]{:S(2)}, u32[]{:S(2)}) %collective-permute-start.18) | collective-permute-done | bytes 393248 | tf_op jit(solution)/shard_map/ppermute | solution.py:267
  168.4 0.7 copy-done.14
  169.1 0.1 copy-done.15
  169.2 2.3 %shard_map.92 = (f32[2,64,256]{2,1,0:T(8,128)}, f32[2,4,64,256]{3,2,1,0:T(8,128)}, f32[1,64,256]{2,1,0:T(8,128)}) custom-call(s32[2]{0:T(128)} %pad_add_fusion.place, f32[6,64,256]{2,1,0:T(8,128)} %get-tuple-element.42.refs_0_, f32[6,64,256]{2,1,0:T(8,128)} %copy-done.13, f32[6,64,256]{2,1,0:T(8,128)} %copy-done.14, f32[6,64,256]{2,1,0:T(8,128)} %copy-done.15), custom_call_target="tpu_custom_call" | custom-call | flops 2000000000 | bytes 2000000 | tf_op jit(solution)/shard_map/pallas_call | solution.py:231
  (44 shorter events, 0.2 us)
Async XLA Ops:
  1.2 12.7 %copy-start = (f32[2,4,512,128]{3,2,1,0:T(8,128)S(1)}, f32[2,4,512,128]{3,2,1,0:T(8,128)}, u32[]{:S(2)}) copy-start(f32[2,4,512,128]{3,2,1,0:T(8,128)} %param.7) | copy-start | bytes 6291460
  3.6 17.8 %copy-start.3 = (f32[2,128,256]{2,1,0:T(8,128)S(1)}, f32[2,128,256]{2,1,0:T(8,128)}, u32[]{:S(2)}) copy-start(f32[2,128,256]{2,1,0:T(8,128)} %get-tuple-element.36) | copy-start | bytes 786436
  3.6 27.3 %collective-permute-start = (f32[8,128,128]{2,1,0:T(8,128)}, f32[8,128,128]{2,1,0:T(8,128)}, u32[]{:S(2)}, u32[]{:S(2)}) collective-permute-start(f32[8,128,128]{2,1,0:T(8,128)} %get-tuple-element.26.own), channel_id=1, source_target_pairs={{1,0},{3,2},{4,5},{6,7},{9,8},{11,10},{12,13},{14,15},{17,16},{19,... | collective-permute-start | bytes 1572872 | tf_op jit(solution)/shard_map/ppermute | solution.py:264
  5.1 22.0 %collective-permute-start.2 = (f32[6,128,128]{2,1,0:T(8,128)}, f32[6,128,128]{2,1,0:T(8,128)S(1)}, u32[]{:S(2)}, u32[]{:S(2)}) collective-permute-start(f32[6,128,128]{2,1,0:T(8,128)} %get-tuple-element.27), channel_id=1, source_target_pairs={{3,0},{1,2},{6,5},{4,7},{11,8},{9,10},{14,13},{12,15},{19,16},{17,... | collective-permute-start | bytes 1179656 | tf_op jit(solution)/shard_map/ppermute | solution.py:264
  6.4 24.6 %collective-permute-start.1 = (f32[6,128,128]{2,1,0:T(8,128)}, f32[6,128,128]{2,1,0:T(8,128)}, u32[]{:S(2)}, u32[]{:S(2)}) collective-permute-start(f32[6,128,128]{2,1,0:T(8,128)} %get-tuple-element.27), channel_id=1, source_target_pairs={{2,0},{0,2},{7,5},{5,7},{10,8},{8,10},{15,13},{13,15},{18,16},{16,... | collective-permute-start | bytes 1179656 | tf_op jit(solution)/shard_map/ppermute | solution.py:264
  12.3 9.1 %collective-permute-start.11 = (f32[2,128,256]{2,1,0:T(8,128)}, f32[2,128,256]{2,1,0:T(8,128)S(1)}, u32[]{:S(2)}, u32[]{:S(2)}) collective-permute-start(f32[2,128,256]{2,1,0:T(8,128)} %get-tuple-element.36), channel_id=1, source_target_pairs={{0,8},{4,12},{8,0},{12,4},{16,24},{20,28},{24,16},{28,20},{1,9},{5... | collective-permute-start | bytes 786440 | tf_op jit(solution)/shard_map/ppermute | solution.py:273
  21.5 11.8 %copy-start.4 = (f32[2,128,256]{2,1,0:T(8,128)}, f32[2,128,256]{2,1,0:T(8,128)S(1)}, u32[]{:S(2)}) copy-start(f32[2,128,256]{2,1,0:T(8,128)S(1)} %collective-permute-done.11) | copy-start | bytes 786436
  21.5 34.3 %collective-permute-start.12 = (f32[4,128,256]{2,1,0:T(8,128)S(1)}, f32[4,128,256]{2,1,0:T(8,128)}, u32[]{:S(2)}, u32[]{:S(2)}) collective-permute-start(f32[4,128,256]{2,1,0:T(8,128)S(1)} %pad_maximum_fusion.1), channel_id=1, source_target_pairs={{0,16},{4,20},{8,24},{12,28},{16,0},{20,4},{24,8},{28,12},{1,17},{... | collective-permute-start | bytes 1572872 | tf_op jit(solution)/shard_map/ppermute | solution.py:273
  27.1 3.9 %copy-start.9 = (f32[6,128,128]{2,1,0:T(8,128)}, f32[6,128,128]{2,1,0:T(8,128)S(1)}, u32[]{:S(2)}) copy-start(f32[6,128,128]{2,1,0:T(8,128)S(1)} %collective-permute-done.2.far3) | copy-start | bytes 1179652
  33.2 41.7 %collective-permute-start.3 = (f32[4,128,256]{2,1,0:T(8,128)}, f32[4,128,256]{2,1,0:T(8,128)}, u32[]{:S(2)}, u32[]{:S(2)}) collective-permute-start(f32[4,128,256]{2,1,0:T(8,128)} %shard_map.87), channel_id=1, source_target_pairs={{5,0},{7,2},{0,5},{2,7},{13,8},{15,10},{8,13},{10,15},{21,16},{23,... | collective-permute-start | bytes 1572872 | tf_op jit(solution)/shard_map/ppermute | solution.py:270
  57.0 22.4 %copy-start.2 = (f32[8,128,256]{2,1,0:T(8,128)}, f32[8,128,256]{2,1,0:T(8,128)S(1)}, u32[]{:S(2)}) copy-start(f32[8,128,256]{2,1,0:T(8,128)S(1)} %pad_maximum_fusion.low) | copy-start | bytes 3145732
  57.0 31.1 %collective-permute-start.13 = (f32[8,128,256]{2,1,0:T(8,128)S(1)}, f32[8,128,256]{2,1,0:T(8,128)}, u32[]{:S(2)}, u32[]{:S(2)}) collective-permute-start(f32[8,128,256]{2,1,0:T(8,128)S(1)} %pad_maximum_fusion.low), channel_id=1, source_target_pairs={{0,4},{4,0},{8,12},{12,8},{16,20},{20,16},{24,28},{28,24},{1,5},{5... | collective-permute-start | bytes 3145736 | tf_op jit(solution)/shard_map/ppermute | solution.py:273
  57.2 17.8 %copy-start.6 = (f32[4,128,128]{2,1,0:T(8,128)}, f32[4,128,128]{2,1,0:T(8,128)S(1)}, u32[]{:S(2)}) copy-start(f32[4,128,128]{2,1,0:T(8,128)S(1)} %get-tuple-element.30.n0) | copy-start | bytes 786436
  57.2 8.3 %collective-permute-start.4 = (f32[4,128,128]{2,1,0:T(8,128)S(1)}, f32[4,128,128]{2,1,0:T(8,128)S(1)}, u32[]{:S(2)}, u32[]{:S(2)}) collective-permute-start(f32[4,128,128]{2,1,0:T(8,128)S(1)} %get-tuple-element.30.n0), channel_id=1, source_target_pairs={{1,0},{3,2},{4,5},{6,7},{9,8},{11,10},{12,13},{14,15},{17,16},{19,... | collective-permute-start | bytes 786440 | tf_op jit(solution)/shard_map/ppermute | solution.py:264
  58.5 12.9 %collective-permute-start.6 = (f32[4,128,128]{2,1,0:T(8,128)S(1)}, f32[4,128,128]{2,1,0:T(8,128)S(1)}, u32[]{:S(2)}, u32[]{:S(2)}) collective-permute-start(f32[4,128,128]{2,1,0:T(8,128)S(1)} %get-tuple-element.31), channel_id=1, source_target_pairs={{3,0},{1,2},{6,5},{4,7},{11,8},{9,10},{14,13},{12,15},{19,16},{17,... | collective-permute-start | bytes 786440 | tf_op jit(solution)/shard_map/ppermute | solution.py:264
  59.8 15.1 %collective-permute-start.5 = (f32[4,128,128]{2,1,0:T(8,128)S(1)}, f32[4,128,128]{2,1,0:T(8,128)S(1)}, u32[]{:S(2)}, u32[]{:S(2)}) collective-permute-start(f32[4,128,128]{2,1,0:T(8,128)S(1)} %get-tuple-element.31), channel_id=1, source_target_pairs={{2,0},{0,2},{7,5},{5,7},{10,8},{8,10},{15,13},{13,15},{18,16},{16,... | collective-permute-start | bytes 786440 | tf_op jit(solution)/shard_map/ppermute | solution.py:264
  65.4 9.5 %copy-start.16 = (f32[4,128,128]{2,1,0:T(8,128)}, f32[4,128,128]{2,1,0:T(8,128)S(1)}, u32[]{:S(2)}) copy-start(f32[4,128,128]{2,1,0:T(8,128)S(1)} %collective-permute-done.4.n1) | copy-start | bytes 786436
  65.4 26.5 %collective-permute-start.8 = (f32[12,128,128]{2,1,0:T(8,128)}, f32[12,128,128]{2,1,0:T(8,128)}, u32[]{:S(2)}, u32[]{:S(2)}) collective-permute-start(f32[12,128,128]{2,1,0:T(8,128)} %get-tuple-element.34.refs_0_), channel_id=1, source_target_pairs={{1,0},{3,2},{4,5},{6,7},{9,8},{11,10},{12,13},{14,15},{17,16},{19,... | collective-permute-start | bytes 2359304 | tf_op jit(solution)/shard_map/ppermute | solution.py:264
  71.4 3.5 %copy-start.17 = (f32[4,128,128]{2,1,0:T(8,128)}, f32[4,128,128]{2,1,0:T(8,128)S(1)}, u32[]{:S(2)}) copy-start(f32[4,128,128]{2,1,0:T(8,128)S(1)} %collective-permute-done.6.n3) | copy-start | bytes 786436
  74.9 0.7 copy-start.18
  75.6 5.2 %copy-start.1 = (f32[1,512,512]{2,1,0:T(8,128)S(1)}, f32[1,512,512]{2,1,0:T(8,128)}, u32[]{:S(2)}) copy-start(f32[1,512,512]{2,1,0:T(8,128)} %param.11) | copy-start | bytes 3145732
  79.4 2.8 %copy-start.5 = (f32[12,128,128]{2,1,0:T(8,128)S(1)}, f32[12,128,128]{2,1,0:T(8,128)}, u32[]{:S(2)}) copy-start(f32[12,128,128]{2,1,0:T(8,128)} %get-tuple-element.35) | copy-start | bytes 2359300
  79.4 14.6 %collective-permute-start.7 = (f32[2,256,256]{2,1,0:T(8,128)}, f32[2,256,256]{2,1,0:T(8,128)S(1)}, u32[]{:S(2)}, u32[]{:S(2)}) collective-permute-start(f32[2,256,256]{2,1,0:T(8,128)} %get-tuple-element.33.own), channel_id=1, source_target_pairs={{5,0},{2,7},{13,8},{10,15},{21,16},{18,23},{29,24},{26,31}} | collective-permute-start | bytes 1572872 | tf_op jit(solution)/shard_map/ppermute | solution.py:270
  82.1 33.0 %collective-permute-start.10 = (f32[12,128,128]{2,1,0:T(8,128)S(1)}, f32[12,128,128]{2,1,0:T(8,128)S(1)}, u32[]{:S(2)}, u32[]{:S(2)}) collective-permute-start(f32[12,128,128]{2,1,0:T(8,128)S(1)} %copy-done.5), channel_id=1, source_target_pairs={{3,0},{1,2},{6,5},{4,7},{11,8},{9,10},{14,13},{12,15},{19,16},{17,... | collective-permute-start | bytes 2359304 | tf_op jit(solution)/shard_map/ppermute | solution.py:264
  83.4 48.3 %collective-permute-start.9 = (f32[12,128,128]{2,1,0:T(8,128)S(1)}, f32[12,128,128]{2,1,0:T(8,128)}, u32[]{:S(2)}, u32[]{:S(2)}) collective-permute-start(f32[12,128,128]{2,1,0:T(8,128)S(1)} %copy-done.5), channel_id=1, source_target_pairs={{2,0},{0,2},{7,5},{5,7},{10,8},{8,10},{15,13},{13,15},{18,16},{16,... | collective-permute-start | bytes 2359304 | tf_op jit(solution)/shard_map/ppermute | solution.py:264
  90.7 41.1 %collective-permute-start.16 = (f32[3,128,256]{2,1,0:T(8,128)}, f32[3,128,256]{2,1,0:T(8,128)S(1)}, u32[]{:S(2)}, u32[]{:S(2)}) collective-permute-start(f32[3,128,256]{2,1,0:T(8,128)} %get-tuple-element.41), channel_id=1, source_target_pairs={{3,0},{1,2},{6,5},{4,7},{11,8},{9,10},{14,13},{12,15},{19,16},{17,... | collective-permute-start | bytes 1179656 | tf_op jit(solution)/shard_map/ppermute | solution.py:264
  92.0 47.4 %collective-permute-start.15 = (f32[3,128,256]{2,1,0:T(8,128)}, f32[3,128,256]{2,1,0:T(8,128)S(1)}, u32[]{:S(2)}, u32[]{:S(2)}) collective-permute-start(f32[3,128,256]{2,1,0:T(8,128)} %get-tuple-element.41), channel_id=1, source_target_pairs={{2,0},{0,2},{7,5},{5,7},{10,8},{8,10},{15,13},{13,15},{18,16},{16,... | collective-permute-start | bytes 1179656 | tf_op jit(solution)/shard_map/ppermute | solution.py:264
  94.0 1.5 copy-start.8
  94.0 37.7 %collective-permute-start.14 = (f32[3,128,256]{2,1,0:T(8,128)}, f32[3,128,256]{2,1,0:T(8,128)S(1)}, u32[]{:S(2)}, u32[]{:S(2)}) collective-permute-start(f32[3,128,256]{2,1,0:T(8,128)} %get-tuple-element.40.refs_4_), channel_id=1, source_target_pairs={{1,0},{3,2},{4,5},{6,7},{9,8},{11,10},{12,13},{14,15},{17,16},{19,... | collective-permute-start | bytes 1179656 | tf_op jit(solution)/shard_map/ppermute | solution.py:264
  115.2 24.2 %copy-start.7 = (f32[12,128,128]{2,1,0:T(8,128)}, f32[12,128,128]{2,1,0:T(8,128)S(1)}, u32[]{:S(2)}) copy-start(f32[12,128,128]{2,1,0:T(8,128)S(1)} %collective-permute-done.10.refs_3_) | copy-start | bytes 2359300
  131.7 7.7 %copy-start.12 = (f32[3,128,256]{2,1,0:T(8,128)}, f32[3,128,256]{2,1,0:T(8,128)S(1)}, u32[]{:S(2)}) copy-start(f32[3,128,256]{2,1,0:T(8,128)S(1)} %collective-permute-done.14.refs_5_) | copy-start | bytes 1179652
  131.7 7.7 %copy-start.10 = (f32[3,128,256]{2,1,0:T(8,128)}, f32[3,128,256]{2,1,0:T(8,128)S(1)}, u32[]{:S(2)}) copy-start(f32[3,128,256]{2,1,0:T(8,128)S(1)} %collective-permute-done.16.refs_7_) | copy-start | bytes 1179652
  139.4 0.8 copy-start.11
  147.9 6.9 %collective-permute-start.17 = (f32[6,64,256]{2,1,0:T(8,128)}, f32[6,64,256]{2,1,0:T(8,128)S(1)}, u32[]{:S(2)}, u32[]{:S(2)}) collective-permute-start(f32[6,64,256]{2,1,0:T(8,128)} %get-tuple-element.43), channel_id=1, source_target_pairs={{0,1},{2,3},{5,4},{7,6},{8,9},{10,11},{13,12},{15,14},{16,17},{18,... | collective-permute-start | bytes 1179656 | tf_op jit(solution)/shard_map/ppermute | solution.py:267
  149.2 19.2 %collective-permute-start.18 = (f32[6,64,256]{2,1,0:T(8,128)}, f32[6,64,256]{2,1,0:T(8,128)S(1)}, u32[]{:S(2)}, u32[]{:S(2)}) collective-permute-start(f32[6,64,256]{2,1,0:T(8,128)} %get-tuple-element.44), channel_id=1, source_target_pairs={{0,2},{2,0},{5,7},{7,5},{8,10},{10,8},{13,15},{15,13},{16,18},{18,... | collective-permute-start | bytes 1179656 | tf_op jit(solution)/shard_map/ppermute | solution.py:267
  151.9 16.5 %collective-permute-start.19 = (f32[6,64,256]{2,1,0:T(8,128)}, f32[6,64,256]{2,1,0:T(8,128)S(1)}, u32[]{:S(2)}, u32[]{:S(2)}) collective-permute-start(f32[6,64,256]{2,1,0:T(8,128)} %get-tuple-element.45), channel_id=1, source_target_pairs={{0,3},{2,1},{5,6},{7,4},{8,11},{10,9},{13,14},{15,12},{16,19},{18,... | collective-permute-start | bytes 1179656 | tf_op jit(solution)/shard_map/ppermute | solution.py:267
  154.7 13.6 %copy-start.13 = (f32[6,64,256]{2,1,0:T(8,128)}, f32[6,64,256]{2,1,0:T(8,128)S(1)}, u32[]{:S(2)}) copy-start(f32[6,64,256]{2,1,0:T(8,128)S(1)} %collective-permute-done.17.refs_1_) | copy-start | bytes 1179652
  168.4 0.7 copy-start.14
  168.4 0.9 copy-start.15
where the time goes:
time: 174 us; the launch traced here: 172 us
  waiting for transfers between devices  64.7 us (37%)
  Pallas kernels  60.3 us (35%)
  starting transfers between devices  38.8 us (22%)
  local copies, waits for them, and re-layouts  4.91 us (3%)
  other arithmetic  1.8 us (1%)
    pallas_call x8, Pallas kernels, call(): pl.pallas_call(kernel, out_shape=shapes, in_specs=specs, out_specs=[vmem]...  60.3 us
    ppermute x12, waiting for transfers between devices, to_owner(): lax.ppermute(x, both, [(r * n_col + (z ^ j), r * n_col + z) for r, z in o...  43.3 us
    ppermute x12, starting transfers between devices, to_owner(): lax.ppermute(x, both, [(r * n_col + (z ^ j), r * n_col + z) for r, z in o...  25.9 us
    ppermute x3, waiting for transfers between devices, from_owner(): lax.ppermute(x, both, [(r * n_col + z, r * n_col + (z ^ j)) for r, z in o...  15.1 us
    ppermute x3, waiting for transfers between devices, across(): return lax.ppermute(x, 'row', [(r, r ^ bit) for r in range(n_row)])  6.33 us
    ppermute x3, starting transfers between devices, from_owner(): lax.ppermute(x, both, [(r * n_col + z, r * n_col + (z ^ j)) for r, z in o...  5.36 us
    ppermute x2, starting transfers between devices, from_sibling(): lax.ppermute(x, both, [((r ^ 1) * n_col + (z ^ 1), r * n_col + z) for r,...  4.28 us
  transfers between devices with their start and end apart: 20, of which 10 were waited for; matrix products, arithmetic and copies ran while one was open for 2% of the time, Pallas kernels for 28%

commit v1 on v0

--- a/solution.py
+++ b/solution.py
@@ -141,15 +141,42 @@
         out[j] = wide(ref, ref.shape[0] - 2, 2)
 
 
-def name_kernel(place, ids, low, high, mine_ref, other_ref):
+def split_kernel(place, near, v, first_mine, first_other, rest_mine, rest_other, turned):
+    mine = place[1] >> 1
+    count = first_mine.shape[0]
+    turned[...] = v[...].T
+    for which, first, rest in ((mine, first_mine, rest_mine), (1 - mine, first_other, rest_other)):
+        for i in range(near.shape[1]):
+            if i < count:
+                first[i] = near[which, i]
+            else:
+                rest[i - count] = near[which, i]
+
+
+def name_kernel(place, ids, low0, low1, high0, high1, _, __, rest_mine, rest_other, found, sems):
     row, mine = place[0], place[1] >> 1
     clusters, slots = ids.shape
-    for which, out in ((mine, mine_ref), (1 - mine, other_ref)):
+    edge = found.shape[2]
+    copies = []
+    for side, (which, rest) in enumerate(((mine, rest_mine), (1 - mine, rest_other))):
         for k in range(1, slots):
             name = ids[which, k]
             apart = lax.div(name, clusters) ^ row
             spot = (apart >> 1) * clusters + lax.rem(name, clusters)
-            out[k - 1] = jnp.where((apart & 1) > 0, high[spot], low[spot])
+            inner = lax.rem(spot, low0.shape[0])
+            late = spot >= low0.shape[0]
+            low = jnp.where(late, low1[inner], low0[inner])
+            base = jnp.where((apart & 1) > 0, jnp.where(late, high1[inner], high0[inner]), low)
+            for b in range(2):
+                found[side, 2 * (k - 1) + b] = base[:, b * edge : (b + 1) * edge]
+        count = found.shape[1]
+        copy = pltpu.make_async_copy(
+            found.at[side], rest.at[pl.ds(rest.shape[0] - count, count)], sems.at[side]
+        )
+        copy.start()
+        copies.append(copy)
+    for copy in copies:
+        copy.wait()
 
 
 def coupling(w_ref, blocks, bases):
@@ -177,12 +204,12 @@
 
 def near_rest_kernel(place, count, w_ref, schur, first, parent, *refs):
     z = place[1]
-    blocks, named, parts, flipped = refs[:4], refs[4:8], refs[8:12], refs[12]
-    total = named[0].shape[0]
+    blocks, parts, flipped = refs[:4], refs[4:8], refs[8]
+    total = blocks[0].shape[0] // 6
     flipped[0] = schur[...]
     flipped[1] = first[...]
     for k in range(total):
-        result = coupling(w_ref, [tall(n, 4 * k) for n in blocks], [s[k] for s in named])
+        result = coupling(w_ref, [tall(n, 4 * k) for n in blocks], [wide(n, 4 * total + 2 * k, 2) for n in blocks])
         flipped[k + 2] = jnp.where(count[z >> 1] > k + 1, result, 0.0).T
     flipped[total + 2] = parent[...]
     for i in range(total + 3):
@@ -238,16 +265,12 @@
     )(*scalars, *arrays)
 
 
-def pick(array, index):
-    return lax.dynamic_index_in_dim(array, index, 0, keepdims=False)
-
-
 def after(values, ready):
     return lax.optimization_barrier((values, ready))[0]
 
 
 def levels(diag_blocks, near_blocks, cluster_bases, near_ids, near_count, parent_bases):
-    clusters, edge, _ = cluster_bases.shape
+    clusters, edge, size = cluster_bases.shape
     slots = near_blocks.shape[1]
     skeleton = K
     n_row, n_col = lax.axis_size("row"), lax.axis_size("col")
@@ -255,7 +278,6 @@
     quarter = skeleton // n_col
     row, column = lax.axis_index("row"), lax.axis_index("col")
     place = jnp.stack([row, column]).astype(jnp.int32)
-    mine, other = column // 2, 1 - column // 2
     both = ("row", "col")
     owned = [(r, z) for r in range(n_row) for z in range(n_col) if z % 2 == r % 2]
     heads = [(r, (n_col - 1) * (r % 2)) for r in range(n_row)]
@@ -290,13 +312,36 @@
     leaf = gather(full, half)
 
     bits = [1 << t for t in range(1, n_row.bit_length() - 1)]
+    pieces = [table]
     for bit in bits:
-        table = jnp.concatenate([table, across(table, bit)], axis=0)
+        pieces = [jnp.concatenate(pieces, axis=0) if len(pieces) > 1 else table]
+        pieces.append(across(pieces[0], bit))
 
     near = near_blocks.reshape(clusters, slots * 4, edge, edge)
-    n_mine, n_other = pick(near, mine), pick(near, other)
-    ready = after((n_mine[:4], n_other[:4], n_mine[4:], n_other[4:]), leaf[1:])
-    n_early, n_late = gather(*ready[:2]), gather(*ready[2:])
+    rest_blocks = (slots - 1) * 6
+    v = parent_bases[0]
+    split = call(
+        split_kernel,
+        [(4, edge, edge)] * 2 + [(rest_blocks, edge, edge)] * 2 + [(size, size)],
+        [place],
+        [near, v],
+    )
+    anywhere = pl.BlockSpec(memory_space=pl.ANY)
+    swapped = [across(piece, 1) for piece in pieces]
+    scalar, vmem = pl.BlockSpec(memory_space=pltpu.SMEM), pl.BlockSpec(memory_space=pltpu.VMEM)
+    rest = pl.pallas_call(
+        name_kernel,
+        out_shape=[jax.ShapeDtypeStruct((rest_blocks, edge, edge), jnp.float32)] * 2,
+        in_specs=[scalar] * 2 + [vmem] * 4 + [anywhere] * 2,
+        out_specs=[anywhere] * 2,
+        scratch_shapes=[
+            pltpu.VMEM((2, (slots - 1) * 2, edge, edge), jnp.float32),
+            pltpu.SemaphoreType.DMA((2,)),
+        ],
+        input_output_aliases={6: 0, 7: 1},
+    )(place, near_ids, *pieces, *swapped, split[2], split[3])
+    n_early = gather(*after((split[0], split[1]), leaf[1:]))
+    n_rest = gather(*after(rest, leaf[1:]))
     (skeletons,) = call(skeleton_kernel, [(4, edge, skeleton)], [place], leaf)
     sibling = from_sibling(skeletons, owned)
 
@@ -313,25 +358,15 @@
     )
     arrived = from_sibling(pair, heads)
 
-    table = after(table, w)
-    s_mine, s_other = call(
-        name_kernel,
-        [(slots - 1, edge, skeleton)] * 2,
-        [place, near_ids],
-        [table, across(table, 1)],
-    )
-    named = gather(*after((s_mine, s_other), pair))
-
-    v = parent_bases[0]
     (parent,) = call(
-        parent_kernel, [(skeleton, skeleton)], [place], [pair, arrived, v.T, v], 22
+        parent_kernel, [(skeleton, skeleton)], [place], [pair, arrived, split[4], v], 22
     )
     total = slots + 2
     results = call(
         near_rest_kernel,
         [(total, quarter, skeleton)] * 4,
         [place, near_count],
-        [w, schur, first, parent, *n_late, *named],
+        [w, schur, first, parent, *n_rest],
         7,
         [(total, skeleton, skeleton)],
     )

time: 174 us -> 165 us (0.948)
  waiting for transfers between devices: 64.7 us -> 49.8 us
  Pallas kernels: 60.3 us -> 64.2 us
  starting transfers between devices: 38.8 us -> 41.8 us
    ppermute x12 -> x9, waiting for transfers between devices: 43.3 us -> 32.5 us  [to_owner(): lax.ppermute(x, both, [(r * n_col + (z ^ j), r * n_col + z) for r, z in o...]
    ppermute x3 -> x4, waiting for transfers between devices: 6.33 us -> 2.57 us  [across(): return lax.ppermute(x, 'row', [(r, r ^ bit) for r in range(n_row)])]
    ppermute x3 -> x4, starting transfers between devices: 3.21 us -> 6.45 us  [across(): return lax.ppermute(x, 'row', [(r, r ^ bit) for r in range(n_row)])]
    unnamed x38 -> x35, local copies, waits for them, and re-layouts: 2.32 us -> 5.29 us
    pallas_call x0 -> x1, Pallas kernels: none -> 2.55 us  [levels(): pl.pallas_call(name_kernel, out_shape=[jax.ShapeDtypeStruct((rest_blocks,...]
    ppermute x3, starting transfers between devices: 5.36 us -> 7.68 us  [from_owner(): lax.ppermute(x, both, [(r * n_col + z, r * n_col + (z ^ j)) for r, z in o...]
    ppermute x12 -> x9, starting transfers between devices: 25.9 us -> 24.5 us  [to_owner(): lax.ppermute(x, both, [(r * n_col + (z ^ j), r * n_col + z) for r, z in o...]
  transfers between devices with their start and end apart: 20 -> 18, of which waited for: 10 -> 6; matrix products, arithmetic and copies ran while one was open for 2% -> 1% of each run, Pallas kernels for 28% -> 32%
where the time goes in v1:
time: 165 us; the launch traced here: 163 us
  Pallas kernels  64.2 us (39%)
  waiting for transfers between devices  49.8 us (30%)
  starting transfers between devices  41.8 us (25%)
  local copies, waits for them, and re-layouts  5.31 us (3%)
    pallas_call x8, Pallas kernels, call(): pl.pallas_call(kernel, out_shape=shapes, in_specs=specs, out_specs=[vmem]...  61.6 us
    ppermute x9, waiting for transfers between devices, to_owner(): lax.ppermute(x, both, [(r * n_col + (z ^ j), r * n_col + z) for r, z in o...  32.5 us
    ppermute x9, starting transfers between devices, to_owner(): lax.ppermute(x, both, [(r * n_col + (z ^ j), r * n_col + z) for r, z in o...  24.5 us
    ppermute x3, waiting for transfers between devices, from_owner(): lax.ppermute(x, both, [(r * n_col + z, r * n_col + (z ^ j)) for r, z in o...  14.8 us
    ppermute x3, starting transfers between devices, from_owner(): lax.ppermute(x, both, [(r * n_col + z, r * n_col + (z ^ j)) for r, z in o...  7.68 us
    ppermute x4, starting transfers between devices, across(): return lax.ppermute(x, 'row', [(r, r ^ bit) for r in range(n_row)])  6.45 us
    unnamed x35, local copies, waits for them, and re-layouts  5.29 us
  transfers between devices with their start and end apart: 18, of which 6 were waited for; matrix products, arithmetic and copies ran while one was open for 1% of the time, Pallas kernels for 32%

profile of v1, /device:TPU:0, one launch (start us, length us, event | category | flops | bytes accessed | tf_op | source)
XLA Modules:
  0.0 162.7 jit_solution(102780793450432089)
XLA Ops:
  0.6 0.6 pad_add_fusion.place
  1.3 2.3 %shard_map.85 = (f32[8,128,128]{2,1,0:T(8,128)}, f32[6,128,128]{2,1,0:T(8,128)}, f32[2,128,256]{2,1,0:T(8,128)}) custom-call(s32[2]{0:T(128)} %pad_add_fusion.place, f32[2,512,128]{2,1,0:T(8,128)} %diag.1, f32[2,128,512]{2,1,0:T(8,128)} %bases.1), custom_call_target="tpu_custom_call" | custom-call | flops 2000000000 | bytes 2000000 | tf_op jit(solution)/shard_map/pallas_call | solution.py:258
  3.5 1.3 collective-permute-start
  4.8 6.0 %collective-permute-start.1 = (f32[6,128,128]{2,1,0:T(8,128)}, f32[6,128,128]{2,1,0:T(8,128)S(1)}, u32[]{:S(2)}, u32[]{:S(2)}) collective-permute-start(f32[6,128,128]{2,1,0:T(8,128)} %get-tuple-element.29), channel_id=1, source_target_pairs={{2,0},{0,2},{7,5},{5,7},{10,8},{8,10},{15,13},{13,15},{18,16},{16,... | collective-permute-start | bytes 1179656 | tf_op jit(solution)/shard_map/ppermute | solution.py:286
  10.8 1.3 collective-permute-start.2
  12.1 1.6 collective-permute-start.8
  13.7 1.0 constant_dynamic-update-slice_fusion.1
  14.7 4.0 %shard_map.88 = (f32[4,128,128]{2,1,0:T(8,128)}, f32[4,128,128]{2,1,0:T(8,128)}, f32[18,128,128]{2,1,0:T(8,128)}, f32[18,128,128]{2,1,0:T(8,128)}, f32[512,512]{1,0:T(8,128)}) custom-call(s32[2]{0:T(128)} %pad_add_fusion.place, f32[2,16,128,128]{3,2,1,0:T(8,128)} %bitcast.7, f32[512,512]{1,0:T(8,128)} %bitcast.8), custom_call_target="tpu_custom_call" | custom-call | flops 2000000000 | bytes 2000000 | tf_op jit(solution)/shard_map/pallas_call | solution.py:258
  18.7 2.6 %collective-permute-done.8 = f32[2,128,256]{2,1,0:T(8,128)S(1)} collective-permute-done((f32[2,128,256]{2,1,0:T(8,128)}, f32[2,128,256]{2,1,0:T(8,128)S(1)}, u32[]{:S(2)}, u32[]{:S(2)}) %collective-permute-start.8) | collective-permute-done | bytes 262176 | tf_op jit(solution)/shard_map/ppermute | solution.py:295
  21.3 1.6 collective-permute-start.9
  22.9 4.6 %collective-permute-done.1.far2 = f32[6,128,128]{2,1,0:T(8,128)S(1)} collective-permute-done((f32[6,128,128]{2,1,0:T(8,128)}, f32[6,128,128]{2,1,0:T(8,128)S(1)}, u32[]{:S(2)}, u32[]{:S(2)}) %collective-permute-start.1) | collective-permute-done | bytes 393248 | tf_op jit(solution)/shard_map/ppermute | solution.py:286
  27.6 5.8 %collective-permute-start.5 = (f32[4,128,128]{2,1,0:T(8,128)}, f32[4,128,128]{2,1,0:T(8,128)S(1)}, u32[]{:S(2)}, u32[]{:S(2)}) collective-permute-start(f32[4,128,128]{2,1,0:T(8,128)} %get-tuple-element.35), channel_id=1, source_target_pairs={{2,0},{0,2},{7,5},{5,7},{10,8},{8,10},{15,13},{13,15},{18,16},{16,... | collective-permute-start | bytes 786440 | tf_op jit(solution)/shard_map/ppermute | solution.py:286
  33.4 1.3 collective-permute-start.6
  34.7 2.3 %shard_map.87 = f32[4,128,256]{2,1,0:T(8,128)} custom-call(s32[2]{0:T(128)} %pad_add_fusion.place, f32[8,128,128]{2,1,0:T(8,128)} %get-tuple-element.28.own, f32[8,128,128]{2,1,0:T(8,128)} %copy-done.7, f32[6,128,128]{2,1,0:T(8,128)} %copy-done.9, f32[6,128,128]{2,1,0:T(8,128)} %copy-done.10), custom_call_target="tpu_custom_call" | custom-call | flops 2000000000 | bytes 2000000 | tf_op jit(solution)/shard_map/pallas_call | solution.py:258
  37.0 1.9 %collective-permute-start.3 = (f32[4,128,256]{2,1,0:T(8,128)}, f32[4,128,256]{2,1,0:T(8,128)S(1)}, u32[]{:S(2)}, u32[]{:S(2)}) collective-permute-start(f32[4,128,256]{2,1,0:T(8,128)} %shard_map.87), channel_id=1, source_target_pairs={{5,0},{7,2},{0,5},{2,7},{13,8},{15,10},{8,13},{10,15},{21,16},{23,... | collective-permute-start | bytes 1572872 | tf_op jit(solution)/shard_map/ppermute | solution.py:292
  38.9 1.3 collective-permute-start.4
  40.2 19.7 %shard_map.86 = (f32[4,256,128]{2,1,0:T(8,128)}, f32[256,256]{1,0:T(8,128)}) custom-call(s32[2]{0:T(128)} %pad_add_fusion.place, f32[8,128,128]{2,1,0:T(8,128)} %get-tuple-element.28.own, f32[8,128,128]{2,1,0:T(8,128)} %copy-done.7, f32[6,128,128]{2,1,0:T(8,128)} %copy-done.9, f32[6,128,128]{2,1,0:T(8,128)} %copy-done.10), custom_call_target="tpu_custom_call" | custom-call | flops 22000001024 | bytes 22000000 | tf_op jit(solution)/shard_map/pallas_call | solution.py:258
  59.9 0.0 collective-permute-done.4.n1
  59.9 3.2 %collective-permute-start.10 = (f32[4,128,256]{2,1,0:T(8,128)S(1)}, f32[4,128,256]{2,1,0:T(8,128)S(1)}, u32[]{:S(2)}, u32[]{:S(2)}) collective-permute-start(f32[4,128,256]{2,1,0:T(8,128)S(1)} %constant_dynamic-update-slice_fusion.low0), channel_id=1, source_target_pairs={{0,4},{4,0},{8,12},{12,8},{16,20},{20,16},{24,28},{28,24},{1,5},{5... | collective-permute-start | bytes 1572872 | tf_op jit(solution)/shard_map/ppermute | solution.py:295
  63.1 0.0 collective-permute-done.9.low1
  63.2 0.1 collective-permute-start.11
  63.3 0.0 copy-start.8
  63.3 0.8 copy-done.15
  64.1 0.1 copy-done.16
  64.1 0.2 copy-done.8
  64.3 3.7 %shard_map.89 = (f32[2,256,256]{2,1,0:T(8,128)}, f32[256,256]{1,0:T(8,128)}) custom-call(s32[2]{0:T(128)} %pad_add_fusion.place, s32[2]{0:T(128)} %count.3, f32[4,256,128]{2,1,0:T(8,128)} %get-tuple-element.30.w_ref, f32[4,128,256]{2,1,0:T(8,128)} %copy-done.8, f32[4,128,128]{2,1,0:T(8,128)} %get-tuple-element.34.n0, ...), custom_call_target="tpu_custom_call" | custom-call | flops 4000000000 | bytes 4000000 | tf_op jit(solution)/shard_map/pallas_call | solution.py:258
  68.0 1.3 collective-permute-start.7
  69.3 0.0 copy-start.2
  69.3 0.8 copy-done.2
  70.1 0.2 copy-done.3
  70.2 2.5 %shard_map.91 = (f32[18,128,128]{2,1,0:T(8,128)}, f32[18,128,128]{2,1,0:T(8,128)}) custom-call(s32[2]{0:T(128)} %pad_add_fusion.place, s32[2,4]{1,0:T(2,128)} %ids.1, f32[4,128,256]{2,1,0:T(8,128)} %copy-done, f32[4,128,256]{2,1,0:T(8,128)} %copy-done.1, f32[4,128,256]{2,1,0:T(8,128)} %copy-done.2, ...), custom_call_target="tpu_custom_call", output_to_operand_aliasing={{0}: (6, {}), {1}: (7, {})} | custom-call | tf_op jit(solution)/shard_map/pallas_call | solution.py:332
  72.8 4.8 %collective-permute-start.13 = (f32[18,128,128]{2,1,0:T(8,128)}, f32[18,128,128]{2,1,0:T(8,128)S(1)}, u32[]{:S(2)}, u32[]{:S(2)}) collective-permute-start(f32[18,128,128]{2,1,0:T(8,128)} %get-tuple-element.45), channel_id=1, source_target_pairs={{2,0},{0,2},{7,5},{5,7},{10,8},{8,10},{15,13},{13,15},{18,16},{16,... | collective-permute-start | bytes 3538952 | tf_op jit(solution)/shard_map/ppermute | solution.py:286
  77.6 1.3 collective-permute-start.14
  78.9 1.5 collective-permute-start.12
  80.4 19.7 %shard_map.90.parent = f32[256,256]{1,0:T(8,128)} custom-call(s32[2]{0:T(128)} %pad_add_fusion.place, f32[2,256,256]{2,1,0:T(8,128)} %get-tuple-element.37.own, f32[2,256,256]{2,1,0:T(8,128)} %collective-permute-done.7.arrived, f32[512,512]{1,0:T(8,128)} %get-tuple-element.38.vt_ref, f32[512,512]{1,0:T(8,128)} %bitcast.9), custom_call_target="tpu_custom_call" | custom-call | flops 22000001024 | bytes 22000000 | tf_op jit(solution)/shard_map/pallas_call | solution.py:258
  100.0 12.8 %collective-permute-done.12.refs_1_ = f32[18,128,128]{2,1,0:T(8,128)S(1)} collective-permute-done((f32[18,128,128]{2,1,0:T(8,128)}, f32[18,128,128]{2,1,0:T(8,128)S(1)}, u32[]{:S(2)}, u32[]{:S(2)}) %collective-permute-start.12) | collective-permute-done | bytes 1179680 | tf_op jit(solution)/shard_map/ppermute | solution.py:286
  112.8 15.0 %collective-permute-done.13.refs_2_ = f32[18,128,128]{2,1,0:T(8,128)S(1)} collective-permute-done((f32[18,128,128]{2,1,0:T(8,128)}, f32[18,128,128]{2,1,0:T(8,128)S(1)}, u32[]{:S(2)}, u32[]{:S(2)}) %collective-permute-start.13) | collective-permute-done | bytes 1179680 | tf_op jit(solution)/shard_map/ppermute | solution.py:286
  127.8 1.0 copy-done.4
  128.8 0.4 copy-done.5
  129.2 7.7 %shard_map.92 = (f32[6,64,256]{2,1,0:T(8,128)}, f32[6,64,256]{2,1,0:T(8,128)}, f32[6,64,256]{2,1,0:T(8,128)}, f32[6,64,256]{2,1,0:T(8,128)}) custom-call(s32[2]{0:T(128)} %pad_add_fusion.place, s32[2]{0:T(128)} %count.3, f32[4,256,128]{2,1,0:T(8,128)} %get-tuple-element.30.w_ref, f32[256,256]{1,0:T(8,128)} %get-tuple-element.31.schur, ...), custom_call_target="tpu_custom_call" | custom-call | flops 7000000000 | bytes 7000000 | tf_op jit(solution)/shard_map/pallas_call | solution.py:258
  137.0 3.3 %collective-permute-start.15 = (f32[6,64,256]{2,1,0:T(8,128)}, f32[6,64,256]{2,1,0:T(8,128)S(1)}, u32[]{:S(2)}, u32[]{:S(2)}) collective-permute-start(f32[6,64,256]{2,1,0:T(8,128)} %get-tuple-element.47), channel_id=1, source_target_pairs={{0,1},{2,3},{5,4},{7,6},{8,9},{10,11},{13,12},{15,14},{16,17},{18,... | collective-permute-start | bytes 1179656 | tf_op jit(solution)/shard_map/ppermute | solution.py:289
  140.3 3.1 %collective-permute-start.16 = (f32[6,64,256]{2,1,0:T(8,128)}, f32[6,64,256]{2,1,0:T(8,128)S(1)}, u32[]{:S(2)}, u32[]{:S(2)}) collective-permute-start(f32[6,64,256]{2,1,0:T(8,128)} %get-tuple-element.48), channel_id=1, source_target_pairs={{0,2},{2,0},{5,7},{7,5},{8,10},{10,8},{13,15},{15,13},{16,18},{18,... | collective-permute-start | bytes 1179656 | tf_op jit(solution)/shard_map/ppermute | solution.py:289
  143.4 1.3 collective-permute-start.17
  144.7 1.1 collective-permute-done.15.refs_1_
  145.8 13.6 %collective-permute-done.16.refs_2_ = f32[6,64,256]{2,1,0:T(8,128)S(1)} collective-permute-done((f32[6,64,256]{2,1,0:T(8,128)}, f32[6,64,256]{2,1,0:T(8,128)S(1)}, u32[]{:S(2)}, u32[]{:S(2)}) %collective-permute-start.16) | collective-permute-done | bytes 393248 | tf_op jit(solution)/shard_map/ppermute | solution.py:289
  159.5 0.7 copy-done.12
  160.2 0.2 copy-done.13
  160.4 2.3 %shard_map.93 = (f32[2,64,256]{2,1,0:T(8,128)}, f32[2,4,64,256]{3,2,1,0:T(8,128)}, f32[1,64,256]{2,1,0:T(8,128)}) custom-call(s32[2]{0:T(128)} %pad_add_fusion.place, f32[6,64,256]{2,1,0:T(8,128)} %get-tuple-element.46.refs_0_, f32[6,64,256]{2,1,0:T(8,128)} %copy-done.11, f32[6,64,256]{2,1,0:T(8,128)} %copy-done.12, f32[6,64,256]{2,1,0:T(8,128)} %copy-done.13), custom_call_target="tpu_custom_call" | custom-call | flops 2000000000 | bytes 2000000 | tf_op jit(solution)/shard_map/pallas_call | solution.py:258
  (34 shorter events, 0.1 us)
Async XLA Ops:
  3.5 24.0 %collective-permute-start = (f32[8,128,128]{2,1,0:T(8,128)}, f32[8,128,128]{2,1,0:T(8,128)S(1)}, u32[]{:S(2)}, u32[]{:S(2)}) collective-permute-start(f32[8,128,128]{2,1,0:T(8,128)} %get-tuple-element.28.own), channel_id=1, source_target_pairs={{1,0},{3,2},{4,5},{6,7},{9,8},{11,10},{12,13},{14,15},{17,16},{19,... | collective-permute-start | bytes 1572872 | tf_op jit(solution)/shard_map/ppermute | solution.py:286
  4.8 22.7 %collective-permute-start.1 = (f32[6,128,128]{2,1,0:T(8,128)}, f32[6,128,128]{2,1,0:T(8,128)S(1)}, u32[]{:S(2)}, u32[]{:S(2)}) collective-permute-start(f32[6,128,128]{2,1,0:T(8,128)} %get-tuple-element.29), channel_id=1, source_target_pairs={{2,0},{0,2},{7,5},{5,7},{10,8},{8,10},{15,13},{13,15},{18,16},{16,... | collective-permute-start | bytes 1179656 | tf_op jit(solution)/shard_map/ppermute | solution.py:286
  10.8 16.7 %collective-permute-start.2 = (f32[6,128,128]{2,1,0:T(8,128)}, f32[6,128,128]{2,1,0:T(8,128)S(1)}, u32[]{:S(2)}, u32[]{:S(2)}) collective-permute-start(f32[6,128,128]{2,1,0:T(8,128)} %get-tuple-element.29), channel_id=1, source_target_pairs={{3,0},{1,2},{6,5},{4,7},{11,8},{9,10},{14,13},{12,15},{19,16},{17,... | collective-permute-start | bytes 1179656 | tf_op jit(solution)/shard_map/ppermute | solution.py:286
  12.1 9.2 %collective-permute-start.8 = (f32[2,128,256]{2,1,0:T(8,128)}, f32[2,128,256]{2,1,0:T(8,128)S(1)}, u32[]{:S(2)}, u32[]{:S(2)}) collective-permute-start(f32[2,128,256]{2,1,0:T(8,128)} %get-tuple-element.39), channel_id=1, source_target_pairs={{0,8},{4,12},{8,0},{12,4},{16,24},{20,28},{24,16},{28,20},{1,9},{5... | collective-permute-start | bytes 786440 | tf_op jit(solution)/shard_map/ppermute | solution.py:295
  21.3 38.6 %copy-start = (f32[4,128,256]{2,1,0:T(8,128)}, f32[4,128,256]{2,1,0:T(8,128)S(1)}, u32[]{:S(2)}) copy-start(f32[4,128,256]{2,1,0:T(8,128)S(1)} %constant_dynamic-update-slice_fusion.low0) | copy-start | bytes 1572868
  21.3 41.8 %collective-permute-start.9 = (f32[4,128,256]{2,1,0:T(8,128)S(1)}, f32[4,128,256]{2,1,0:T(8,128)S(1)}, u32[]{:S(2)}, u32[]{:S(2)}) collective-permute-start(f32[4,128,256]{2,1,0:T(8,128)S(1)} %constant_dynamic-update-slice_fusion.low0), channel_id=1, source_target_pairs={{0,16},{4,20},{8,24},{12,28},{16,0},{20,4},{24,8},{28,12},{1,17},{... | collective-permute-start | bytes 1572872 | tf_op jit(solution)/shard_map/ppermute | solution.py:295
  27.5 7.2 %copy-start.9 = (f32[6,128,128]{2,1,0:T(8,128)}, f32[6,128,128]{2,1,0:T(8,128)S(1)}, u32[]{:S(2)}) copy-start(f32[6,128,128]{2,1,0:T(8,128)S(1)} %collective-permute-done.1.far2) | copy-start | bytes 1179652
  27.5 7.2 %copy-start.10 = (f32[6,128,128]{2,1,0:T(8,128)}, f32[6,128,128]{2,1,0:T(8,128)S(1)}, u32[]{:S(2)}) copy-start(f32[6,128,128]{2,1,0:T(8,128)S(1)} %collective-permute-done.2.far3) | copy-start | bytes 1179652
  27.6 7.2 %copy-start.7 = (f32[8,128,128]{2,1,0:T(8,128)}, f32[8,128,128]{2,1,0:T(8,128)S(1)}, u32[]{:S(2)}) copy-start(f32[8,128,128]{2,1,0:T(8,128)S(1)} %collective-permute-done.near) | copy-start | bytes 1572868
  27.6 11.3 %copy-start.14 = (f32[4,128,128]{2,1,0:T(8,128)S(1)}, f32[4,128,128]{2,1,0:T(8,128)}, u32[]{:S(2)}) copy-start(f32[4,128,128]{2,1,0:T(8,128)} %get-tuple-element.34.n0) | copy-start | bytes 786436
  27.6 35.7 %collective-permute-start.5 = (f32[4,128,128]{2,1,0:T(8,128)}, f32[4,128,128]{2,1,0:T(8,128)S(1)}, u32[]{:S(2)}, u32[]{:S(2)}) collective-permute-start(f32[4,128,128]{2,1,0:T(8,128)} %get-tuple-element.35), channel_id=1, source_target_pairs={{2,0},{0,2},{7,5},{5,7},{10,8},{8,10},{15,13},{13,15},{18,16},{16,... | collective-permute-start | bytes 786440 | tf_op jit(solution)/shard_map/ppermute | solution.py:286
  33.4 29.9 %collective-permute-start.6 = (f32[4,128,128]{2,1,0:T(8,128)}, f32[4,128,128]{2,1,0:T(8,128)S(1)}, u32[]{:S(2)}, u32[]{:S(2)}) collective-permute-start(f32[4,128,128]{2,1,0:T(8,128)} %get-tuple-element.35), channel_id=1, source_target_pairs={{3,0},{1,2},{6,5},{4,7},{11,8},{9,10},{14,13},{12,15},{19,16},{17,... | collective-permute-start | bytes 786440 | tf_op jit(solution)/shard_map/ppermute | solution.py:286
  37.0 26.3 %collective-permute-start.3 = (f32[4,128,256]{2,1,0:T(8,128)}, f32[4,128,256]{2,1,0:T(8,128)S(1)}, u32[]{:S(2)}, u32[]{:S(2)}) collective-permute-start(f32[4,128,256]{2,1,0:T(8,128)} %shard_map.87), channel_id=1, source_target_pairs={{5,0},{7,2},{0,5},{2,7},{13,8},{15,10},{8,13},{10,15},{21,16},{23,... | collective-permute-start | bytes 1572872 | tf_op jit(solution)/shard_map/ppermute | solution.py:292
  38.9 21.0 %collective-permute-start.4 = (f32[4,128,128]{2,1,0:T(8,128)S(1)}, f32[4,128,128]{2,1,0:T(8,128)}, u32[]{:S(2)}, u32[]{:S(2)}) collective-permute-start(f32[4,128,128]{2,1,0:T(8,128)S(1)} %copy-done.14), channel_id=1, source_target_pairs={{1,0},{3,2},{4,5},{6,7},{9,8},{11,10},{12,13},{14,15},{17,16},{19,... | collective-permute-start | bytes 786440 | tf_op jit(solution)/shard_map/ppermute | solution.py:286
  59.9 9.3 %collective-permute-start.10 = (f32[4,128,256]{2,1,0:T(8,128)S(1)}, f32[4,128,256]{2,1,0:T(8,128)S(1)}, u32[]{:S(2)}, u32[]{:S(2)}) collective-permute-start(f32[4,128,256]{2,1,0:T(8,128)S(1)} %constant_dynamic-update-slice_fusion.low0), channel_id=1, source_target_pairs={{0,4},{4,0},{8,12},{12,8},{16,20},{20,16},{24,28},{28,24},{1,5},{5... | collective-permute-start | bytes 1572872 | tf_op jit(solution)/shard_map/ppermute | solution.py:295
  63.2 4.8 %copy-start.1 = (f32[4,128,256]{2,1,0:T(8,128)}, f32[4,128,256]{2,1,0:T(8,128)S(1)}, u32[]{:S(2)}) copy-start(f32[4,128,256]{2,1,0:T(8,128)S(1)} %collective-permute-done.9.low1) | copy-start | bytes 1572868
  63.2 6.1 %collective-permute-start.11 = (f32[4,128,256]{2,1,0:T(8,128)S(1)}, f32[4,128,256]{2,1,0:T(8,128)S(1)}, u32[]{:S(2)}, u32[]{:S(2)}) collective-permute-start(f32[4,128,256]{2,1,0:T(8,128)S(1)} %collective-permute-done.9.low1), channel_id=1, source_target_pairs={{0,4},{4,0},{8,12},{12,8},{16,20},{20,16},{24,28},{28,24},{1,5},{5... | collective-permute-start | bytes 1572872 | tf_op jit(solution)/shard_map/ppermute | solution.py:295
  63.2 0.8 copy-start.15
  63.3 0.9 copy-start.16
  63.3 1.0 copy-start.8
  68.0 12.4 %collective-permute-start.7 = (f32[2,256,256]{2,1,0:T(8,128)}, f32[2,256,256]{2,1,0:T(8,128)}, u32[]{:S(2)}, u32[]{:S(2)}) collective-permute-start(f32[2,256,256]{2,1,0:T(8,128)} %get-tuple-element.37.own), channel_id=1, source_target_pairs={{5,0},{2,7},{13,8},{10,15},{21,16},{18,23},{29,24},{26,31}} | collective-permute-start | bytes 1572872 | tf_op jit(solution)/shard_map/ppermute | solution.py:292
  69.3 0.8 copy-start.2
  69.3 1.0 copy-start.3
  72.8 55.0 %collective-permute-start.13 = (f32[18,128,128]{2,1,0:T(8,128)}, f32[18,128,128]{2,1,0:T(8,128)S(1)}, u32[]{:S(2)}, u32[]{:S(2)}) collective-permute-start(f32[18,128,128]{2,1,0:T(8,128)} %get-tuple-element.45), channel_id=1, source_target_pairs={{2,0},{0,2},{7,5},{5,7},{10,8},{8,10},{15,13},{13,15},{18,16},{16,... | collective-permute-start | bytes 3538952 | tf_op jit(solution)/shard_map/ppermute | solution.py:286
  77.6 50.3 %collective-permute-start.14 = (f32[18,128,128]{2,1,0:T(8,128)}, f32[18,128,128]{2,1,0:T(8,128)S(1)}, u32[]{:S(2)}, u32[]{:S(2)}) collective-permute-start(f32[18,128,128]{2,1,0:T(8,128)} %get-tuple-element.45), channel_id=1, source_target_pairs={{3,0},{1,2},{6,5},{4,7},{11,8},{9,10},{14,13},{12,15},{19,16},{17,... | collective-permute-start | bytes 3538952 | tf_op jit(solution)/shard_map/ppermute | solution.py:286
  78.9 33.9 %collective-permute-start.12 = (f32[18,128,128]{2,1,0:T(8,128)}, f32[18,128,128]{2,1,0:T(8,128)S(1)}, u32[]{:S(2)}, u32[]{:S(2)}) collective-permute-start(f32[18,128,128]{2,1,0:T(8,128)} %get-tuple-element.44.refs_0_), channel_id=1, source_target_pairs={{1,0},{3,2},{4,5},{6,7},{9,8},{11,10},{12,13},{14,15},{17,16},{19,... | collective-permute-start | bytes 3538952 | tf_op jit(solution)/shard_map/ppermute | solution.py:286
  112.8 15.0 %copy-start.6 = (f32[18,128,128]{2,1,0:T(8,128)}, f32[18,128,128]{2,1,0:T(8,128)S(1)}, u32[]{:S(2)}) copy-start(f32[18,128,128]{2,1,0:T(8,128)S(1)} %collective-permute-done.12.refs_1_) | copy-start | bytes 3538948
  127.8 1.0 copy-start.4
  127.8 1.4 copy-start.5
  137.0 8.8 %collective-permute-start.15 = (f32[6,64,256]{2,1,0:T(8,128)}, f32[6,64,256]{2,1,0:T(8,128)S(1)}, u32[]{:S(2)}, u32[]{:S(2)}) collective-permute-start(f32[6,64,256]{2,1,0:T(8,128)} %get-tuple-element.47), channel_id=1, source_target_pairs={{0,1},{2,3},{5,4},{7,6},{8,9},{10,11},{13,12},{15,14},{16,17},{18,... | collective-permute-start | bytes 1179656 | tf_op jit(solution)/shard_map/ppermute | solution.py:289
  140.3 19.2 %collective-permute-start.16 = (f32[6,64,256]{2,1,0:T(8,128)}, f32[6,64,256]{2,1,0:T(8,128)S(1)}, u32[]{:S(2)}, u32[]{:S(2)}) collective-permute-start(f32[6,64,256]{2,1,0:T(8,128)} %get-tuple-element.48), channel_id=1, source_target_pairs={{0,2},{2,0},{5,7},{7,5},{8,10},{10,8},{13,15},{15,13},{16,18},{18,... | collective-permute-start | bytes 1179656 | tf_op jit(solution)/shard_map/ppermute | solution.py:289
  143.4 16.1 %collective-permute-start.17 = (f32[6,64,256]{2,1,0:T(8,128)}, f32[6,64,256]{2,1,0:T(8,128)S(1)}, u32[]{:S(2)}, u32[]{:S(2)}) collective-permute-start(f32[6,64,256]{2,1,0:T(8,128)} %get-tuple-element.49), channel_id=1, source_target_pairs={{0,3},{2,1},{5,6},{7,4},{8,11},{10,9},{13,14},{15,12},{16,19},{18,... | collective-permute-start | bytes 1179656 | tf_op jit(solution)/shard_map/ppermute | solution.py:289
  145.8 13.6 %copy-start.11 = (f32[6,64,256]{2,1,0:T(8,128)}, f32[6,64,256]{2,1,0:T(8,128)S(1)}, u32[]{:S(2)}) copy-start(f32[6,64,256]{2,1,0:T(8,128)S(1)} %collective-permute-done.15.refs_1_) | copy-start | bytes 1179652
  159.5 0.8 copy-start.12
  159.5 0.9 copy-start.13

commit v2 on v1

--- a/solution.py
+++ b/solution.py
@@ -153,12 +153,10 @@
                 rest[i - count] = near[which, i]
 
 
-def name_kernel(place, ids, low0, low1, high0, high1, _, __, rest_mine, rest_other, found, sems):
+def name_kernel(place, ids, low0, low1, high0, high1, mine_ref, other_ref):
     row, mine = place[0], place[1] >> 1
     clusters, slots = ids.shape
-    edge = found.shape[2]
-    copies = []
-    for side, (which, rest) in enumerate(((mine, rest_mine), (1 - mine, rest_other))):
+    for which, out in ((mine, mine_ref), (1 - mine, other_ref)):
         for k in range(1, slots):
             name = ids[which, k]
             apart = lax.div(name, clusters) ^ row
@@ -166,17 +164,8 @@
             inner = lax.rem(spot, low0.shape[0])
             late = spot >= low0.shape[0]
             low = jnp.where(late, low1[inner], low0[inner])
-            base = jnp.where((apart & 1) > 0, jnp.where(late, high1[inner], high0[inner]), low)
-            for b in range(2):
-                found[side, 2 * (k - 1) + b] = base[:, b * edge : (b + 1) * edge]
-        count = found.shape[1]
-        copy = pltpu.make_async_copy(
-            found.at[side], rest.at[pl.ds(rest.shape[0] - count, count)], sems.at[side]
-        )
-        copy.start()
-        copies.append(copy)
-    for copy in copies:
-        copy.wait()
+            high = jnp.where(late, high1[inner], high0[inner])
+            out[k - 1] = jnp.where((apart & 1) > 0, high, low)
 
 
 def coupling(w_ref, blocks, bases):
@@ -194,22 +183,22 @@
         part[index] = flipped[index, pl.ds(pl.multiple_of((z ^ j) * quarter, quarter), quarter), :]
 
 
-def near_first_kernel(place, count, w_ref, bases, n0, n1, n2, n3, schur, pair, flipped):
+def near_first_kernel(place, count, w_ref, bases, n0, n1, n2, n3, top, low, flipped):
     result = coupling(w_ref, [tall(n, 0) for n in (n0, n1, n2, n3)], [bases[j ^ 1] for j in range(4)])
     result = jnp.where(count[place[1] >> 1] > 0, result, 0.0)
-    pair[0] = schur[...]
-    pair[1] = result
+    half = top.shape[0]
+    top[...], low[...] = result[:half], result[half:]
     flipped[...] = result.T
 
 
 def near_rest_kernel(place, count, w_ref, schur, first, parent, *refs):
     z = place[1]
-    blocks, parts, flipped = refs[:4], refs[4:8], refs[8]
-    total = blocks[0].shape[0] // 6
+    blocks, named, parts, flipped = refs[:4], refs[4:8], refs[8:12], refs[12]
+    total = named[0].shape[0]
     flipped[0] = schur[...]
     flipped[1] = first[...]
     for k in range(total):
-        result = coupling(w_ref, [tall(n, 4 * k) for n in blocks], [wide(n, 4 * total + 2 * k, 2) for n in blocks])
+        result = coupling(w_ref, [tall(n, 4 * k) for n in blocks], [s[k] for s in named])
         flipped[k + 2] = jnp.where(count[z >> 1] > k + 1, result, 0.0).T
     flipped[total + 2] = parent[...]
     for i in range(total + 3):
@@ -236,15 +225,19 @@
     final[0] = jnp.where(swap == (row & 1), here, there)
 
 
-def parent_kernel(place, own, arrived, vt_ref, v_ref, flipped_ref):
-    size = own.shape[1]
+def parent_kernel(place, diag, near0, near1, diag_got, near0_got, near1_got, vt_ref, v_ref, flipped_ref):
+    size = diag.shape[0]
     swap = (place[0] & 1) > 0
-
-    def choose(a, b, index):
-        return jnp.where(swap, b[index], a[index])
-
-    top = jnp.concatenate([choose(own, arrived, 0), choose(own, arrived, 1)], axis=1)
-    low = jnp.concatenate([choose(arrived, own, 1), choose(arrived, own, 0)], axis=1)
+    near = jnp.concatenate([near0[...], near1[...]], axis=0)
+    near_got = jnp.concatenate([near0_got[...], near1_got[...]], axis=0)
+
+    def order(a, b):
+        return jnp.where(swap, b, a), jnp.where(swap, a, b)
+
+    diag_first, diag_second = order(diag[...], diag_got[...])
+    near_first, near_second = order(near, near_got)
+    top = jnp.concatenate([diag_first, near_first], axis=1)
+    low = jnp.concatenate([near_second, diag_second], axis=1)
     merged = jnp.concatenate([top, low], axis=0)
     dense = dot(dot(vt_ref[...], merged), v_ref[...])
     flipped_ref[...] = eliminate(dense, size)[1].T
@@ -318,7 +311,7 @@
         pieces.append(across(pieces[0], bit))
 
     near = near_blocks.reshape(clusters, slots * 4, edge, edge)
-    rest_blocks = (slots - 1) * 6
+    rest_blocks = (slots - 1) * 4
     v = parent_bases[0]
     split = call(
         split_kernel,
@@ -326,22 +319,11 @@
         [place],
         [near, v],
     )
-    anywhere = pl.BlockSpec(memory_space=pl.ANY)
-    swapped = [across(piece, 1) for piece in pieces]
-    scalar, vmem = pl.BlockSpec(memory_space=pltpu.SMEM), pl.BlockSpec(memory_space=pltpu.VMEM)
-    rest = pl.pallas_call(
-        name_kernel,
-        out_shape=[jax.ShapeDtypeStruct((rest_blocks, edge, edge), jnp.float32)] * 2,
-        in_specs=[scalar] * 2 + [vmem] * 4 + [anywhere] * 2,
-        out_specs=[anywhere] * 2,
-        scratch_shapes=[
-            pltpu.VMEM((2, (slots - 1) * 2, edge, edge), jnp.float32),
-            pltpu.SemaphoreType.DMA((2,)),
-        ],
-        input_output_aliases={6: 0, 7: 1},
-    )(place, near_ids, *pieces, *swapped, split[2], split[3])
+    swapped = []
+    for piece in pieces:
+        swapped.append(across(piece, 1))
     n_early = gather(*after((split[0], split[1]), leaf[1:]))
-    n_rest = gather(*after(rest, leaf[1:]))
+    n_rest = gather(*after((split[2], split[3]), leaf[1:]))
     (skeletons,) = call(skeleton_kernel, [(4, edge, skeleton)], [place], leaf)
     sibling = from_sibling(skeletons, owned)
 
@@ -349,24 +331,31 @@
         leaf_kernel, [(4, skeleton, edge), (skeleton, skeleton)], [place], leaf, 22
     )
 
-    pair, first = call(
+    diag_got = from_sibling(schur, heads)
+    top, low, first = call(
         near_first_kernel,
-        [(2, skeleton, skeleton), (skeleton, skeleton)],
+        [(skeleton // 2, skeleton)] * 2 + [(skeleton, skeleton)],
         [place, near_count],
-        [w, sibling, *n_early, schur],
+        [w, sibling, *n_early],
         4,
     )
-    arrived = from_sibling(pair, heads)
-
+    top_got = from_sibling(top, heads)
+    low_got = from_sibling(low, heads)
+    chosen = call(name_kernel, [(slots - 1, edge, skeleton)] * 2, [place, near_ids], [*after(pieces, first), *swapped])
+    named = gather(*chosen)
     (parent,) = call(
-        parent_kernel, [(skeleton, skeleton)], [place], [pair, arrived, split[4], v], 22
+        parent_kernel,
+        [(skeleton, skeleton)],
+        [place],
+        [schur, top, low, diag_got, top_got, low_got, split[4], v],
+        22,
     )
     total = slots + 2
     results = call(
         near_rest_kernel,
         [(total, quarter, skeleton)] * 4,
         [place, near_count],
-        [w, schur, first, parent, *n_rest],
+        [w, schur, first, parent, *n_rest, *named],
         7,
         [(total, skeleton, skeleton)],
     )

time: 165 us -> 162 us (0.982)
  waiting for transfers between devices: 49.8 us -> 39.4 us
  starting transfers between devices: 41.8 us -> 51.1 us
  local copies, waits for them, and re-layouts: 5.31 us -> 3.41 us
    ppermute x9 -> x12, waiting for transfers between devices: 32.5 us -> 24.6 us  [to_owner(): lax.ppermute(x, both, [(r * n_col + (z ^ j), r * n_col + z) for r, z in o...]
    ppermute x9 -> x12, starting transfers between devices: 24.5 us -> 30.4 us  [to_owner(): lax.ppermute(x, both, [(r * n_col + (z ^ j), r * n_col + z) for r, z in o...]
    ppermute x2 -> x4, starting transfers between devices: 3.19 us -> 5.91 us  [from_sibling(): lax.ppermute(x, both, [((r ^ 1) * n_col + (z ^ 1), r * n_col + z) for r,...]
    ppermute x4, waiting for transfers between devices: 2.57 us -> 0.01 us  [across(): return lax.ppermute(x, 'row', [(r, r ^ bit) for r in range(n_row)])]
    pallas_call x1 -> x0, Pallas kernels: 2.55 us -> none  [levels(): pl.pallas_call(name_kernel, out_shape=[jax.ShapeDtypeStruct((rest_blocks,...]
    ppermute x3, starting transfers between devices: 7.68 us -> 10.1 us  [from_owner(): lax.ppermute(x, both, [(r * n_col + z, r * n_col + (z ^ j)) for r, z in o...]
    pallas_call x8 -> x9, Pallas kernels: 61.6 us -> 64 us  [call(): pl.pallas_call(kernel, out_shape=shapes, in_specs=specs, out_specs=[vmem]...]
    unnamed x35 -> x33, local copies, waits for them, and re-layouts: 5.29 us -> 3.39 us
  transfers between devices with their start and end apart: 18 -> 23, of which waited for: 6 -> 6; matrix products, arithmetic and copies ran while one was open for 1% -> 1% of each run, Pallas kernels for 32% -> 32%
where the time goes in v2:
time: 162 us; the launch traced here: 160 us
  Pallas kernels  64 us (40%)
  starting transfers between devices  51.1 us (32%)
  waiting for transfers between devices  39.4 us (24%)
  local copies, waits for them, and re-layouts  3.41 us (2%)
    pallas_call x9, Pallas kernels, call(): pl.pallas_call(kernel, out_shape=shapes, in_specs=specs, out_specs=[vmem]...  64 us
    ppermute x12, starting transfers between devices, to_owner(): lax.ppermute(x, both, [(r * n_col + (z ^ j), r * n_col + z) for r, z in o...  30.4 us
    ppermute x12, waiting for transfers between devices, to_owner(): lax.ppermute(x, both, [(r * n_col + (z ^ j), r * n_col + z) for r, z in o...  24.6 us
    ppermute x3, waiting for transfers between devices, from_owner(): lax.ppermute(x, both, [(r * n_col + z, r * n_col + (z ^ j)) for r, z in o...  14.8 us
    ppermute x3, starting transfers between devices, from_owner(): lax.ppermute(x, both, [(r * n_col + z, r * n_col + (z ^ j)) for r, z in o...  10.1 us
    ppermute x4, starting transfers between devices, from_sibling(): lax.ppermute(x, both, [((r ^ 1) * n_col + (z ^ 1), r * n_col + z) for r,...  5.91 us
    ppermute x4, starting transfers between devices, across(): return lax.ppermute(x, 'row', [(r, r ^ bit) for r in range(n_row)])  4.7 us
    unnamed x33, local copies, waits for them, and re-layouts  3.39 us
  transfers between devices with their start and end apart: 23, of which 6 were waited for; matrix products, arithmetic and copies ran while one was open for 1% of the time, Pallas kernels for 32%

profile of v2, /device:TPU:0, one launch (start us, length us, event | category | flops | bytes accessed | tf_op | source)
XLA Modules:
  0.0 159.5 jit_solution(5359585657396939027)
XLA Ops:
  0.6 0.6 pad_add_fusion.place
  1.3 2.3 %shard_map.85 = (f32[8,128,128]{2,1,0:T(8,128)}, f32[6,128,128]{2,1,0:T(8,128)}, f32[2,128,256]{2,1,0:T(8,128)}) custom-call(s32[2]{0:T(128)} %pad_add_fusion.place, f32[2,512,128]{2,1,0:T(8,128)} %diag.1, f32[2,128,512]{2,1,0:T(8,128)} %bases.1), custom_call_target="tpu_custom_call" | custom-call | flops 2000000000 | bytes 2000000 | tf_op jit(solution)/shard_map/pallas_call | solution.py:251
  3.6 3.0 %collective-permute-start.13 = (f32[2,128,256]{2,1,0:T(8,128)}, f32[2,128,256]{2,1,0:T(8,128)S(1)}, u32[]{:S(2)}, u32[]{:S(2)}) collective-permute-start(f32[2,128,256]{2,1,0:T(8,128)} %get-tuple-element.47), channel_id=1, source_target_pairs={{0,8},{4,12},{8,0},{12,4},{16,24},{20,28},{24,16},{28,20},{1,9},{5... | collective-permute-start | bytes 786440 | tf_op jit(solution)/shard_map/ppermute | solution.py:288
  6.5 1.3 collective-permute-start
  7.8 4.5 %collective-permute-start.1 = (f32[6,128,128]{2,1,0:T(8,128)}, f32[6,128,128]{2,1,0:T(8,128)S(1)}, u32[]{:S(2)}, u32[]{:S(2)}) collective-permute-start(f32[6,128,128]{2,1,0:T(8,128)} %get-tuple-element.32), channel_id=1, source_target_pairs={{2,0},{0,2},{7,5},{5,7},{10,8},{8,10},{15,13},{13,15},{18,16},{16,... | collective-permute-start | bytes 1179656 | tf_op jit(solution)/shard_map/ppermute | solution.py:279
  12.3 1.3 collective-permute-start.2
  13.6 1.0 constant_dynamic-update-slice_fusion.1
  14.6 1.6 collective-permute-start.14
  16.2 3.8 %shard_map.88 = (f32[4,128,128]{2,1,0:T(8,128)}, f32[4,128,128]{2,1,0:T(8,128)}, f32[12,128,128]{2,1,0:T(8,128)}, f32[12,128,128]{2,1,0:T(8,128)}, f32[512,512]{1,0:T(8,128)}) custom-call(s32[2]{0:T(128)} %pad_add_fusion.place, f32[2,16,128,128]{3,2,1,0:T(8,128)} %bitcast.7, f32[512,512]{1,0:T(8,128)} %bitcast.8), custom_call_target="tpu_custom_call" | custom-call | flops 2000000000 | bytes 2000000 | tf_op jit(solution)/shard_map/pallas_call | solution.py:251
  20.1 9.4 %collective-permute-done.1.far2 = f32[6,128,128]{2,1,0:T(8,128)S(1)} collective-permute-done((f32[6,128,128]{2,1,0:T(8,128)}, f32[6,128,128]{2,1,0:T(8,128)S(1)}, u32[]{:S(2)}, u32[]{:S(2)}) %collective-permute-start.1) | collective-permute-done | bytes 393248 | tf_op jit(solution)/shard_map/ppermute | solution.py:279
  29.5 0.0 collective-permute-done.2.far3
  29.5 0.0 collective-permute-done.near
  29.5 1.3 collective-permute-start.4
  30.8 5.0 %collective-permute-start.5 = (f32[4,128,128]{2,1,0:T(8,128)}, f32[4,128,128]{2,1,0:T(8,128)}, u32[]{:S(2)}, u32[]{:S(2)}) collective-permute-start(f32[4,128,128]{2,1,0:T(8,128)} %get-tuple-element.38), channel_id=1, source_target_pairs={{2,0},{0,2},{7,5},{5,7},{10,8},{8,10},{15,13},{13,15},{18,16},{16,... | collective-permute-start | bytes 786440 | tf_op jit(solution)/shard_map/ppermute | solution.py:279
  35.8 0.1 collective-permute-start.15
  35.9 1.3 collective-permute-start.6
  37.2 2.3 %shard_map.87 = f32[4,128,256]{2,1,0:T(8,128)} custom-call(s32[2]{0:T(128)} %pad_add_fusion.place, f32[8,128,128]{2,1,0:T(8,128)} %get-tuple-element.31.own, f32[8,128,128]{2,1,0:T(8,128)} %copy-done.5, f32[6,128,128]{2,1,0:T(8,128)} %copy-done.6, f32[6,128,128]{2,1,0:T(8,128)} %copy-done.7), custom_call_target="tpu_custom_call" | custom-call | flops 2000000000 | bytes 2000000 | tf_op jit(solution)/shard_map/pallas_call | solution.py:251
  39.6 2.0 %collective-permute-start.3 = (f32[4,128,256]{2,1,0:T(8,128)}, f32[4,128,256]{2,1,0:T(8,128)}, u32[]{:S(2)}, u32[]{:S(2)}) collective-permute-start(f32[4,128,256]{2,1,0:T(8,128)} %shard_map.87), channel_id=1, source_target_pairs={{5,0},{7,2},{0,5},{2,7},{13,8},{15,10},{8,13},{10,15},{21,16},{23,... | collective-permute-start | bytes 1572872 | tf_op jit(solution)/shard_map/ppermute | solution.py:285
  41.6 5.9 %collective-permute-done.5.n2 = f32[4,128,128]{2,1,0:T(8,128)} collective-permute-done((f32[4,128,128]{2,1,0:T(8,128)}, f32[4,128,128]{2,1,0:T(8,128)}, u32[]{:S(2)}, u32[]{:S(2)}) %collective-permute-start.5) | collective-permute-done | bytes 262176 | tf_op jit(solution)/shard_map/ppermute | solution.py:279
  47.5 1.3 collective-permute-start.10
  48.8 0.0 collective-permute-done.14.low1
  48.8 0.1 collective-permute-start.16
  48.9 19.8 %shard_map.86 = (f32[4,256,128]{2,1,0:T(8,128)}, f32[256,256]{1,0:T(8,128)}) custom-call(s32[2]{0:T(128)} %pad_add_fusion.place, f32[8,128,128]{2,1,0:T(8,128)} %get-tuple-element.31.own, f32[8,128,128]{2,1,0:T(8,128)} %copy-done.5, f32[6,128,128]{2,1,0:T(8,128)} %copy-done.6, f32[6,128,128]{2,1,0:T(8,128)} %copy-done.7), custom_call_target="tpu_custom_call" | custom-call | flops 22000001024 | bytes 22000000 | tf_op jit(solution)/shard_map/pallas_call | solution.py:251
  68.7 1.3 collective-permute-start.7
  70.0 5.4 %collective-permute-start.11 = (f32[12,128,128]{2,1,0:T(8,128)S(1)}, f32[12,128,128]{2,1,0:T(8,128)}, u32[]{:S(2)}, u32[]{:S(2)}) collective-permute-start(f32[12,128,128]{2,1,0:T(8,128)S(1)} %copy-done.2), channel_id=1, source_target_pairs={{2,0},{0,2},{7,5},{5,7},{10,8},{8,10},{15,13},{13,15},{18,16},{16,... | collective-permute-start | bytes 2359304 | tf_op jit(solution)/shard_map/ppermute | solution.py:279
  75.4 3.5 %shard_map.89 = (f32[128,256]{1,0:T(8,128)}, f32[128,256]{1,0:T(8,128)}, f32[256,256]{1,0:T(8,128)}) custom-call(s32[2]{0:T(128)} %pad_add_fusion.place, s32[2]{0:T(128)} %count.3, f32[4,256,128]{2,1,0:T(8,128)} %get-tuple-element.33.w_ref, f32[4,128,256]{2,1,0:T(8,128)} %collective-permute-done.3.bases, f32[4,128,128]{2,1,0:T(8,128)} %get-tuple-element.37.n0, ...), custom_call_target="tpu_custom_call" | custom-call | flops 4000000000 | bytes 4000000 | tf_op jit(solution)/shard_map/pallas_call | solution.py:251
  78.9 1.3 collective-permute-start.8
  80.2 1.3 collective-permute-start.9
  81.5 2.5 %shard_map.91 = (f32[3,128,256]{2,1,0:T(8,128)}, f32[3,128,256]{2,1,0:T(8,128)}) custom-call(s32[2]{0:T(128)} %pad_add_fusion.place, s32[2,4]{1,0:T(2,128)} %ids.1, f32[4,128,256]{2,1,0:T(8,128)} %copy-done, f32[4,128,256]{2,1,0:T(8,128)} %copy-done.4, f32[4,128,256]{2,1,0:T(8,128)} %collective-permute-done.15.high0, ...), custom_call_target="tpu_custom_call" | custom-call | flops 2000000000 | bytes 2000000 | tf_op jit(solution)/shard_map/pallas_call | solution.py:251
  84.1 1.3 collective-permute-start.12
  85.4 0.0 collective-permute-done.8.near0_got
  85.4 5.0 %collective-permute-start.18 = (f32[3,128,256]{2,1,0:T(8,128)}, f32[3,128,256]{2,1,0:T(8,128)S(1)}, u32[]{:S(2)}, u32[]{:S(2)}) collective-permute-start(f32[3,128,256]{2,1,0:T(8,128)} %get-tuple-element.51), channel_id=1, source_target_pairs={{2,0},{0,2},{7,5},{5,7},{10,8},{8,10},{15,13},{13,15},{18,16},{16,... | collective-permute-start | bytes 1179656 | tf_op jit(solution)/shard_map/ppermute | solution.py:279
  90.5 1.3 collective-permute-start.19
  91.8 1.5 collective-permute-start.17
  93.3 19.7 %shard_map.90.parent = f32[256,256]{1,0:T(8,128)} custom-call(s32[2]{0:T(128)} %pad_add_fusion.place, f32[256,256]{1,0:T(8,128)} %get-tuple-element.34.diag.schur, f32[128,256]{1,0:T(8,128)} %get-tuple-element.40.near0, f32[128,256]{1,0:T(8,128)} %get-tuple-element.41.near1, f32[256,256]{1,0:T(8,128)} %collective-permute-done.7.diag_got, ...), custom_call_target="tpu_custom_call" | custom-call | flops 22000001024 | bytes 22000000 | tf_op jit(solution)/shard_map/pallas_call | solution.py:251
  113.0 0.9 collective-permute-done.11.refs_2_
  113.9 8.3 %collective-permute-done.18.refs_6_ = f32[3,128,256]{2,1,0:T(8,128)S(1)} collective-permute-done((f32[3,128,256]{2,1,0:T(8,128)}, f32[3,128,256]{2,1,0:T(8,128)S(1)}, u32[]{:S(2)}, u32[]{:S(2)}) %collective-permute-start.18) | collective-permute-done | bytes 393248 | tf_op jit(solution)/shard_map/ppermute | solution.py:279
  122.2 0.7 copy-done.8
  122.9 0.7 copy-done.9
  123.7 7.7 %shard_map.92 = (f32[6,64,256]{2,1,0:T(8,128)}, f32[6,64,256]{2,1,0:T(8,128)}, f32[6,64,256]{2,1,0:T(8,128)}, f32[6,64,256]{2,1,0:T(8,128)}) custom-call(s32[2]{0:T(128)} %pad_add_fusion.place, s32[2]{0:T(128)} %count.3, f32[4,256,128]{2,1,0:T(8,128)} %get-tuple-element.33.w_ref, f32[256,256]{1,0:T(8,128)} %get-tuple-element.34.diag.schur, ...), custom_call_target="tpu_custom_call" | custom-call | flops 7000000000 | bytes 7000000 | tf_op jit(solution)/shard_map/pallas_call | solution.py:251
  131.4 5.7 %collective-permute-start.20 = (f32[6,64,256]{2,1,0:T(8,128)}, f32[6,64,256]{2,1,0:T(8,128)S(1)}, u32[]{:S(2)}, u32[]{:S(2)}) collective-permute-start(f32[6,64,256]{2,1,0:T(8,128)} %get-tuple-element.53), channel_id=1, source_target_pairs={{0,1},{2,3},{5,4},{7,6},{8,9},{10,11},{13,12},{15,14},{16,17},{18,... | collective-permute-start | bytes 1179656 | tf_op jit(solution)/shard_map/ppermute | solution.py:282
  137.2 3.1 %collective-permute-start.21 = (f32[6,64,256]{2,1,0:T(8,128)}, f32[6,64,256]{2,1,0:T(8,128)S(1)}, u32[]{:S(2)}, u32[]{:S(2)}) collective-permute-start(f32[6,64,256]{2,1,0:T(8,128)} %get-tuple-element.54), channel_id=1, source_target_pairs={{0,2},{2,0},{5,7},{7,5},{8,10},{10,8},{13,15},{15,13},{16,18},{18,... | collective-permute-start | bytes 1179656 | tf_op jit(solution)/shard_map/ppermute | solution.py:282
  140.3 1.3 collective-permute-start.22
  141.6 1.1 collective-permute-done.20.refs_1_
  142.7 13.6 %collective-permute-done.21.refs_2_ = f32[6,64,256]{2,1,0:T(8,128)S(1)} collective-permute-done((f32[6,64,256]{2,1,0:T(8,128)}, f32[6,64,256]{2,1,0:T(8,128)S(1)}, u32[]{:S(2)}, u32[]{:S(2)}) %collective-permute-start.21) | collective-permute-done | bytes 393248 | tf_op jit(solution)/shard_map/ppermute | solution.py:282
  156.4 0.8 copy-done.12
  157.1 0.1 copy-done.13
  157.3 2.3 %shard_map.93 = (f32[2,64,256]{2,1,0:T(8,128)}, f32[2,4,64,256]{3,2,1,0:T(8,128)}, f32[1,64,256]{2,1,0:T(8,128)}) custom-call(s32[2]{0:T(128)} %pad_add_fusion.place, f32[6,64,256]{2,1,0:T(8,128)} %get-tuple-element.52.refs_0_, f32[6,64,256]{2,1,0:T(8,128)} %copy-done.11, f32[6,64,256]{2,1,0:T(8,128)} %copy-done.12, f32[6,64,256]{2,1,0:T(8,128)} %copy-done.13), custom_call_target="tpu_custom_call" | custom-call | flops 2000000000 | bytes 2000000 | tf_op jit(solution)/shard_map/pallas_call | solution.py:251
  (42 shorter events, 0.1 us)
Async XLA Ops:
  3.6 11.0 %collective-permute-start.13 = (f32[2,128,256]{2,1,0:T(8,128)}, f32[2,128,256]{2,1,0:T(8,128)S(1)}, u32[]{:S(2)}, u32[]{:S(2)}) collective-permute-start(f32[2,128,256]{2,1,0:T(8,128)} %get-tuple-element.47), channel_id=1, source_target_pairs={{0,8},{4,12},{8,0},{12,4},{16,24},{20,28},{24,16},{28,20},{1,9},{5... | collective-permute-start | bytes 786440 | tf_op jit(solution)/shard_map/ppermute | solution.py:288
  6.5 22.9 %collective-permute-start = (f32[8,128,128]{2,1,0:T(8,128)}, f32[8,128,128]{2,1,0:T(8,128)S(1)}, u32[]{:S(2)}, u32[]{:S(2)}) collective-permute-start(f32[8,128,128]{2,1,0:T(8,128)} %get-tuple-element.31.own), channel_id=1, source_target_pairs={{1,0},{3,2},{4,5},{6,7},{9,8},{11,10},{12,13},{14,15},{17,16},{19,... | collective-permute-start | bytes 1572872 | tf_op jit(solution)/shard_map/ppermute | solution.py:279
  7.8 21.6 %collective-permute-start.1 = (f32[6,128,128]{2,1,0:T(8,128)}, f32[6,128,128]{2,1,0:T(8,128)S(1)}, u32[]{:S(2)}, u32[]{:S(2)}) collective-permute-start(f32[6,128,128]{2,1,0:T(8,128)} %get-tuple-element.32), channel_id=1, source_target_pairs={{2,0},{0,2},{7,5},{5,7},{10,8},{8,10},{15,13},{13,15},{18,16},{16,... | collective-permute-start | bytes 1179656 | tf_op jit(solution)/shard_map/ppermute | solution.py:279
  12.3 17.1 %collective-permute-start.2 = (f32[6,128,128]{2,1,0:T(8,128)}, f32[6,128,128]{2,1,0:T(8,128)S(1)}, u32[]{:S(2)}, u32[]{:S(2)}) collective-permute-start(f32[6,128,128]{2,1,0:T(8,128)} %get-tuple-element.32), channel_id=1, source_target_pairs={{3,0},{1,2},{6,5},{4,7},{11,8},{9,10},{14,13},{12,15},{19,16},{17,... | collective-permute-start | bytes 1179656 | tf_op jit(solution)/shard_map/ppermute | solution.py:279
  14.6 21.2 %copy-start = (f32[4,128,256]{2,1,0:T(8,128)}, f32[4,128,256]{2,1,0:T(8,128)S(1)}, u32[]{:S(2)}) copy-start(f32[4,128,256]{2,1,0:T(8,128)S(1)} %constant_dynamic-update-slice_fusion.low0) | copy-start | bytes 1572868
  14.6 34.2 %collective-permute-start.14 = (f32[4,128,256]{2,1,0:T(8,128)S(1)}, f32[4,128,256]{2,1,0:T(8,128)S(1)}, u32[]{:S(2)}, u32[]{:S(2)}) collective-permute-start(f32[4,128,256]{2,1,0:T(8,128)S(1)} %constant_dynamic-update-slice_fusion.low0), channel_id=1, source_target_pairs={{0,16},{4,20},{8,24},{12,28},{16,0},{20,4},{24,8},{28,12},{1,17},{... | collective-permute-start | bytes 1572872 | tf_op jit(solution)/shard_map/ppermute | solution.py:288
  29.5 7.7 %copy-start.6 = (f32[6,128,128]{2,1,0:T(8,128)}, f32[6,128,128]{2,1,0:T(8,128)S(1)}, u32[]{:S(2)}) copy-start(f32[6,128,128]{2,1,0:T(8,128)S(1)} %collective-permute-done.1.far2) | copy-start | bytes 1179652
  29.5 7.7 %copy-start.7 = (f32[6,128,128]{2,1,0:T(8,128)}, f32[6,128,128]{2,1,0:T(8,128)S(1)}, u32[]{:S(2)}) copy-start(f32[6,128,128]{2,1,0:T(8,128)S(1)} %collective-permute-done.2.far3) | copy-start | bytes 1179652
  29.5 7.7 %copy-start.5 = (f32[8,128,128]{2,1,0:T(8,128)}, f32[8,128,128]{2,1,0:T(8,128)S(1)}, u32[]{:S(2)}) copy-start(f32[8,128,128]{2,1,0:T(8,128)S(1)} %collective-permute-done.near) | copy-start | bytes 1572868
  29.5 10.1 %collective-permute-start.4 = (f32[4,128,128]{2,1,0:T(8,128)}, f32[4,128,128]{2,1,0:T(8,128)}, u32[]{:S(2)}, u32[]{:S(2)}) collective-permute-start(f32[4,128,128]{2,1,0:T(8,128)} %get-tuple-element.37.n0), channel_id=1, source_target_pairs={{1,0},{3,2},{4,5},{6,7},{9,8},{11,10},{12,13},{14,15},{17,16},{19,... | collective-permute-start | bytes 786440 | tf_op jit(solution)/shard_map/ppermute | solution.py:279
  30.8 16.7 %collective-permute-start.5 = (f32[4,128,128]{2,1,0:T(8,128)}, f32[4,128,128]{2,1,0:T(8,128)}, u32[]{:S(2)}, u32[]{:S(2)}) collective-permute-start(f32[4,128,128]{2,1,0:T(8,128)} %get-tuple-element.38), channel_id=1, source_target_pairs={{2,0},{0,2},{7,5},{5,7},{10,8},{8,10},{15,13},{13,15},{18,16},{16,... | collective-permute-start | bytes 786440 | tf_op jit(solution)/shard_map/ppermute | solution.py:279
  35.8 43.1 %collective-permute-start.15 = (f32[4,128,256]{2,1,0:T(8,128)S(1)}, f32[4,128,256]{2,1,0:T(8,128)}, u32[]{:S(2)}, u32[]{:S(2)}) collective-permute-start(f32[4,128,256]{2,1,0:T(8,128)S(1)} %constant_dynamic-update-slice_fusion.low0), channel_id=1, source_target_pairs={{0,4},{4,0},{8,12},{12,8},{16,20},{20,16},{24,28},{28,24},{1,5},{5... | collective-permute-start | bytes 1572872 | tf_op jit(solution)/shard_map/ppermute | solution.py:288
  35.9 32.8 %collective-permute-start.6 = (f32[4,128,128]{2,1,0:T(8,128)}, f32[4,128,128]{2,1,0:T(8,128)}, u32[]{:S(2)}, u32[]{:S(2)}) collective-permute-start(f32[4,128,128]{2,1,0:T(8,128)} %get-tuple-element.38), channel_id=1, source_target_pairs={{3,0},{1,2},{6,5},{4,7},{11,8},{9,10},{14,13},{12,15},{19,16},{17,... | collective-permute-start | bytes 786440 | tf_op jit(solution)/shard_map/ppermute | solution.py:279
  37.2 10.3 %copy-start.1 = (f32[12,128,128]{2,1,0:T(8,128)S(1)}, f32[12,128,128]{2,1,0:T(8,128)}, u32[]{:S(2)}) copy-start(f32[12,128,128]{2,1,0:T(8,128)} %get-tuple-element.45.refs_0_) | copy-start | bytes 2359300
  39.6 30.5 %copy-start.2 = (f32[12,128,128]{2,1,0:T(8,128)S(1)}, f32[12,128,128]{2,1,0:T(8,128)}, u32[]{:S(2)}) copy-start(f32[12,128,128]{2,1,0:T(8,128)} %get-tuple-element.46) | copy-start | bytes 2359300
  39.6 30.4 %collective-permute-start.3 = (f32[4,128,256]{2,1,0:T(8,128)}, f32[4,128,256]{2,1,0:T(8,128)}, u32[]{:S(2)}, u32[]{:S(2)}) collective-permute-start(f32[4,128,256]{2,1,0:T(8,128)} %shard_map.87), channel_id=1, source_target_pairs={{5,0},{7,2},{0,5},{2,7},{13,8},{15,10},{8,13},{10,15},{21,16},{23,... | collective-permute-start | bytes 1572872 | tf_op jit(solution)/shard_map/ppermute | solution.py:285
  47.5 44.2 %collective-permute-start.10 = (f32[12,128,128]{2,1,0:T(8,128)S(1)}, f32[12,128,128]{2,1,0:T(8,128)S(1)}, u32[]{:S(2)}, u32[]{:S(2)}) collective-permute-start(f32[12,128,128]{2,1,0:T(8,128)S(1)} %copy-done.1), channel_id=1, source_target_pairs={{1,0},{3,2},{4,5},{6,7},{9,8},{11,10},{12,13},{14,15},{17,16},{19,... | collective-permute-start | bytes 2359304 | tf_op jit(solution)/shard_map/ppermute | solution.py:279
  48.8 19.9 %copy-start.4 = (f32[4,128,256]{2,1,0:T(8,128)}, f32[4,128,256]{2,1,0:T(8,128)S(1)}, u32[]{:S(2)}) copy-start(f32[4,128,256]{2,1,0:T(8,128)S(1)} %collective-permute-done.14.low1) | copy-start | bytes 1572868
  48.8 31.4 %collective-permute-start.16 = (f32[4,128,256]{2,1,0:T(8,128)S(1)}, f32[4,128,256]{2,1,0:T(8,128)}, u32[]{:S(2)}, u32[]{:S(2)}) collective-permute-start(f32[4,128,256]{2,1,0:T(8,128)S(1)} %collective-permute-done.14.low1), channel_id=1, source_target_pairs={{0,4},{4,0},{8,12},{12,8},{16,20},{20,16},{24,28},{28,24},{1,5},{5... | collective-permute-start | bytes 1572872 | tf_op jit(solution)/shard_map/ppermute | solution.py:288
  68.7 15.4 %collective-permute-start.7 = (f32[256,256]{1,0:T(8,128)}, f32[256,256]{1,0:T(8,128)}, u32[]{:S(2)}, u32[]{:S(2)}) collective-permute-start(f32[256,256]{1,0:T(8,128)} %get-tuple-element.34.diag.schur), channel_id=1, source_target_pairs={{5,0},{2,7},{13,8},{10,15},{21,16},{18,23},{29,24},{26,31}} | collective-permute-start | bytes 786440 | tf_op jit(solution)/shard_map/ppermute | solution.py:285
  70.0 43.9 %collective-permute-start.11 = (f32[12,128,128]{2,1,0:T(8,128)S(1)}, f32[12,128,128]{2,1,0:T(8,128)}, u32[]{:S(2)}, u32[]{:S(2)}) collective-permute-start(f32[12,128,128]{2,1,0:T(8,128)S(1)} %copy-done.2), channel_id=1, source_target_pairs={{2,0},{0,2},{7,5},{5,7},{10,8},{8,10},{15,13},{13,15},{18,16},{16,... | collective-permute-start | bytes 2359304 | tf_op jit(solution)/shard_map/ppermute | solution.py:279
  78.9 6.5 %collective-permute-start.8 = (f32[128,256]{1,0:T(8,128)}, f32[128,256]{1,0:T(8,128)S(1)}, u32[]{:S(2)}, u32[]{:S(2)}) collective-permute-start(f32[128,256]{1,0:T(8,128)} %get-tuple-element.40.near0), channel_id=1, source_target_pairs={{5,0},{2,7},{13,8},{10,15},{21,16},{18,23},{29,24},{26,31}} | collective-permute-start | bytes 393224 | tf_op jit(solution)/shard_map/ppermute | solution.py:285
  80.2 10.2 %collective-permute-start.9 = (f32[128,256]{1,0:T(8,128)}, f32[128,256]{1,0:T(8,128)S(1)}, u32[]{:S(2)}, u32[]{:S(2)}) collective-permute-start(f32[128,256]{1,0:T(8,128)} %get-tuple-element.41.near1), channel_id=1, source_target_pairs={{5,0},{2,7},{13,8},{10,15},{21,16},{18,23},{29,24},{26,31}} | collective-permute-start | bytes 393224 | tf_op jit(solution)/shard_map/ppermute | solution.py:285
  84.1 29.8 %collective-permute-start.12 = (f32[12,128,128]{2,1,0:T(8,128)S(1)}, f32[12,128,128]{2,1,0:T(8,128)}, u32[]{:S(2)}, u32[]{:S(2)}) collective-permute-start(f32[12,128,128]{2,1,0:T(8,128)S(1)} %copy-done.2), channel_id=1, source_target_pairs={{3,0},{1,2},{6,5},{4,7},{11,8},{9,10},{14,13},{12,15},{19,16},{17,... | collective-permute-start | bytes 2359304 | tf_op jit(solution)/shard_map/ppermute | solution.py:279
  85.4 7.8 %copy-start.14 = (f32[128,256]{1,0:T(8,128)}, f32[128,256]{1,0:T(8,128)S(1)}, u32[]{:S(2)}) copy-start(f32[128,256]{1,0:T(8,128)S(1)} %collective-permute-done.8.near0_got) | copy-start | bytes 393220
  85.4 36.8 %collective-permute-start.18 = (f32[3,128,256]{2,1,0:T(8,128)}, f32[3,128,256]{2,1,0:T(8,128)S(1)}, u32[]{:S(2)}, u32[]{:S(2)}) collective-permute-start(f32[3,128,256]{2,1,0:T(8,128)} %get-tuple-element.51), channel_id=1, source_target_pairs={{2,0},{0,2},{7,5},{5,7},{10,8},{8,10},{15,13},{13,15},{18,16},{16,... | collective-permute-start | bytes 1179656 | tf_op jit(solution)/shard_map/ppermute | solution.py:279
  90.4 2.8 %copy-start.15 = (f32[128,256]{1,0:T(8,128)}, f32[128,256]{1,0:T(8,128)S(1)}, u32[]{:S(2)}) copy-start(f32[128,256]{1,0:T(8,128)S(1)} %collective-permute-done.9.near1_got) | copy-start | bytes 393220
  90.5 31.8 %collective-permute-start.19 = (f32[3,128,256]{2,1,0:T(8,128)}, f32[3,128,256]{2,1,0:T(8,128)S(1)}, u32[]{:S(2)}, u32[]{:S(2)}) collective-permute-start(f32[3,128,256]{2,1,0:T(8,128)} %get-tuple-element.51), channel_id=1, source_target_pairs={{3,0},{1,2},{6,5},{4,7},{11,8},{9,10},{14,13},{12,15},{19,16},{17,... | collective-permute-start | bytes 1179656 | tf_op jit(solution)/shard_map/ppermute | solution.py:279
  91.8 21.2 %copy-start.3 = (f32[12,128,128]{2,1,0:T(8,128)}, f32[12,128,128]{2,1,0:T(8,128)S(1)}, u32[]{:S(2)}) copy-start(f32[12,128,128]{2,1,0:T(8,128)S(1)} %collective-permute-done.10.refs_1_) | copy-start | bytes 2359300
  91.8 22.1 %collective-permute-start.17 = (f32[3,128,256]{2,1,0:T(8,128)}, f32[3,128,256]{2,1,0:T(8,128)S(1)}, u32[]{:S(2)}, u32[]{:S(2)}) collective-permute-start(f32[3,128,256]{2,1,0:T(8,128)} %get-tuple-element.50.refs_4_), channel_id=1, source_target_pairs={{1,0},{3,2},{4,5},{6,7},{9,8},{11,10},{12,13},{14,15},{17,16},{19,... | collective-permute-start | bytes 1179656 | tf_op jit(solution)/shard_map/ppermute | solution.py:279
  113.9 8.3 %copy-start.10 = (f32[3,128,256]{2,1,0:T(8,128)}, f32[3,128,256]{2,1,0:T(8,128)S(1)}, u32[]{:S(2)}) copy-start(f32[3,128,256]{2,1,0:T(8,128)S(1)} %collective-permute-done.17.refs_5_) | copy-start | bytes 1179652
  122.2 0.7 copy-start.8
  122.9 0.7 copy-start.9
  131.4 11.3 %collective-permute-start.20 = (f32[6,64,256]{2,1,0:T(8,128)}, f32[6,64,256]{2,1,0:T(8,128)S(1)}, u32[]{:S(2)}, u32[]{:S(2)}) collective-permute-start(f32[6,64,256]{2,1,0:T(8,128)} %get-tuple-element.53), channel_id=1, source_target_pairs={{0,1},{2,3},{5,4},{7,6},{8,9},{10,11},{13,12},{15,14},{16,17},{18,... | collective-permute-start | bytes 1179656 | tf_op jit(solution)/shard_map/ppermute | solution.py:282
  137.2 19.2 %collective-permute-start.21 = (f32[6,64,256]{2,1,0:T(8,128)}, f32[6,64,256]{2,1,0:T(8,128)S(1)}, u32[]{:S(2)}, u32[]{:S(2)}) collective-permute-start(f32[6,64,256]{2,1,0:T(8,128)} %get-tuple-element.54), channel_id=1, source_target_pairs={{0,2},{2,0},{5,7},{7,5},{8,10},{10,8},{13,15},{15,13},{16,18},{18,... | collective-permute-start | bytes 1179656 | tf_op jit(solution)/shard_map/ppermute | solution.py:282
  140.3 16.1 %collective-permute-start.22 = (f32[6,64,256]{2,1,0:T(8,128)}, f32[6,64,256]{2,1,0:T(8,128)S(1)}, u32[]{:S(2)}, u32[]{:S(2)}) collective-permute-start(f32[6,64,256]{2,1,0:T(8,128)} %get-tuple-element.55), channel_id=1, source_target_pairs={{0,3},{2,1},{5,6},{7,4},{8,11},{10,9},{13,14},{15,12},{16,19},{18,... | collective-permute-start | bytes 1179656 | tf_op jit(solution)/shard_map/ppermute | solution.py:282
  142.7 13.6 %copy-start.11 = (f32[6,64,256]{2,1,0:T(8,128)}, f32[6,64,256]{2,1,0:T(8,128)S(1)}, u32[]{:S(2)}) copy-start(f32[6,64,256]{2,1,0:T(8,128)S(1)} %collective-permute-done.20.refs_1_) | copy-start | bytes 1179652
  156.4 0.8 copy-start.12
  156.4 0.9 copy-start.13

commit v3 on v2

--- a/solution.py
+++ b/solution.py
@@ -110,10 +110,9 @@
     bases = [wide(own, 4, 4), wide(near, 4, 4), wide(far2, 2, 4), wide(far3, 2, 4)]
     u = jnp.concatenate(bases, axis=0)
     ut = u.T
-    ut_near, ut_far = ut[:, : 2 * edge], ut[:, 2 * edge :]
-    yt_near = dot(ut_near, corner) + dot(ut_far, side)
-    yt_far = dot(ut_near, side, 1, 1) + dot(ut_far, far)
-    dense = dot(jnp.concatenate([yt_near, yt_far], axis=1), u)
+    left = jnp.concatenate([corner, side], axis=0)
+    right = jnp.concatenate([side.T, far], axis=0)
+    dense = dot3(dot3(ut, jnp.concatenate([left, right], axis=1)), u)
     solved, schur = eliminate(dense, redundant)
     schur_ref[...] = schur
     wt = ut[redundant:] - dot(solved.T, ut[:redundant])
@@ -239,7 +238,7 @@
     top = jnp.concatenate([diag_first, near_first], axis=1)
     low = jnp.concatenate([near_second, diag_second], axis=1)
     merged = jnp.concatenate([top, low], axis=0)
-    dense = dot(dot(vt_ref[...], merged), v_ref[...])
+    dense = dot3(dot3(vt_ref[...], merged), v_ref[...])
     flipped_ref[...] = eliminate(dense, size)[1].T
 
 

time: 162 us -> 160 us (0.988)
  Pallas kernels: 64 us -> 60.6 us
  waiting for transfers between devices: 39.4 us -> 41.1 us
    pallas_call x9, Pallas kernels: 64 us -> 60.6 us  [call(): pl.pallas_call(kernel, out_shape=shapes, in_specs=specs, out_specs=[vmem]...]
    ppermute x12, waiting for transfers between devices: 24.6 us -> 26.3 us  [to_owner(): lax.ppermute(x, both, [(r * n_col + (z ^ j), r * n_col + z) for r, z in o...]
  transfers between devices with their start and end apart: 23 -> 23, of which waited for: 6 -> 6; matrix products, arithmetic and copies ran while one was open for 1% -> 1% of each run, Pallas kernels for 32% -> 31%
where the time goes in v3:
time: 160 us; the launch traced here: 158 us
  Pallas kernels  60.6 us (38%)
  starting transfers between devices  51.1 us (32%)
  waiting for transfers between devices  41.1 us (26%)
  local copies, waits for them, and re-layouts  3.41 us (2%)
    pallas_call x9, Pallas kernels, call(): pl.pallas_call(kernel, out_shape=shapes, in_specs=specs, out_specs=[vmem]...  60.6 us
    ppermute x12, starting transfers between devices, to_owner(): lax.ppermute(x, both, [(r * n_col + (z ^ j), r * n_col + z) for r, z in o...  30.4 us
    ppermute x12, waiting for transfers between devices, to_owner(): lax.ppermute(x, both, [(r * n_col + (z ^ j), r * n_col + z) for r, z in o...  26.3 us
    ppermute x3, waiting for transfers between devices, from_owner(): lax.ppermute(x, both, [(r * n_col + z, r * n_col + (z ^ j)) for r, z in o...  14.8 us
    ppermute x3, starting transfers between devices, from_owner(): lax.ppermute(x, both, [(r * n_col + z, r * n_col + (z ^ j)) for r, z in o...  10.1 us
    ppermute x4, starting transfers between devices, from_sibling(): lax.ppermute(x, both, [((r ^ 1) * n_col + (z ^ 1), r * n_col + z) for r,...  5.91 us
    ppermute x4, starting transfers between devices, across(): return lax.ppermute(x, 'row', [(r, r ^ bit) for r in range(n_row)])  4.7 us
    unnamed x33, local copies, waits for them, and re-layouts  3.39 us
  transfers between devices with their start and end apart: 23, of which 6 were waited for; matrix products, arithmetic and copies ran while one was open for 1% of the time, Pallas kernels for 31%

profile of v3, /device:TPU:0, one launch (start us, length us, event | category | flops | bytes accessed | tf_op | source)
XLA Modules:
  0.0 157.9 jit_solution(8563172947160494563)
XLA Ops:
  0.6 0.6 pad_add_fusion.place
  1.3 2.3 %shard_map.85 = (f32[8,128,128]{2,1,0:T(8,128)}, f32[6,128,128]{2,1,0:T(8,128)}, f32[2,128,256]{2,1,0:T(8,128)}) custom-call(s32[2]{0:T(128)} %pad_add_fusion.place, f32[2,512,128]{2,1,0:T(8,128)} %diag.1, f32[2,128,512]{2,1,0:T(8,128)} %bases.1), custom_call_target="tpu_custom_call" | custom-call | flops 2000000000 | bytes 2000000 | tf_op jit(solution)/shard_map/pallas_call | solution.py:250
  3.6 3.0 %collective-permute-start.13 = (f32[2,128,256]{2,1,0:T(8,128)}, f32[2,128,256]{2,1,0:T(8,128)S(1)}, u32[]{:S(2)}, u32[]{:S(2)}) collective-permute-start(f32[2,128,256]{2,1,0:T(8,128)} %get-tuple-element.47), channel_id=1, source_target_pairs={{0,8},{4,12},{8,0},{12,4},{16,24},{20,28},{24,16},{28,20},{1,9},{5... | collective-permute-start | bytes 786440 | tf_op jit(solution)/shard_map/ppermute | solution.py:287
  6.5 1.3 collective-permute-start
  7.8 4.5 %collective-permute-start.1 = (f32[6,128,128]{2,1,0:T(8,128)}, f32[6,128,128]{2,1,0:T(8,128)S(1)}, u32[]{:S(2)}, u32[]{:S(2)}) collective-permute-start(f32[6,128,128]{2,1,0:T(8,128)} %get-tuple-element.32), channel_id=1, source_target_pairs={{2,0},{0,2},{7,5},{5,7},{10,8},{8,10},{15,13},{13,15},{18,16},{16,... | collective-permute-start | bytes 1179656 | tf_op jit(solution)/shard_map/ppermute | solution.py:278
  12.3 1.3 collective-permute-start.2
  13.6 1.0 constant_dynamic-update-slice_fusion.1
  14.6 1.6 %collective-permute-start.14 = (f32[4,128,256]{2,1,0:T(8,128)S(1)}, f32[4,128,256]{2,1,0:T(8,128)S(1)}, u32[]{:S(2)}, u32[]{:S(2)}) collective-permute-start(f32[4,128,256]{2,1,0:T(8,128)S(1)} %constant_dynamic-update-slice_fusion.low0), channel_id=1, source_target_pairs={{0,16},{4,20},{8,24},{12,28},{16,0},{20,4},{24,8},{28,12},{1,17},{... | collective-permute-start | bytes 1572872 | tf_op jit(solution)/shard_map/ppermute | solution.py:287
  16.2 3.8 %shard_map.88 = (f32[4,128,128]{2,1,0:T(8,128)}, f32[4,128,128]{2,1,0:T(8,128)}, f32[12,128,128]{2,1,0:T(8,128)}, f32[12,128,128]{2,1,0:T(8,128)}, f32[512,512]{1,0:T(8,128)}) custom-call(s32[2]{0:T(128)} %pad_add_fusion.place, f32[2,16,128,128]{3,2,1,0:T(8,128)} %bitcast.7, f32[512,512]{1,0:T(8,128)} %bitcast.8), custom_call_target="tpu_custom_call" | custom-call | flops 2000000000 | bytes 2000000 | tf_op jit(solution)/shard_map/pallas_call | solution.py:250
  20.1 9.4 %collective-permute-done.1.far2 = f32[6,128,128]{2,1,0:T(8,128)S(1)} collective-permute-done((f32[6,128,128]{2,1,0:T(8,128)}, f32[6,128,128]{2,1,0:T(8,128)S(1)}, u32[]{:S(2)}, u32[]{:S(2)}) %collective-permute-start.1) | collective-permute-done | bytes 393248 | tf_op jit(solution)/shard_map/ppermute | solution.py:278
  29.5 0.0 collective-permute-done.2.far3
  29.5 0.0 collective-permute-done.near
  29.5 1.3 collective-permute-start.4
  30.8 5.0 %collective-permute-start.5 = (f32[4,128,128]{2,1,0:T(8,128)}, f32[4,128,128]{2,1,0:T(8,128)}, u32[]{:S(2)}, u32[]{:S(2)}) collective-permute-start(f32[4,128,128]{2,1,0:T(8,128)} %get-tuple-element.38), channel_id=1, source_target_pairs={{2,0},{0,2},{7,5},{5,7},{10,8},{8,10},{15,13},{13,15},{18,16},{16,... | collective-permute-start | bytes 786440 | tf_op jit(solution)/shard_map/ppermute | solution.py:278
  35.8 0.1 collective-permute-start.15
  35.9 1.3 collective-permute-start.6
  37.2 2.3 %shard_map.87 = f32[4,128,256]{2,1,0:T(8,128)} custom-call(s32[2]{0:T(128)} %pad_add_fusion.place, f32[8,128,128]{2,1,0:T(8,128)} %get-tuple-element.31.own, f32[8,128,128]{2,1,0:T(8,128)} %copy-done.5, f32[6,128,128]{2,1,0:T(8,128)} %copy-done.6, f32[6,128,128]{2,1,0:T(8,128)} %copy-done.7), custom_call_target="tpu_custom_call" | custom-call | flops 2000000000 | bytes 2000000 | tf_op jit(solution)/shard_map/pallas_call | solution.py:250
  39.6 2.0 %collective-permute-start.3 = (f32[4,128,256]{2,1,0:T(8,128)}, f32[4,128,256]{2,1,0:T(8,128)}, u32[]{:S(2)}, u32[]{:S(2)}) collective-permute-start(f32[4,128,256]{2,1,0:T(8,128)} %shard_map.87), channel_id=1, source_target_pairs={{5,0},{7,2},{0,5},{2,7},{13,8},{15,10},{8,13},{10,15},{21,16},{23,... | collective-permute-start | bytes 1572872 | tf_op jit(solution)/shard_map/ppermute | solution.py:284
  41.6 5.9 %collective-permute-done.5.n2 = f32[4,128,128]{2,1,0:T(8,128)} collective-permute-done((f32[4,128,128]{2,1,0:T(8,128)}, f32[4,128,128]{2,1,0:T(8,128)}, u32[]{:S(2)}, u32[]{:S(2)}) %collective-permute-start.5) | collective-permute-done | bytes 262176 | tf_op jit(solution)/shard_map/ppermute | solution.py:278
  47.5 1.3 collective-permute-start.10
  48.8 0.0 collective-permute-done.14.low1
  48.8 0.1 collective-permute-start.16
  48.9 18.1 %shard_map.86 = (f32[4,256,128]{2,1,0:T(8,128)}, f32[256,256]{1,0:T(8,128)}) custom-call(s32[2]{0:T(128)} %pad_add_fusion.place, f32[8,128,128]{2,1,0:T(8,128)} %get-tuple-element.31.own, f32[8,128,128]{2,1,0:T(8,128)} %copy-done.5, f32[6,128,128]{2,1,0:T(8,128)} %copy-done.6, f32[6,128,128]{2,1,0:T(8,128)} %copy-done.7), custom_call_target="tpu_custom_call" | custom-call | flops 22000001024 | bytes 22000000 | tf_op jit(solution)/shard_map/pallas_call | solution.py:250
  67.0 1.3 collective-permute-start.7
  68.4 5.4 %collective-permute-start.11 = (f32[12,128,128]{2,1,0:T(8,128)S(1)}, f32[12,128,128]{2,1,0:T(8,128)}, u32[]{:S(2)}, u32[]{:S(2)}) collective-permute-start(f32[12,128,128]{2,1,0:T(8,128)S(1)} %copy-done.2), channel_id=1, source_target_pairs={{2,0},{0,2},{7,5},{5,7},{10,8},{8,10},{15,13},{13,15},{18,16},{16,... | collective-permute-start | bytes 2359304 | tf_op jit(solution)/shard_map/ppermute | solution.py:278
  73.8 3.5 %shard_map.89 = (f32[128,256]{1,0:T(8,128)}, f32[128,256]{1,0:T(8,128)}, f32[256,256]{1,0:T(8,128)}) custom-call(s32[2]{0:T(128)} %pad_add_fusion.place, s32[2]{0:T(128)} %count.3, f32[4,256,128]{2,1,0:T(8,128)} %get-tuple-element.33.w_ref, f32[4,128,256]{2,1,0:T(8,128)} %collective-permute-done.3.bases, f32[4,128,128]{2,1,0:T(8,128)} %get-tuple-element.37.n0, ...), custom_call_target="tpu_custom_call" | custom-call | flops 4000000000 | bytes 4000000 | tf_op jit(solution)/shard_map/pallas_call | solution.py:250
  77.3 1.3 collective-permute-start.8
  78.6 1.3 collective-permute-start.9
  79.9 2.5 %shard_map.91 = (f32[3,128,256]{2,1,0:T(8,128)}, f32[3,128,256]{2,1,0:T(8,128)}) custom-call(s32[2]{0:T(128)} %pad_add_fusion.place, s32[2,4]{1,0:T(2,128)} %ids.1, f32[4,128,256]{2,1,0:T(8,128)} %copy-done, f32[4,128,256]{2,1,0:T(8,128)} %copy-done.4, f32[4,128,256]{2,1,0:T(8,128)} %collective-permute-done.15.high0, ...), custom_call_target="tpu_custom_call" | custom-call | flops 2000000000 | bytes 2000000 | tf_op jit(solution)/shard_map/pallas_call | solution.py:250
  82.4 1.3 collective-permute-start.12
  83.7 0.0 collective-permute-done.8.near0_got
  83.8 5.0 %collective-permute-start.18 = (f32[3,128,256]{2,1,0:T(8,128)}, f32[3,128,256]{2,1,0:T(8,128)S(1)}, u32[]{:S(2)}, u32[]{:S(2)}) collective-permute-start(f32[3,128,256]{2,1,0:T(8,128)} %get-tuple-element.51), channel_id=1, source_target_pairs={{2,0},{0,2},{7,5},{5,7},{10,8},{8,10},{15,13},{13,15},{18,16},{16,... | collective-permute-start | bytes 1179656 | tf_op jit(solution)/shard_map/ppermute | solution.py:278
  88.8 1.3 collective-permute-start.19
  90.1 1.5 collective-permute-start.17
  91.6 18.0 %shard_map.90.parent = f32[256,256]{1,0:T(8,128)} custom-call(s32[2]{0:T(128)} %pad_add_fusion.place, f32[256,256]{1,0:T(8,128)} %get-tuple-element.34.diag.schur, f32[128,256]{1,0:T(8,128)} %get-tuple-element.40.near0, f32[128,256]{1,0:T(8,128)} %get-tuple-element.41.near1, f32[256,256]{1,0:T(8,128)} %collective-permute-done.7.diag_got, ...), custom_call_target="tpu_custom_call" | custom-call | flops 22000001024 | bytes 22000000 | tf_op jit(solution)/shard_map/pallas_call | solution.py:250
  109.6 2.6 %collective-permute-done.11.refs_2_ = f32[12,128,128]{2,1,0:T(8,128)} collective-permute-done((f32[12,128,128]{2,1,0:T(8,128)S(1)}, f32[12,128,128]{2,1,0:T(8,128)}, u32[]{:S(2)}, u32[]{:S(2)}) %collective-permute-start.11) | collective-permute-done | bytes 786464 | tf_op jit(solution)/shard_map/ppermute | solution.py:278
  112.2 8.3 %collective-permute-done.18.refs_6_ = f32[3,128,256]{2,1,0:T(8,128)S(1)} collective-permute-done((f32[3,128,256]{2,1,0:T(8,128)}, f32[3,128,256]{2,1,0:T(8,128)S(1)}, u32[]{:S(2)}, u32[]{:S(2)}) %collective-permute-start.18) | collective-permute-done | bytes 393248 | tf_op jit(solution)/shard_map/ppermute | solution.py:278
  120.5 0.7 copy-done.8
  121.3 0.7 copy-done.9
  122.0 7.7 %shard_map.92 = (f32[6,64,256]{2,1,0:T(8,128)}, f32[6,64,256]{2,1,0:T(8,128)}, f32[6,64,256]{2,1,0:T(8,128)}, f32[6,64,256]{2,1,0:T(8,128)}) custom-call(s32[2]{0:T(128)} %pad_add_fusion.place, s32[2]{0:T(128)} %count.3, f32[4,256,128]{2,1,0:T(8,128)} %get-tuple-element.33.w_ref, f32[256,256]{1,0:T(8,128)} %get-tuple-element.34.diag.schur, ...), custom_call_target="tpu_custom_call" | custom-call | flops 7000000000 | bytes 7000000 | tf_op jit(solution)/shard_map/pallas_call | solution.py:250
  129.8 5.7 %collective-permute-start.20 = (f32[6,64,256]{2,1,0:T(8,128)}, f32[6,64,256]{2,1,0:T(8,128)S(1)}, u32[]{:S(2)}, u32[]{:S(2)}) collective-permute-start(f32[6,64,256]{2,1,0:T(8,128)} %get-tuple-element.53), channel_id=1, source_target_pairs={{0,1},{2,3},{5,4},{7,6},{8,9},{10,11},{13,12},{15,14},{16,17},{18,... | collective-permute-start | bytes 1179656 | tf_op jit(solution)/shard_map/ppermute | solution.py:281
  135.5 3.1 %collective-permute-start.21 = (f32[6,64,256]{2,1,0:T(8,128)}, f32[6,64,256]{2,1,0:T(8,128)S(1)}, u32[]{:S(2)}, u32[]{:S(2)}) collective-permute-start(f32[6,64,256]{2,1,0:T(8,128)} %get-tuple-element.54), channel_id=1, source_target_pairs={{0,2},{2,0},{5,7},{7,5},{8,10},{10,8},{13,15},{15,13},{16,18},{18,... | collective-permute-start | bytes 1179656 | tf_op jit(solution)/shard_map/ppermute | solution.py:281
  138.6 1.3 collective-permute-start.22
  139.9 1.1 collective-permute-done.20.refs_1_
  141.1 13.6 %collective-permute-done.21.refs_2_ = f32[6,64,256]{2,1,0:T(8,128)S(1)} collective-permute-done((f32[6,64,256]{2,1,0:T(8,128)}, f32[6,64,256]{2,1,0:T(8,128)S(1)}, u32[]{:S(2)}, u32[]{:S(2)}) %collective-permute-start.21) | collective-permute-done | bytes 393248 | tf_op jit(solution)/shard_map/ppermute | solution.py:281
  154.7 0.8 copy-done.12
  155.5 0.1 copy-done.13
  155.6 2.3 %shard_map.93 = (f32[2,64,256]{2,1,0:T(8,128)}, f32[2,4,64,256]{3,2,1,0:T(8,128)}, f32[1,64,256]{2,1,0:T(8,128)}) custom-call(s32[2]{0:T(128)} %pad_add_fusion.place, f32[6,64,256]{2,1,0:T(8,128)} %get-tuple-element.52.refs_0_, f32[6,64,256]{2,1,0:T(8,128)} %copy-done.11, f32[6,64,256]{2,1,0:T(8,128)} %copy-done.12, f32[6,64,256]{2,1,0:T(8,128)} %copy-done.13), custom_call_target="tpu_custom_call" | custom-call | flops 2000000000 | bytes 2000000 | tf_op jit(solution)/shard_map/pallas_call | solution.py:250
  (42 shorter events, 0.1 us)
Async XLA Ops:
  3.6 11.0 %collective-permute-start.13 = (f32[2,128,256]{2,1,0:T(8,128)}, f32[2,128,256]{2,1,0:T(8,128)S(1)}, u32[]{:S(2)}, u32[]{:S(2)}) collective-permute-start(f32[2,128,256]{2,1,0:T(8,128)} %get-tuple-element.47), channel_id=1, source_target_pairs={{0,8},{4,12},{8,0},{12,4},{16,24},{20,28},{24,16},{28,20},{1,9},{5... | collective-permute-start | bytes 786440 | tf_op jit(solution)/shard_map/ppermute | solution.py:287
  6.5 22.9 %collective-permute-start = (f32[8,128,128]{2,1,0:T(8,128)}, f32[8,128,128]{2,1,0:T(8,128)S(1)}, u32[]{:S(2)}, u32[]{:S(2)}) collective-permute-start(f32[8,128,128]{2,1,0:T(8,128)} %get-tuple-element.31.own), channel_id=1, source_target_pairs={{1,0},{3,2},{4,5},{6,7},{9,8},{11,10},{12,13},{14,15},{17,16},{19,... | collective-permute-start | bytes 1572872 | tf_op jit(solution)/shard_map/ppermute | solution.py:278
  7.8 21.6 %collective-permute-start.1 = (f32[6,128,128]{2,1,0:T(8,128)}, f32[6,128,128]{2,1,0:T(8,128)S(1)}, u32[]{:S(2)}, u32[]{:S(2)}) collective-permute-start(f32[6,128,128]{2,1,0:T(8,128)} %get-tuple-element.32), channel_id=1, source_target_pairs={{2,0},{0,2},{7,5},{5,7},{10,8},{8,10},{15,13},{13,15},{18,16},{16,... | collective-permute-start | bytes 1179656 | tf_op jit(solution)/shard_map/ppermute | solution.py:278
  12.3 17.1 %collective-permute-start.2 = (f32[6,128,128]{2,1,0:T(8,128)}, f32[6,128,128]{2,1,0:T(8,128)S(1)}, u32[]{:S(2)}, u32[]{:S(2)}) collective-permute-start(f32[6,128,128]{2,1,0:T(8,128)} %get-tuple-element.32), channel_id=1, source_target_pairs={{3,0},{1,2},{6,5},{4,7},{11,8},{9,10},{14,13},{12,15},{19,16},{17,... | collective-permute-start | bytes 1179656 | tf_op jit(solution)/shard_map/ppermute | solution.py:278
  14.6 21.2 %copy-start = (f32[4,128,256]{2,1,0:T(8,128)}, f32[4,128,256]{2,1,0:T(8,128)S(1)}, u32[]{:S(2)}) copy-start(f32[4,128,256]{2,1,0:T(8,128)S(1)} %constant_dynamic-update-slice_fusion.low0) | copy-start | bytes 1572868
  14.6 34.2 %collective-permute-start.14 = (f32[4,128,256]{2,1,0:T(8,128)S(1)}, f32[4,128,256]{2,1,0:T(8,128)S(1)}, u32[]{:S(2)}, u32[]{:S(2)}) collective-permute-start(f32[4,128,256]{2,1,0:T(8,128)S(1)} %constant_dynamic-update-slice_fusion.low0), channel_id=1, source_target_pairs={{0,16},{4,20},{8,24},{12,28},{16,0},{20,4},{24,8},{28,12},{1,17},{... | collective-permute-start | bytes 1572872 | tf_op jit(solution)/shard_map/ppermute | solution.py:287
  29.5 7.7 %copy-start.6 = (f32[6,128,128]{2,1,0:T(8,128)}, f32[6,128,128]{2,1,0:T(8,128)S(1)}, u32[]{:S(2)}) copy-start(f32[6,128,128]{2,1,0:T(8,128)S(1)} %collective-permute-done.1.far2) | copy-start | bytes 1179652
  29.5 7.7 %copy-start.7 = (f32[6,128,128]{2,1,0:T(8,128)}, f32[6,128,128]{2,1,0:T(8,128)S(1)}, u32[]{:S(2)}) copy-start(f32[6,128,128]{2,1,0:T(8,128)S(1)} %collective-permute-done.2.far3) | copy-start | bytes 1179652
  29.5 7.7 %copy-start.5 = (f32[8,128,128]{2,1,0:T(8,128)}, f32[8,128,128]{2,1,0:T(8,128)S(1)}, u32[]{:S(2)}) copy-start(f32[8,128,128]{2,1,0:T(8,128)S(1)} %collective-permute-done.near) | copy-start | bytes 1572868
  29.5 10.1 %collective-permute-start.4 = (f32[4,128,128]{2,1,0:T(8,128)}, f32[4,128,128]{2,1,0:T(8,128)}, u32[]{:S(2)}, u32[]{:S(2)}) collective-permute-start(f32[4,128,128]{2,1,0:T(8,128)} %get-tuple-element.37.n0), channel_id=1, source_target_pairs={{1,0},{3,2},{4,5},{6,7},{9,8},{11,10},{12,13},{14,15},{17,16},{19,... | collective-permute-start | bytes 786440 | tf_op jit(solution)/shard_map/ppermute | solution.py:278
  30.8 16.7 %collective-permute-start.5 = (f32[4,128,128]{2,1,0:T(8,128)}, f32[4,128,128]{2,1,0:T(8,128)}, u32[]{:S(2)}, u32[]{:S(2)}) collective-permute-start(f32[4,128,128]{2,1,0:T(8,128)} %get-tuple-element.38), channel_id=1, source_target_pairs={{2,0},{0,2},{7,5},{5,7},{10,8},{8,10},{15,13},{13,15},{18,16},{16,... | collective-permute-start | bytes 786440 | tf_op jit(solution)/shard_map/ppermute | solution.py:278
  35.8 41.5 %collective-permute-start.15 = (f32[4,128,256]{2,1,0:T(8,128)S(1)}, f32[4,128,256]{2,1,0:T(8,128)}, u32[]{:S(2)}, u32[]{:S(2)}) collective-permute-start(f32[4,128,256]{2,1,0:T(8,128)S(1)} %constant_dynamic-update-slice_fusion.low0), channel_id=1, source_target_pairs={{0,4},{4,0},{8,12},{12,8},{16,20},{20,16},{24,28},{28,24},{1,5},{5... | collective-permute-start | bytes 1572872 | tf_op jit(solution)/shard_map/ppermute | solution.py:287
  35.9 31.1 %collective-permute-start.6 = (f32[4,128,128]{2,1,0:T(8,128)}, f32[4,128,128]{2,1,0:T(8,128)}, u32[]{:S(2)}, u32[]{:S(2)}) collective-permute-start(f32[4,128,128]{2,1,0:T(8,128)} %get-tuple-element.38), channel_id=1, source_target_pairs={{3,0},{1,2},{6,5},{4,7},{11,8},{9,10},{14,13},{12,15},{19,16},{17,... | collective-permute-start | bytes 786440 | tf_op jit(solution)/shard_map/ppermute | solution.py:278
  37.2 10.3 %copy-start.1 = (f32[12,128,128]{2,1,0:T(8,128)S(1)}, f32[12,128,128]{2,1,0:T(8,128)}, u32[]{:S(2)}) copy-start(f32[12,128,128]{2,1,0:T(8,128)} %get-tuple-element.45.refs_0_) | copy-start | bytes 2359300
  39.6 28.8 %copy-start.2 = (f32[12,128,128]{2,1,0:T(8,128)S(1)}, f32[12,128,128]{2,1,0:T(8,128)}, u32[]{:S(2)}) copy-start(f32[12,128,128]{2,1,0:T(8,128)} %get-tuple-element.46) | copy-start | bytes 2359300
  39.6 28.8 %collective-permute-start.3 = (f32[4,128,256]{2,1,0:T(8,128)}, f32[4,128,256]{2,1,0:T(8,128)}, u32[]{:S(2)}, u32[]{:S(2)}) collective-permute-start(f32[4,128,256]{2,1,0:T(8,128)} %shard_map.87), channel_id=1, source_target_pairs={{5,0},{7,2},{0,5},{2,7},{13,8},{15,10},{8,13},{10,15},{21,16},{23,... | collective-permute-start | bytes 1572872 | tf_op jit(solution)/shard_map/ppermute | solution.py:284
  47.5 42.6 %collective-permute-start.10 = (f32[12,128,128]{2,1,0:T(8,128)S(1)}, f32[12,128,128]{2,1,0:T(8,128)S(1)}, u32[]{:S(2)}, u32[]{:S(2)}) collective-permute-start(f32[12,128,128]{2,1,0:T(8,128)S(1)} %copy-done.1), channel_id=1, source_target_pairs={{1,0},{3,2},{4,5},{6,7},{9,8},{11,10},{12,13},{14,15},{17,16},{19,... | collective-permute-start | bytes 2359304 | tf_op jit(solution)/shard_map/ppermute | solution.py:278
  48.8 18.2 %copy-start.4 = (f32[4,128,256]{2,1,0:T(8,128)}, f32[4,128,256]{2,1,0:T(8,128)S(1)}, u32[]{:S(2)}) copy-start(f32[4,128,256]{2,1,0:T(8,128)S(1)} %collective-permute-done.14.low1) | copy-start | bytes 1572868
  48.8 29.7 %collective-permute-start.16 = (f32[4,128,256]{2,1,0:T(8,128)S(1)}, f32[4,128,256]{2,1,0:T(8,128)}, u32[]{:S(2)}, u32[]{:S(2)}) collective-permute-start(f32[4,128,256]{2,1,0:T(8,128)S(1)} %collective-permute-done.14.low1), channel_id=1, source_target_pairs={{0,4},{4,0},{8,12},{12,8},{16,20},{20,16},{24,28},{28,24},{1,5},{5... | collective-permute-start | bytes 1572872 | tf_op jit(solution)/shard_map/ppermute | solution.py:287
  67.0 15.4 %collective-permute-start.7 = (f32[256,256]{1,0:T(8,128)}, f32[256,256]{1,0:T(8,128)}, u32[]{:S(2)}, u32[]{:S(2)}) collective-permute-start(f32[256,256]{1,0:T(8,128)} %get-tuple-element.34.diag.schur), channel_id=1, source_target_pairs={{5,0},{2,7},{13,8},{10,15},{21,16},{18,23},{29,24},{26,31}} | collective-permute-start | bytes 786440 | tf_op jit(solution)/shard_map/ppermute | solution.py:284
  68.4 43.9 %collective-permute-start.11 = (f32[12,128,128]{2,1,0:T(8,128)S(1)}, f32[12,128,128]{2,1,0:T(8,128)}, u32[]{:S(2)}, u32[]{:S(2)}) collective-permute-start(f32[12,128,128]{2,1,0:T(8,128)S(1)} %copy-done.2), channel_id=1, source_target_pairs={{2,0},{0,2},{7,5},{5,7},{10,8},{8,10},{15,13},{13,15},{18,16},{16,... | collective-permute-start | bytes 2359304 | tf_op jit(solution)/shard_map/ppermute | solution.py:278
  77.3 6.5 %collective-permute-start.8 = (f32[128,256]{1,0:T(8,128)}, f32[128,256]{1,0:T(8,128)S(1)}, u32[]{:S(2)}, u32[]{:S(2)}) collective-permute-start(f32[128,256]{1,0:T(8,128)} %get-tuple-element.40.near0), channel_id=1, source_target_pairs={{5,0},{2,7},{13,8},{10,15},{21,16},{18,23},{29,24},{26,31}} | collective-permute-start | bytes 393224 | tf_op jit(solution)/shard_map/ppermute | solution.py:284
  78.6 10.2 %collective-permute-start.9 = (f32[128,256]{1,0:T(8,128)}, f32[128,256]{1,0:T(8,128)S(1)}, u32[]{:S(2)}, u32[]{:S(2)}) collective-permute-start(f32[128,256]{1,0:T(8,128)} %get-tuple-element.41.near1), channel_id=1, source_target_pairs={{5,0},{2,7},{13,8},{10,15},{21,16},{18,23},{29,24},{26,31}} | collective-permute-start | bytes 393224 | tf_op jit(solution)/shard_map/ppermute | solution.py:284
  82.4 29.8 %collective-permute-start.12 = (f32[12,128,128]{2,1,0:T(8,128)S(1)}, f32[12,128,128]{2,1,0:T(8,128)}, u32[]{:S(2)}, u32[]{:S(2)}) collective-permute-start(f32[12,128,128]{2,1,0:T(8,128)S(1)} %copy-done.2), channel_id=1, source_target_pairs={{3,0},{1,2},{6,5},{4,7},{11,8},{9,10},{14,13},{12,15},{19,16},{17,... | collective-permute-start | bytes 2359304 | tf_op jit(solution)/shard_map/ppermute | solution.py:278
  83.8 7.8 %copy-start.14 = (f32[128,256]{1,0:T(8,128)}, f32[128,256]{1,0:T(8,128)S(1)}, u32[]{:S(2)}) copy-start(f32[128,256]{1,0:T(8,128)S(1)} %collective-permute-done.8.near0_got) | copy-start | bytes 393220
  83.8 36.8 %collective-permute-start.18 = (f32[3,128,256]{2,1,0:T(8,128)}, f32[3,128,256]{2,1,0:T(8,128)S(1)}, u32[]{:S(2)}, u32[]{:S(2)}) collective-permute-start(f32[3,128,256]{2,1,0:T(8,128)} %get-tuple-element.51), channel_id=1, source_target_pairs={{2,0},{0,2},{7,5},{5,7},{10,8},{8,10},{15,13},{13,15},{18,16},{16,... | collective-permute-start | bytes 1179656 | tf_op jit(solution)/shard_map/ppermute | solution.py:278
  88.8 2.8 %copy-start.15 = (f32[128,256]{1,0:T(8,128)}, f32[128,256]{1,0:T(8,128)S(1)}, u32[]{:S(2)}) copy-start(f32[128,256]{1,0:T(8,128)S(1)} %collective-permute-done.9.near1_got) | copy-start | bytes 393220
  88.8 31.8 %collective-permute-start.19 = (f32[3,128,256]{2,1,0:T(8,128)}, f32[3,128,256]{2,1,0:T(8,128)S(1)}, u32[]{:S(2)}, u32[]{:S(2)}) collective-permute-start(f32[3,128,256]{2,1,0:T(8,128)} %get-tuple-element.51), channel_id=1, source_target_pairs={{3,0},{1,2},{6,5},{4,7},{11,8},{9,10},{14,13},{12,15},{19,16},{17,... | collective-permute-start | bytes 1179656 | tf_op jit(solution)/shard_map/ppermute | solution.py:278
  90.1 19.5 %copy-start.3 = (f32[12,128,128]{2,1,0:T(8,128)}, f32[12,128,128]{2,1,0:T(8,128)S(1)}, u32[]{:S(2)}) copy-start(f32[12,128,128]{2,1,0:T(8,128)S(1)} %collective-permute-done.10.refs_1_) | copy-start | bytes 2359300
  90.1 22.1 %collective-permute-start.17 = (f32[3,128,256]{2,1,0:T(8,128)}, f32[3,128,256]{2,1,0:T(8,128)S(1)}, u32[]{:S(2)}, u32[]{:S(2)}) collective-permute-start(f32[3,128,256]{2,1,0:T(8,128)} %get-tuple-element.50.refs_4_), channel_id=1, source_target_pairs={{1,0},{3,2},{4,5},{6,7},{9,8},{11,10},{12,13},{14,15},{17,16},{19,... | collective-permute-start | bytes 1179656 | tf_op jit(solution)/shard_map/ppermute | solution.py:278
  112.2 8.3 %copy-start.10 = (f32[3,128,256]{2,1,0:T(8,128)}, f32[3,128,256]{2,1,0:T(8,128)S(1)}, u32[]{:S(2)}) copy-start(f32[3,128,256]{2,1,0:T(8,128)S(1)} %collective-permute-done.17.refs_5_) | copy-start | bytes 1179652
  120.5 0.7 copy-start.8
  121.3 0.7 copy-start.9
  129.8 11.3 %collective-permute-start.20 = (f32[6,64,256]{2,1,0:T(8,128)}, f32[6,64,256]{2,1,0:T(8,128)S(1)}, u32[]{:S(2)}, u32[]{:S(2)}) collective-permute-start(f32[6,64,256]{2,1,0:T(8,128)} %get-tuple-element.53), channel_id=1, source_target_pairs={{0,1},{2,3},{5,4},{7,6},{8,9},{10,11},{13,12},{15,14},{16,17},{18,... | collective-permute-start | bytes 1179656 | tf_op jit(solution)/shard_map/ppermute | solution.py:281
  135.5 19.2 %collective-permute-start.21 = (f32[6,64,256]{2,1,0:T(8,128)}, f32[6,64,256]{2,1,0:T(8,128)S(1)}, u32[]{:S(2)}, u32[]{:S(2)}) collective-permute-start(f32[6,64,256]{2,1,0:T(8,128)} %get-tuple-element.54), channel_id=1, source_target_pairs={{0,2},{2,0},{5,7},{7,5},{8,10},{10,8},{13,15},{15,13},{16,18},{18,... | collective-permute-start | bytes 1179656 | tf_op jit(solution)/shard_map/ppermute | solution.py:281
  138.6 16.1 %collective-permute-start.22 = (f32[6,64,256]{2,1,0:T(8,128)}, f32[6,64,256]{2,1,0:T(8,128)S(1)}, u32[]{:S(2)}, u32[]{:S(2)}) collective-permute-start(f32[6,64,256]{2,1,0:T(8,128)} %get-tuple-element.55), channel_id=1, source_target_pairs={{0,3},{2,1},{5,6},{7,4},{8,11},{10,9},{13,14},{15,12},{16,19},{18,... | collective-permute-start | bytes 1179656 | tf_op jit(solution)/shard_map/ppermute | solution.py:281
  141.1 13.6 %copy-start.11 = (f32[6,64,256]{2,1,0:T(8,128)}, f32[6,64,256]{2,1,0:T(8,128)S(1)}, u32[]{:S(2)}) copy-start(f32[6,64,256]{2,1,0:T(8,128)S(1)} %collective-permute-done.20.refs_1_) | copy-start | bytes 1179652
  154.7 0.8 copy-start.12
  154.7 0.9 copy-start.13

commit v4 on v3

--- a/solution.py
+++ b/solution.py
@@ -182,64 +182,68 @@
         part[index] = flipped[index, pl.ds(pl.multiple_of((z ^ j) * quarter, quarter), quarter), :]
 
 
-def near_first_kernel(place, count, w_ref, bases, n0, n1, n2, n3, top, low, flipped):
+def near_first_kernel(place, count, w_ref, bases, n0, n1, n2, n3, schur, top, low, flipped, pair):
     result = coupling(w_ref, [tall(n, 0) for n in (n0, n1, n2, n3)], [bases[j ^ 1] for j in range(4)])
     result = jnp.where(count[place[1] >> 1] > 0, result, 0.0)
     half = top.shape[0]
     top[...], low[...] = result[:half], result[half:]
+    pair[0], pair[1] = schur[...], result
     flipped[...] = result.T
 
 
-def near_rest_kernel(place, count, w_ref, schur, first, parent, *refs):
-    z = place[1]
+def near_rest_kernel(place, count, w_ref, schur, first, *refs):
+    row, z = place[0], place[1]
     blocks, named, parts, flipped = refs[:4], refs[4:8], refs[8:12], refs[12]
     total = named[0].shape[0]
-    flipped[0] = schur[...]
-    flipped[1] = first[...]
-    for k in range(total):
-        result = coupling(w_ref, [tall(n, 4 * k) for n in blocks], [s[k] for s in named])
-        flipped[k + 2] = jnp.where(count[z >> 1] > k + 1, result, 0.0).T
-    flipped[total + 2] = parent[...]
-    for i in range(total + 3):
-        deal(z, flipped, i, parts)
+
+    @pl.when((z & 1) == (row & 1))
+    def _():
+        flipped[0] = schur[...]
+        flipped[1] = first[...]
+        for k in range(total):
+            result = coupling(w_ref, [tall(n, 4 * k) for n in blocks], [s[k] for s in named])
+            flipped[k + 2] = jnp.where(count[z >> 1] > k + 1, result, 0.0).T
+        for i in range(total + 2):
+            deal(z, flipped, i, parts)
 
 
 def finish_kernel(place, *refs):
     row, z = place[0], place[1]
-    parts, (diag, near, final) = refs[:4], refs[4:]
+    parts, crown, (diag, near, final) = refs[:4], refs[4:8], refs[8:]
     owner = (z & 1) == (row & 1)
     swap = z >> 1
-    last = parts[0].shape[0] - 1
-
-    def sides(i):
-        return jnp.where(owner, parts[0][i], parts[1][i]), parts[2][i] + parts[3][i]
-
-    for i in range(last):
-        for side, value in zip((swap, 1 - swap), sides(i)):
+    for i in range(parts[0].shape[0]):
+        here = jnp.where(owner, parts[0][i], parts[1][i])
+        there = parts[2][i] + parts[3][i]
+        for side, value in ((swap, here), (1 - swap, there)):
             if i == 0:
                 diag[side] = value
             else:
                 near[side, i - 1] = value
-    here, there = sides(last)
-    final[0] = jnp.where(swap == (row & 1), here, there)
-
-
-def parent_kernel(place, diag, near0, near1, diag_got, near0_got, near1_got, vt_ref, v_ref, flipped_ref):
+    arrived = crown[1][0] + (crown[2][0] + crown[3][0])
+    final[0] = jnp.where(z == 1 + (row & 1), crown[0][0], arrived)
+
+
+def parent_kernel(place, diag, near0, near1, pair, vt_ref, v_ref, p0, p1, p2, p3, flipped):
+    row, z = place[0], place[1]
     size = diag.shape[0]
-    swap = (place[0] & 1) > 0
-    near = jnp.concatenate([near0[...], near1[...]], axis=0)
-    near_got = jnp.concatenate([near0_got[...], near1_got[...]], axis=0)
-
-    def order(a, b):
-        return jnp.where(swap, b, a), jnp.where(swap, a, b)
-
-    diag_first, diag_second = order(diag[...], diag_got[...])
-    near_first, near_second = order(near, near_got)
-    top = jnp.concatenate([diag_first, near_first], axis=1)
-    low = jnp.concatenate([near_second, diag_second], axis=1)
-    merged = jnp.concatenate([top, low], axis=0)
-    dense = dot3(dot3(vt_ref[...], merged), v_ref[...])
-    flipped_ref[...] = eliminate(dense, size)[1].T
+
+    @pl.when(z == 1 + (row & 1))
+    def _():
+        swap = (row & 1) > 0
+        near = jnp.concatenate([near0[...], near1[...]], axis=0)
+
+        def order(a, b):
+            return jnp.where(swap, b, a), jnp.where(swap, a, b)
+
+        diag_first, diag_second = order(diag[...], pair[0])
+        near_first, near_second = order(near, pair[1])
+        top = jnp.concatenate([diag_first, near_first], axis=1)
+        low = jnp.concatenate([near_second, diag_second], axis=1)
+        merged = jnp.concatenate([top, low], axis=0)
+        dense = dot3(dot3(vt_ref[...], merged), v_ref[...])
+        flipped[0] = eliminate(dense, size)[1].T
+        deal(z, flipped, 0, (p0, p1, p2, p3))
 
 
 def call(kernel, outs, scalars, arrays, us=2, scratch=()):
@@ -272,7 +276,7 @@
     place = jnp.stack([row, column]).astype(jnp.int32)
     both = ("row", "col")
     owned = [(r, z) for r in range(n_row) for z in range(n_col) if z % 2 == r % 2]
-    heads = [(r, (n_col - 1) * (r % 2)) for r in range(n_row)]
+    heads = [(r, 1 + r % 2) for r in range(n_row)]
 
     def to_owner(x, j):
         return lax.ppermute(x, both, [(r * n_col + (z ^ j), r * n_col + z) for r, z in owned])
@@ -280,8 +284,17 @@
     def from_owner(x, j):
         return lax.ppermute(x, both, [(r * n_col + z, r * n_col + (z ^ j)) for r, z in owned])
 
-    def from_sibling(x, places):
-        return lax.ppermute(x, both, [((r ^ 1) * n_col + (z ^ 1), r * n_col + z) for r, z in places])
+    def from_sibling(x):
+        return lax.ppermute(x, both, [((r ^ 1) * n_col + (z ^ 1), r * n_col + z) for r, z in owned])
+
+    def from_neighbour(x):
+        return lax.ppermute(x, both, [(r * n_col + (z ^ 1), r * n_col + z) for r, z in heads])
+
+    def from_chip(x):
+        return lax.ppermute(x, both, [((r ^ 1) * n_col + z, r * n_col + z) for r, z in heads])
+
+    def from_head(x, j):
+        return lax.ppermute(x, both, [(r * n_col + z, r * n_col + (z ^ j)) for r, z in heads])
 
     def across(x, bit):
         return lax.ppermute(x, "row", [(r, r ^ bit) for r in range(n_row)])
@@ -292,8 +305,11 @@
             got.append(to_owner(payload, j))
         return got
 
-    def scatter(parts):
-        return [parts[0]] + [from_owner(parts[j], j) for j in range(1, 4)]
+    def scatter(parts, send):
+        got = [parts[0]]
+        for j in range(1, 4):
+            got.append(send(parts[j], j))
+        return got
 
     full, half, table = call(
         pack_kernel,
@@ -324,37 +340,44 @@
     n_early = gather(*after((split[0], split[1]), leaf[1:]))
     n_rest = gather(*after((split[2], split[3]), leaf[1:]))
     (skeletons,) = call(skeleton_kernel, [(4, edge, skeleton)], [place], leaf)
-    sibling = from_sibling(skeletons, owned)
+    sibling = from_sibling(skeletons)
 
     w, schur = call(
         leaf_kernel, [(4, skeleton, edge), (skeleton, skeleton)], [place], leaf, 22
     )
 
-    diag_got = from_sibling(schur, heads)
-    top, low, first = call(
+    diag_got = from_neighbour(schur)
+    top, low, first, pair = call(
         near_first_kernel,
-        [(skeleton // 2, skeleton)] * 2 + [(skeleton, skeleton)],
+        [(skeleton // 2, skeleton)] * 2 + [(skeleton, skeleton), (2, skeleton, skeleton)],
         [place, near_count],
-        [w, sibling, *n_early],
+        [w, sibling, *n_early, schur],
         4,
     )
-    top_got = from_sibling(top, heads)
-    low_got = from_sibling(low, heads)
-    chosen = call(name_kernel, [(slots - 1, edge, skeleton)] * 2, [place, near_ids], [*after(pieces, first), *swapped])
+    top_got = from_neighbour(top)
+    low_got = from_neighbour(low)
+    pair_got = from_chip(pair)
+    chosen = call(
+        name_kernel,
+        [(slots - 1, edge, skeleton)] * 2,
+        [place, near_ids],
+        [*after(pieces, first), *swapped],
+    )
     named = gather(*chosen)
-    (parent,) = call(
+    crown = call(
         parent_kernel,
-        [(skeleton, skeleton)],
+        [(1, quarter, skeleton)] * 4,
         [place],
-        [schur, top, low, diag_got, top_got, low_got, split[4], v],
-        22,
-    )
-    total = slots + 2
+        [diag_got, top_got, low_got, pair_got, split[4], v],
+        20,
+        [(1, skeleton, skeleton)],
+    )
+    total = slots + 1
     results = call(
         near_rest_kernel,
         [(total, quarter, skeleton)] * 4,
         [place, near_count],
-        [w, schur, first, parent, *n_rest, *named],
+        [w, schur, first, *n_rest, *named],
         7,
         [(total, skeleton, skeleton)],
     )
@@ -362,7 +385,7 @@
         finish_kernel,
         [(clusters, quarter, skeleton), (clusters, slots, quarter, skeleton), (1, quarter, skeleton)],
         [place],
-        scatter(results),
+        scatter(results, from_owner) + scatter(crown, from_head),
     )
     return tuple(jnp.swapaxes(x, -1, -2) for x in turned)
 

time: 160 us -> 159 us (level)
  waiting for transfers between devices: 41.1 us -> 60.5 us
  Pallas kernels: 60.6 us -> 45.4 us
  starting transfers between devices: 51.1 us -> 45.8 us
    ppermute x12, waiting for transfers between devices: 26.3 us -> 50.3 us  [to_owner(): lax.ppermute(x, both, [(r * n_col + (z ^ j), r * n_col + z) for r, z in o...]
    pallas_call x9, Pallas kernels: 60.6 us -> 45.4 us  [call(): pl.pallas_call(kernel, out_shape=shapes, in_specs=specs, out_specs=[vmem]...]
    ppermute x3, waiting for transfers between devices: 14.8 us -> 0.01 us  [from_owner(): lax.ppermute(x, both, [(r * n_col + z, r * n_col + (z ^ j)) for r, z in o...]
    ppermute x0 -> x7, waiting for transfers between devices: none -> 10.2 us  [the longest x3 10.1 us: from_head(): lax.ppermute(x, both, [(r * n_col + z, r * n_col + (z ^ j)) for r, z in h...]
    ppermute x0 -> x7, starting transfers between devices: none -> 7.29 us  [the longest x3 4 us: from_neighbour(): lax.ppermute(x, both, [(r * n_col + (z ^ 1), r * n_col + z) for r, z in h...]
    ppermute x3, starting transfers between devices: 10.1 us -> 5.26 us  [from_owner(): lax.ppermute(x, both, [(r * n_col + z, r * n_col + (z ^ j)) for r, z in o...]
    ppermute x4 -> x1, starting transfers between devices: 5.91 us -> 2.05 us  [from_sibling(): lax.ppermute(x, both, [((r ^ 1) * n_col + (z ^ 1), r * n_col + z) for r,...]
    ppermute x12, starting transfers between devices: 30.4 us -> 26.5 us  [to_owner(): lax.ppermute(x, both, [(r * n_col + (z ^ j), r * n_col + z) for r, z in o...]
  transfers between devices with their start and end apart: 23 -> 27, of which waited for: 6 -> 5; matrix products, arithmetic and copies ran while one was open for 1% -> 1% of each run, Pallas kernels for 31% -> 26%
where the time goes in v4:
time: 159 us; the launch traced here: 158 us
  waiting for transfers between devices  60.5 us (38%)
  starting transfers between devices  45.8 us (29%)
  Pallas kernels  45.4 us (29%)
  local copies, waits for them, and re-layouts  4.25 us (3%)
    ppermute x12, waiting for transfers between devices, to_owner(): lax.ppermute(x, both, [(r * n_col + (z ^ j), r * n_col + z) for r, z in o...  50.3 us
    pallas_call x9, Pallas kernels, call(): pl.pallas_call(kernel, out_shape=shapes, in_specs=specs, out_specs=[vmem]...  45.4 us
    ppermute x12, starting transfers between devices, to_owner(): lax.ppermute(x, both, [(r * n_col + (z ^ j), r * n_col + z) for r, z in o...  26.5 us
    ppermute x3, waiting for transfers between devices, from_head(): lax.ppermute(x, both, [(r * n_col + z, r * n_col + (z ^ j)) for r, z in h...  10.1 us
    ppermute x3, starting transfers between devices, from_owner(): lax.ppermute(x, both, [(r * n_col + z, r * n_col + (z ^ j)) for r, z in o...  5.26 us
    ppermute x4, starting transfers between devices, across(): return lax.ppermute(x, 'row', [(r, r ^ bit) for r in range(n_row)])  4.7 us
    unnamed x45, local copies, waits for them, and re-layouts  4.23 us
    ppermute x3, starting transfers between devices, from_neighbour(): lax.ppermute(x, both, [(r * n_col + (z ^ 1), r * n_col + z) for r, z in h...  4 us
  transfers between devices with their start and end apart: 27, of which 5 were waited for; matrix products, arithmetic and copies ran while one was open for 1% of the time, Pallas kernels for 26%

profile of v4, /device:TPU:0, one launch (start us, length us, event | category | flops | bytes accessed | tf_op | source)
XLA Modules:
  0.0 157.9 jit_solution(12928487836525020672)
XLA Ops:
  0.6 0.6 pad_add_fusion.place
  1.3 2.3 %shard_map.85 = (f32[8,128,128]{2,1,0:T(8,128)}, f32[6,128,128]{2,1,0:T(8,128)}, f32[2,128,256]{2,1,0:T(8,128)}) custom-call(s32[2]{0:T(128)} %pad_add_fusion.place, f32[2,512,128]{2,1,0:T(8,128)} %diag.1, f32[2,128,512]{2,1,0:T(8,128)} %bases.1), custom_call_target="tpu_custom_call" | custom-call | flops 2000000000 | bytes 2000000 | tf_op jit(solution)/shard_map/pallas_call | solution.py:254
  3.6 3.0 %collective-permute-start.10 = (f32[2,128,256]{2,1,0:T(8,128)}, f32[2,128,256]{2,1,0:T(8,128)S(1)}, u32[]{:S(2)}, u32[]{:S(2)}) collective-permute-start(f32[2,128,256]{2,1,0:T(8,128)} %get-tuple-element.49), channel_id=1, source_target_pairs={{0,8},{4,12},{8,0},{12,4},{16,24},{20,28},{24,16},{28,20},{1,9},{5... | collective-permute-start | bytes 786440 | tf_op jit(solution)/shard_map/ppermute | solution.py:300
  6.5 1.3 collective-permute-start
  7.8 4.5 %collective-permute-start.1 = (f32[6,128,128]{2,1,0:T(8,128)}, f32[6,128,128]{2,1,0:T(8,128)S(1)}, u32[]{:S(2)}, u32[]{:S(2)}) collective-permute-start(f32[6,128,128]{2,1,0:T(8,128)} %get-tuple-element.37), channel_id=1, source_target_pairs={{2,0},{0,2},{7,5},{5,7},{10,8},{8,10},{15,13},{13,15},{18,16},{16,... | collective-permute-start | bytes 1179656 | tf_op jit(solution)/shard_map/ppermute | solution.py:282
  12.3 1.3 collective-permute-start.2
  13.6 1.0 constant_dynamic-update-slice_fusion.1
  14.6 1.6 %collective-permute-start.11 = (f32[4,128,256]{2,1,0:T(8,128)S(1)}, f32[4,128,256]{2,1,0:T(8,128)}, u32[]{:S(2)}, u32[]{:S(2)}) collective-permute-start(f32[4,128,256]{2,1,0:T(8,128)S(1)} %constant_dynamic-update-slice_fusion.low0), channel_id=1, source_target_pairs={{0,16},{4,20},{8,24},{12,28},{16,0},{20,4},{24,8},{28,12},{1,17},{... | collective-permute-start | bytes 1572872 | tf_op jit(solution)/shard_map/ppermute | solution.py:300
  16.2 3.8 %shard_map.88 = (f32[4,128,128]{2,1,0:T(8,128)}, f32[4,128,128]{2,1,0:T(8,128)}, f32[12,128,128]{2,1,0:T(8,128)}, f32[12,128,128]{2,1,0:T(8,128)}, f32[512,512]{1,0:T(8,128)}) custom-call(s32[2]{0:T(128)} %pad_add_fusion.place, f32[2,16,128,128]{3,2,1,0:T(8,128)} %bitcast.7, f32[512,512]{1,0:T(8,128)} %bitcast.8), custom_call_target="tpu_custom_call" | custom-call | flops 2000000000 | bytes 2000000 | tf_op jit(solution)/shard_map/pallas_call | solution.py:254
  20.0 9.4 %collective-permute-done.1.far2 = f32[6,128,128]{2,1,0:T(8,128)S(1)} collective-permute-done((f32[6,128,128]{2,1,0:T(8,128)}, f32[6,128,128]{2,1,0:T(8,128)S(1)}, u32[]{:S(2)}, u32[]{:S(2)}) %collective-permute-start.1) | collective-permute-done | bytes 393248 | tf_op jit(solution)/shard_map/ppermute | solution.py:282
  29.5 1.3 collective-permute-start.4
  30.8 5.0 %collective-permute-start.5 = (f32[4,128,128]{2,1,0:T(8,128)}, f32[4,128,128]{2,1,0:T(8,128)}, u32[]{:S(2)}, u32[]{:S(2)}) collective-permute-start(f32[4,128,128]{2,1,0:T(8,128)} %get-tuple-element.43), channel_id=1, source_target_pairs={{2,0},{0,2},{7,5},{5,7},{10,8},{8,10},{15,13},{13,15},{18,16},{16,... | collective-permute-start | bytes 786440 | tf_op jit(solution)/shard_map/ppermute | solution.py:282
  35.9 1.3 collective-permute-start.6
  37.2 2.4 %shard_map.87 = f32[4,128,256]{2,1,0:T(8,128)} custom-call(s32[2]{0:T(128)} %pad_add_fusion.place, f32[8,128,128]{2,1,0:T(8,128)} %get-tuple-element.36.own, f32[8,128,128]{2,1,0:T(8,128)} %copy-done.5, f32[6,128,128]{2,1,0:T(8,128)} %copy-done.8, f32[6,128,128]{2,1,0:T(8,128)} %copy-done.9), custom_call_target="tpu_custom_call" | custom-call | flops 2000000000 | bytes 2000000 | tf_op jit(solution)/shard_map/pallas_call | solution.py:254
  39.6 2.1 %collective-permute-start.3 = (f32[4,128,256]{2,1,0:T(8,128)}, f32[4,128,256]{2,1,0:T(8,128)S(1)}, u32[]{:S(2)}, u32[]{:S(2)}) collective-permute-start(f32[4,128,256]{2,1,0:T(8,128)} %shard_map.87), channel_id=1, source_target_pairs={{5,0},{7,2},{0,5},{2,7},{13,8},{15,10},{8,13},{10,15},{21,16},{23,... | collective-permute-start | bytes 1572872 | tf_op jit(solution)/shard_map/ppermute | solution.py:288
  41.7 6.2 %collective-permute-done.5.n2 = f32[4,128,128]{2,1,0:T(8,128)} collective-permute-done((f32[4,128,128]{2,1,0:T(8,128)}, f32[4,128,128]{2,1,0:T(8,128)}, u32[]{:S(2)}, u32[]{:S(2)}) %collective-permute-start.5) | collective-permute-done | bytes 262176 | tf_op jit(solution)/shard_map/ppermute | solution.py:282
  47.9 1.3 collective-permute-start.7
  49.2 18.0 %shard_map.86 = (f32[4,256,128]{2,1,0:T(8,128)}, f32[256,256]{1,0:T(8,128)}) custom-call(s32[2]{0:T(128)} %pad_add_fusion.place, f32[8,128,128]{2,1,0:T(8,128)} %get-tuple-element.36.own, f32[8,128,128]{2,1,0:T(8,128)} %copy-done.5, f32[6,128,128]{2,1,0:T(8,128)} %copy-done.8, f32[6,128,128]{2,1,0:T(8,128)} %copy-done.9), custom_call_target="tpu_custom_call" | custom-call | flops 22000001024 | bytes 22000000 | tf_op jit(solution)/shard_map/pallas_call | solution.py:254
  67.3 2.3 %collective-permute-start.8 = (f32[12,128,128]{2,1,0:T(8,128)S(1)}, f32[12,128,128]{2,1,0:T(8,128)}, u32[]{:S(2)}, u32[]{:S(2)}) collective-permute-start(f32[12,128,128]{2,1,0:T(8,128)S(1)} %copy-done.2), channel_id=1, source_target_pairs={{2,0},{0,2},{7,5},{5,7},{10,8},{8,10},{15,13},{13,15},{18,16},{16,... | collective-permute-start | bytes 2359304 | tf_op jit(solution)/shard_map/ppermute | solution.py:282
  69.6 1.3 collective-permute-start.9
  70.9 3.7 %shard_map.89 = (f32[128,256]{1,0:T(8,128)}, f32[128,256]{1,0:T(8,128)}, f32[256,256]{1,0:T(8,128)}, f32[2,256,256]{2,1,0:T(8,128)}) custom-call(s32[2]{0:T(128)} %pad_add_fusion.place, s32[2]{0:T(128)} %count.3, f32[4,256,128]{2,1,0:T(8,128)} %get-tuple-element.38.w_ref, f32[4,128,256]{2,1,0:T(8,128)} %copy-done.7, f32[4,128,128]{2,1,0:T(8,128)} %get-tuple-element.42.n0, ...), custom_call_target="tpu_custom_call" | custom-call | flops 4000000000 | bytes 4000000 | tf_op jit(solution)/shard_map/pallas_call | solution.py:254
  74.7 2.6 %shard_map.90 = (f32[3,128,256]{2,1,0:T(8,128)}, f32[3,128,256]{2,1,0:T(8,128)}) custom-call(s32[2]{0:T(128)} %pad_add_fusion.place, s32[2,4]{1,0:T(2,128)} %ids.1, f32[4,128,256]{2,1,0:T(8,128)} %copy-done, f32[4,128,256]{2,1,0:T(8,128)} %collective-permute-done.11.low1, f32[4,128,256]{2,1,0:T(8,128)} %collective-permute-done.12.high0, ...), custom_call_target="tpu_custom_call" | custom-call | flops 2000000000 | bytes 2000000 | tf_op jit(solution)/shard_map/pallas_call | solution.py:254
  77.3 1.3 collective-permute-start.14
  78.6 4.4 %collective-permute-start.15 = (f32[3,128,256]{2,1,0:T(8,128)}, f32[3,128,256]{2,1,0:T(8,128)}, u32[]{:S(2)}, u32[]{:S(2)}) collective-permute-start(f32[3,128,256]{2,1,0:T(8,128)} %get-tuple-element.53), channel_id=1, source_target_pairs={{2,0},{0,2},{7,5},{5,7},{10,8},{8,10},{15,13},{13,15},{18,16},{16,... | collective-permute-start | bytes 1179656 | tf_op jit(solution)/shard_map/ppermute | solution.py:282
  83.1 1.3 collective-permute-start.16
  84.4 29.7 %collective-permute-done.8.refs_2_ = f32[12,128,128]{2,1,0:T(8,128)} collective-permute-done((f32[12,128,128]{2,1,0:T(8,128)S(1)}, f32[12,128,128]{2,1,0:T(8,128)}, u32[]{:S(2)}, u32[]{:S(2)}) %collective-permute-start.8) | collective-permute-done | bytes 786464 | tf_op jit(solution)/shard_map/ppermute | solution.py:282
  114.1 1.3 collective-permute-start.20
  115.4 0.7 collective-permute-start.23
  116.1 1.4 collective-permute-start.21
  117.6 5.0 %collective-permute-done.15.refs_6_ = f32[3,128,256]{2,1,0:T(8,128)} collective-permute-done((f32[3,128,256]{2,1,0:T(8,128)}, f32[3,128,256]{2,1,0:T(8,128)}, u32[]{:S(2)}, u32[]{:S(2)}) %collective-permute-start.15) | collective-permute-done | bytes 393248 | tf_op jit(solution)/shard_map/ppermute | solution.py:282
  122.5 1.3 collective-permute-start.22
  123.9 0.8 copy-done.10
  124.6 7.6 %shard_map.91 = (f32[5,64,256]{2,1,0:T(8,128)}, f32[5,64,256]{2,1,0:T(8,128)}, f32[5,64,256]{2,1,0:T(8,128)}, f32[5,64,256]{2,1,0:T(8,128)}) custom-call(s32[2]{0:T(128)} %pad_add_fusion.place, s32[2]{0:T(128)} %count.3, f32[4,256,128]{2,1,0:T(8,128)} %get-tuple-element.38.w_ref, f32[256,256]{1,0:T(8,128)} %get-tuple-element.39.schur, ...), custom_call_target="tpu_custom_call" | custom-call | flops 7000000000 | bytes 7000000 | tf_op jit(solution)/shard_map/pallas_call | solution.py:254
  132.2 1.3 collective-permute-start.17
  133.5 0.7 copy-done.14
  134.2 2.6 %collective-permute-start.18 = (f32[5,64,256]{2,1,0:T(8,128)}, f32[5,64,256]{2,1,0:T(8,128)S(1)}, u32[]{:S(2)}, u32[]{:S(2)}) collective-permute-start(f32[5,64,256]{2,1,0:T(8,128)} %get-tuple-element.56), channel_id=1, source_target_pairs={{0,2},{2,0},{5,7},{7,5},{8,10},{10,8},{13,15},{15,13},{16,18},{18,... | collective-permute-start | bytes 983048 | tf_op jit(solution)/shard_map/ppermute | solution.py:285
  136.9 1.3 collective-permute-start.19
  138.3 0.6 copy-done.18
  138.9 0.2 copy-done.6
  139.1 2.8 %shard_map.92 = (f32[1,64,256]{2,1,0:T(8,128)}, f32[1,64,256]{2,1,0:T(8,128)}, f32[1,64,256]{2,1,0:T(8,128)}, f32[1,64,256]{2,1,0:T(8,128)}) custom-call(s32[2]{0:T(128)} %pad_add_fusion.place, f32[256,256]{1,0:T(8,128)} %copy-done.14, f32[128,256]{1,0:T(8,128)} %copy-done.17, f32[128,256]{1,0:T(8,128)} %copy-done.18, f32[2,256,256]{2,1,0:T(8,128)} %copy-done.6, ...), custom_call_target="tpu_custom_call" | custom-call | flops 20000000000 | bytes 20000000 | tf_op jit(solution)/shard_map/pallas_call | solution.py:254
  141.9 1.3 collective-permute-start.24
  143.1 0.7 collective-permute-start.25
  143.8 10.1 %collective-permute-done.24.refs_5_ = f32[1,64,256]{2,1,0:T(8,128)S(1)} collective-permute-done((f32[1,64,256]{2,1,0:T(8,128)}, f32[1,64,256]{2,1,0:T(8,128)S(1)}, u32[]{:S(2)}, u32[]{:S(2)}) %collective-permute-start.24) | collective-permute-done | bytes 65568 | tf_op jit(solution)/shard_map/ppermute | solution.py:297
  154.0 0.7 collective-permute-start.26
  154.7 0.5 copy-done.20
  155.4 0.1 copy-done.12
  155.5 0.1 copy-done.13
  155.6 2.2 %shard_map.93 = (f32[2,64,256]{2,1,0:T(8,128)}, f32[2,4,64,256]{3,2,1,0:T(8,128)}, f32[1,64,256]{2,1,0:T(8,128)}) custom-call(s32[2]{0:T(128)} %pad_add_fusion.place, f32[5,64,256]{2,1,0:T(8,128)} %get-tuple-element.54.refs_0_, f32[5,64,256]{2,1,0:T(8,128)} %copy-done.11, f32[5,64,256]{2,1,0:T(8,128)} %copy-done.12, f32[5,64,256]{2,1,0:T(8,128)} %copy-done.13, ...), custom_call_target="tpu_custom_call" | custom-call | flops 2000000000 | bytes 2000000 | tf_op jit(solution)/shard_map/pallas_call | solution.py:254
  (62 shorter events, 0.4 us)
Async XLA Ops:
  3.6 11.0 %collective-permute-start.10 = (f32[2,128,256]{2,1,0:T(8,128)}, f32[2,128,256]{2,1,0:T(8,128)S(1)}, u32[]{:S(2)}, u32[]{:S(2)}) collective-permute-start(f32[2,128,256]{2,1,0:T(8,128)} %get-tuple-element.49), channel_id=1, source_target_pairs={{0,8},{4,12},{8,0},{12,4},{16,24},{20,28},{24,16},{28,20},{1,9},{5... | collective-permute-start | bytes 786440 | tf_op jit(solution)/shard_map/ppermute | solution.py:300
  6.5 22.9 %collective-permute-start = (f32[8,128,128]{2,1,0:T(8,128)}, f32[8,128,128]{2,1,0:T(8,128)S(1)}, u32[]{:S(2)}, u32[]{:S(2)}) collective-permute-start(f32[8,128,128]{2,1,0:T(8,128)} %get-tuple-element.36.own), channel_id=1, source_target_pairs={{1,0},{3,2},{4,5},{6,7},{9,8},{11,10},{12,13},{14,15},{17,16},{19,... | collective-permute-start | bytes 1572872 | tf_op jit(solution)/shard_map/ppermute | solution.py:282
  7.8 21.6 %collective-permute-start.1 = (f32[6,128,128]{2,1,0:T(8,128)}, f32[6,128,128]{2,1,0:T(8,128)S(1)}, u32[]{:S(2)}, u32[]{:S(2)}) collective-permute-start(f32[6,128,128]{2,1,0:T(8,128)} %get-tuple-element.37), channel_id=1, source_target_pairs={{2,0},{0,2},{7,5},{5,7},{10,8},{8,10},{15,13},{13,15},{18,16},{16,... | collective-permute-start | bytes 1179656 | tf_op jit(solution)/shard_map/ppermute | solution.py:282
  12.3 17.1 %collective-permute-start.2 = (f32[6,128,128]{2,1,0:T(8,128)}, f32[6,128,128]{2,1,0:T(8,128)S(1)}, u32[]{:S(2)}, u32[]{:S(2)}) collective-permute-start(f32[6,128,128]{2,1,0:T(8,128)} %get-tuple-element.37), channel_id=1, source_target_pairs={{3,0},{1,2},{6,5},{4,7},{11,8},{9,10},{14,13},{12,15},{19,16},{17,... | collective-permute-start | bytes 1179656 | tf_op jit(solution)/shard_map/ppermute | solution.py:282
  14.6 21.2 %copy-start = (f32[4,128,256]{2,1,0:T(8,128)}, f32[4,128,256]{2,1,0:T(8,128)S(1)}, u32[]{:S(2)}) copy-start(f32[4,128,256]{2,1,0:T(8,128)S(1)} %constant_dynamic-update-slice_fusion.low0) | copy-start | bytes 1572868
  14.6 34.5 %collective-permute-start.11 = (f32[4,128,256]{2,1,0:T(8,128)S(1)}, f32[4,128,256]{2,1,0:T(8,128)}, u32[]{:S(2)}, u32[]{:S(2)}) collective-permute-start(f32[4,128,256]{2,1,0:T(8,128)S(1)} %constant_dynamic-update-slice_fusion.low0), channel_id=1, source_target_pairs={{0,16},{4,20},{8,24},{12,28},{16,0},{20,4},{24,8},{28,12},{1,17},{... | collective-permute-start | bytes 1572872 | tf_op jit(solution)/shard_map/ppermute | solution.py:300
  29.4 7.7 %copy-start.8 = (f32[6,128,128]{2,1,0:T(8,128)}, f32[6,128,128]{2,1,0:T(8,128)S(1)}, u32[]{:S(2)}) copy-start(f32[6,128,128]{2,1,0:T(8,128)S(1)} %collective-permute-done.1.far2) | copy-start | bytes 1179652
  29.5 7.7 %copy-start.9 = (f32[6,128,128]{2,1,0:T(8,128)}, f32[6,128,128]{2,1,0:T(8,128)S(1)}, u32[]{:S(2)}) copy-start(f32[6,128,128]{2,1,0:T(8,128)S(1)} %collective-permute-done.2.far3) | copy-start | bytes 1179652
  29.5 7.7 %copy-start.5 = (f32[8,128,128]{2,1,0:T(8,128)}, f32[8,128,128]{2,1,0:T(8,128)S(1)}, u32[]{:S(2)}) copy-start(f32[8,128,128]{2,1,0:T(8,128)S(1)} %collective-permute-done.near) | copy-start | bytes 1572868
  29.5 10.1 %collective-permute-start.4 = (f32[4,128,128]{2,1,0:T(8,128)}, f32[4,128,128]{2,1,0:T(8,128)S(1)}, u32[]{:S(2)}, u32[]{:S(2)}) collective-permute-start(f32[4,128,128]{2,1,0:T(8,128)} %get-tuple-element.42.n0), channel_id=1, source_target_pairs={{1,0},{3,2},{4,5},{6,7},{9,8},{11,10},{12,13},{14,15},{17,16},{19,... | collective-permute-start | bytes 786440 | tf_op jit(solution)/shard_map/ppermute | solution.py:282
  30.8 17.1 %collective-permute-start.5 = (f32[4,128,128]{2,1,0:T(8,128)}, f32[4,128,128]{2,1,0:T(8,128)}, u32[]{:S(2)}, u32[]{:S(2)}) collective-permute-start(f32[4,128,128]{2,1,0:T(8,128)} %get-tuple-element.43), channel_id=1, source_target_pairs={{2,0},{0,2},{7,5},{5,7},{10,8},{8,10},{15,13},{13,15},{18,16},{16,... | collective-permute-start | bytes 786440 | tf_op jit(solution)/shard_map/ppermute | solution.py:282
  35.8 38.9 %collective-permute-start.12 = (f32[4,128,256]{2,1,0:T(8,128)S(1)}, f32[4,128,256]{2,1,0:T(8,128)}, u32[]{:S(2)}, u32[]{:S(2)}) collective-permute-start(f32[4,128,256]{2,1,0:T(8,128)S(1)} %constant_dynamic-update-slice_fusion.low0), channel_id=1, source_target_pairs={{0,4},{4,0},{8,12},{12,8},{16,20},{20,16},{24,28},{28,24},{1,5},{5... | collective-permute-start | bytes 1572872 | tf_op jit(solution)/shard_map/ppermute | solution.py:300
  35.9 31.4 %collective-permute-start.6 = (f32[4,128,128]{2,1,0:T(8,128)}, f32[4,128,128]{2,1,0:T(8,128)}, u32[]{:S(2)}, u32[]{:S(2)}) collective-permute-start(f32[4,128,128]{2,1,0:T(8,128)} %get-tuple-element.43), channel_id=1, source_target_pairs={{3,0},{1,2},{6,5},{4,7},{11,8},{9,10},{14,13},{12,15},{19,16},{17,... | collective-permute-start | bytes 786440 | tf_op jit(solution)/shard_map/ppermute | solution.py:282
  37.2 10.7 %copy-start.1 = (f32[12,128,128]{2,1,0:T(8,128)S(1)}, f32[12,128,128]{2,1,0:T(8,128)}, u32[]{:S(2)}) copy-start(f32[12,128,128]{2,1,0:T(8,128)} %get-tuple-element.47.refs_0_) | copy-start | bytes 2359300
  39.6 27.7 %copy-start.2 = (f32[12,128,128]{2,1,0:T(8,128)S(1)}, f32[12,128,128]{2,1,0:T(8,128)}, u32[]{:S(2)}) copy-start(f32[12,128,128]{2,1,0:T(8,128)} %get-tuple-element.48) | copy-start | bytes 2359300
  39.6 2.1 %copy-start.15 = (f32[4,128,128]{2,1,0:T(8,128)}, f32[4,128,128]{2,1,0:T(8,128)S(1)}, u32[]{:S(2)}) copy-start(f32[4,128,128]{2,1,0:T(8,128)S(1)} %collective-permute-done.4.n1) | copy-start | bytes 786436
  39.6 30.0 %collective-permute-start.3 = (f32[4,128,256]{2,1,0:T(8,128)}, f32[4,128,256]{2,1,0:T(8,128)S(1)}, u32[]{:S(2)}, u32[]{:S(2)}) collective-permute-start(f32[4,128,256]{2,1,0:T(8,128)} %shard_map.87), channel_id=1, source_target_pairs={{5,0},{7,2},{0,5},{2,7},{13,8},{15,10},{8,13},{10,15},{21,16},{23,... | collective-permute-start | bytes 1572872 | tf_op jit(solution)/shard_map/ppermute | solution.py:288
  47.9 35.2 %collective-permute-start.7 = (f32[12,128,128]{2,1,0:T(8,128)S(1)}, f32[12,128,128]{2,1,0:T(8,128)S(1)}, u32[]{:S(2)}, u32[]{:S(2)}) collective-permute-start(f32[12,128,128]{2,1,0:T(8,128)S(1)} %copy-done.1), channel_id=1, source_target_pairs={{1,0},{3,2},{4,5},{6,7},{9,8},{11,10},{12,13},{14,15},{17,16},{19,... | collective-permute-start | bytes 2359304 | tf_op jit(solution)/shard_map/ppermute | solution.py:282
  49.2 25.5 %collective-permute-start.13 = (f32[4,128,256]{2,1,0:T(8,128)}, f32[4,128,256]{2,1,0:T(8,128)}, u32[]{:S(2)}, u32[]{:S(2)}) collective-permute-start(f32[4,128,256]{2,1,0:T(8,128)} %collective-permute-done.11.low1), channel_id=1, source_target_pairs={{0,4},{4,0},{8,12},{12,8},{16,20},{20,16},{24,28},{28,24},{1,5},{5... | collective-permute-start | bytes 1572872 | tf_op jit(solution)/shard_map/ppermute | solution.py:300
  67.3 46.9 %collective-permute-start.8 = (f32[12,128,128]{2,1,0:T(8,128)S(1)}, f32[12,128,128]{2,1,0:T(8,128)}, u32[]{:S(2)}, u32[]{:S(2)}) collective-permute-start(f32[12,128,128]{2,1,0:T(8,128)S(1)} %copy-done.2), channel_id=1, source_target_pairs={{2,0},{0,2},{7,5},{5,7},{10,8},{8,10},{15,13},{13,15},{18,16},{16,... | collective-permute-start | bytes 2359304 | tf_op jit(solution)/shard_map/ppermute | solution.py:282
  69.6 1.3 copy-start.7
  69.6 45.8 %collective-permute-start.9 = (f32[12,128,128]{2,1,0:T(8,128)S(1)}, f32[12,128,128]{2,1,0:T(8,128)}, u32[]{:S(2)}, u32[]{:S(2)}) collective-permute-start(f32[12,128,128]{2,1,0:T(8,128)S(1)} %copy-done.2), channel_id=1, source_target_pairs={{3,0},{1,2},{6,5},{4,7},{11,8},{9,10},{14,13},{12,15},{19,16},{17,... | collective-permute-start | bytes 2359304 | tf_op jit(solution)/shard_map/ppermute | solution.py:282
  74.7 40.8 %copy-start.4 = (f32[2,256,256]{2,1,0:T(8,128)S(1)}, f32[2,256,256]{2,1,0:T(8,128)}, u32[]{:S(2)}) copy-start(f32[2,256,256]{2,1,0:T(8,128)} %get-tuple-element.60) | copy-start | bytes 1572868
  74.7 47.9 %copy-start.16 = (f32[128,256]{1,0:T(8,128)S(1)}, f32[128,256]{1,0:T(8,128)}, u32[]{:S(2)}) copy-start(f32[128,256]{1,0:T(8,128)} %get-tuple-element.59) | copy-start | bytes 393220
  77.3 38.8 %collective-permute-start.14 = (f32[3,128,256]{2,1,0:T(8,128)}, f32[3,128,256]{2,1,0:T(8,128)}, u32[]{:S(2)}, u32[]{:S(2)}) collective-permute-start(f32[3,128,256]{2,1,0:T(8,128)} %get-tuple-element.52.refs_4_), channel_id=1, source_target_pairs={{1,0},{3,2},{4,5},{6,7},{9,8},{11,10},{12,13},{14,15},{17,16},{19,... | collective-permute-start | bytes 1179656 | tf_op jit(solution)/shard_map/ppermute | solution.py:282
  78.6 43.9 %collective-permute-start.15 = (f32[3,128,256]{2,1,0:T(8,128)}, f32[3,128,256]{2,1,0:T(8,128)}, u32[]{:S(2)}, u32[]{:S(2)}) collective-permute-start(f32[3,128,256]{2,1,0:T(8,128)} %get-tuple-element.53), channel_id=1, source_target_pairs={{2,0},{0,2},{7,5},{5,7},{10,8},{8,10},{15,13},{13,15},{18,16},{16,... | collective-permute-start | bytes 1179656 | tf_op jit(solution)/shard_map/ppermute | solution.py:282
  83.1 40.8 %copy-start.3 = (f32[12,128,128]{2,1,0:T(8,128)}, f32[12,128,128]{2,1,0:T(8,128)S(1)}, u32[]{:S(2)}) copy-start(f32[12,128,128]{2,1,0:T(8,128)S(1)} %collective-permute-done.7.refs_1_) | copy-start | bytes 2359300
  83.1 40.8 %collective-permute-start.16 = (f32[3,128,256]{2,1,0:T(8,128)}, f32[3,128,256]{2,1,0:T(8,128)S(1)}, u32[]{:S(2)}, u32[]{:S(2)}) collective-permute-start(f32[3,128,256]{2,1,0:T(8,128)} %get-tuple-element.53), channel_id=1, source_target_pairs={{3,0},{1,2},{6,5},{4,7},{11,8},{9,10},{14,13},{12,15},{19,16},{17,... | collective-permute-start | bytes 1179656 | tf_op jit(solution)/shard_map/ppermute | solution.py:282
  114.1 19.4 %collective-permute-start.20 = (f32[256,256]{1,0:T(8,128)}, f32[256,256]{1,0:T(8,128)S(1)}, u32[]{:S(2)}, u32[]{:S(2)}) collective-permute-start(f32[256,256]{1,0:T(8,128)} %get-tuple-element.39.schur), channel_id=1, source_target_pairs={{0,1},{7,6},{8,9},{15,14},{16,17},{23,22},{24,25},{31,30}} | collective-permute-start | bytes 786440 | tf_op jit(solution)/shard_map/ppermute | solution.py:291
  115.4 22.8 %collective-permute-start.23 = (f32[2,256,256]{2,1,0:T(8,128)S(1)}, f32[2,256,256]{2,1,0:T(8,128)S(1)}, u32[]{:S(2)}, u32[]{:S(2)}) collective-permute-start(f32[2,256,256]{2,1,0:T(8,128)S(1)} %copy-done.4), channel_id=1, source_target_pairs={{5,1},{2,6},{13,9},{10,14},{21,17},{18,22},{29,25},{26,30}} | collective-permute-start | bytes 1572872 | tf_op jit(solution)/shard_map/ppermute | solution.py:294
  116.1 20.8 %collective-permute-start.21 = (f32[128,256]{1,0:T(8,128)}, f32[128,256]{1,0:T(8,128)S(1)}, u32[]{:S(2)}, u32[]{:S(2)}) collective-permute-start(f32[128,256]{1,0:T(8,128)} %get-tuple-element.58), channel_id=1, source_target_pairs={{0,1},{7,6},{8,9},{15,14},{16,17},{23,22},{24,25},{31,30}} | collective-permute-start | bytes 393224 | tf_op jit(solution)/shard_map/ppermute | solution.py:291
  122.5 15.7 %collective-permute-start.22 = (f32[128,256]{1,0:T(8,128)S(1)}, f32[128,256]{1,0:T(8,128)S(1)}, u32[]{:S(2)}, u32[]{:S(2)}) collective-permute-start(f32[128,256]{1,0:T(8,128)S(1)} %copy-done.16), channel_id=1, source_target_pairs={{0,1},{7,6},{8,9},{15,14},{16,17},{23,22},{24,25},{31,30}} | collective-permute-start | bytes 393224 | tf_op jit(solution)/shard_map/ppermute | solution.py:291
  123.8 0.8 copy-start.10
  132.2 22.4 %collective-permute-start.17 = (f32[5,64,256]{2,1,0:T(8,128)}, f32[5,64,256]{2,1,0:T(8,128)S(1)}, u32[]{:S(2)}, u32[]{:S(2)}) collective-permute-start(f32[5,64,256]{2,1,0:T(8,128)} %get-tuple-element.55), channel_id=1, source_target_pairs={{0,1},{2,3},{5,4},{7,6},{8,9},{10,11},{13,12},{15,14},{16,17},{18,... | collective-permute-start | bytes 983048 | tf_op jit(solution)/shard_map/ppermute | solution.py:285
  133.5 0.7 copy-start.14
  134.2 20.4 %collective-permute-start.18 = (f32[5,64,256]{2,1,0:T(8,128)}, f32[5,64,256]{2,1,0:T(8,128)S(1)}, u32[]{:S(2)}, u32[]{:S(2)}) collective-permute-start(f32[5,64,256]{2,1,0:T(8,128)} %get-tuple-element.56), channel_id=1, source_target_pairs={{0,2},{2,0},{5,7},{7,5},{8,10},{10,8},{13,15},{15,13},{16,18},{18,... | collective-permute-start | bytes 983048 | tf_op jit(solution)/shard_map/ppermute | solution.py:285
  136.9 1.4 copy-start.17
  136.9 17.8 %collective-permute-start.19 = (f32[5,64,256]{2,1,0:T(8,128)}, f32[5,64,256]{2,1,0:T(8,128)S(1)}, u32[]{:S(2)}, u32[]{:S(2)}) collective-permute-start(f32[5,64,256]{2,1,0:T(8,128)} %get-tuple-element.57), channel_id=1, source_target_pairs={{0,3},{2,1},{5,6},{7,4},{8,11},{10,9},{13,14},{15,12},{16,19},{18,... | collective-permute-start | bytes 983048 | tf_op jit(solution)/shard_map/ppermute | solution.py:285
  138.2 0.7 copy-start.18
  138.3 0.8 copy-start.6
  141.9 12.1 %collective-permute-start.24 = (f32[1,64,256]{2,1,0:T(8,128)}, f32[1,64,256]{2,1,0:T(8,128)S(1)}, u32[]{:S(2)}, u32[]{:S(2)}) collective-permute-start(f32[1,64,256]{2,1,0:T(8,128)} %get-tuple-element.63), channel_id=1, source_target_pairs={{1,0},{6,7},{9,8},{14,15},{17,16},{22,23},{25,24},{30,31}} | collective-permute-start | bytes 196616 | tf_op jit(solution)/shard_map/ppermute | solution.py:297
  143.1 11.5 %collective-permute-start.25 = (f32[1,64,256]{2,1,0:T(8,128)}, f32[1,64,256]{2,1,0:T(8,128)S(1)}, u32[]{:S(2)}, u32[]{:S(2)}) collective-permute-start(f32[1,64,256]{2,1,0:T(8,128)} %get-tuple-element.64), channel_id=1, source_target_pairs={{1,3},{6,4},{9,11},{14,12},{17,19},{22,20},{25,27},{30,28}} | collective-permute-start | bytes 196616 | tf_op jit(solution)/shard_map/ppermute | solution.py:297
  154.0 0.8 copy-start.19
  154.0 0.7 collective-permute-start.26
  154.6 0.6 copy-start.21
  154.7 0.7 copy-start.11
  154.7 0.8 copy-start.12
  154.7 0.9 copy-start.13
  (1 other events, 0.6 us)

commit v5 on v4

--- a/solution.py
+++ b/solution.py
@@ -193,18 +193,38 @@
 
 def near_rest_kernel(place, count, w_ref, schur, first, *refs):
     row, z = place[0], place[1]
-    blocks, named, parts, flipped = refs[:4], refs[4:8], refs[8:12], refs[12]
+    blocks, named, parts = refs[:4], refs[4:8], refs[8:12]
+    flipped, block_buffer, base_buffer, sems = refs[12:]
     total = named[0].shape[0]
 
     @pl.when((z & 1) == (row & 1))
     def _():
+        copies = []
+        for k in range(total):
+            for j in range(4):
+                tile = pl.ds(4 * k, 4)
+                copies.append(
+                    pltpu.make_async_copy(blocks[j].at[tile], block_buffer.at[j, tile], sems.at[k, j, 0])
+                )
+                copies.append(
+                    pltpu.make_async_copy(named[j].at[k], base_buffer.at[j, k], sems.at[k, j, 1])
+                )
+        for copy in copies:
+            copy.start()
         flipped[0] = schur[...]
         flipped[1] = first[...]
+        for i in range(2):
+            deal(z, flipped, i, parts)
         for k in range(total):
-            result = coupling(w_ref, [tall(n, 4 * k) for n in blocks], [s[k] for s in named])
+            for copy in copies[8 * k : 8 * k + 8]:
+                copy.wait()
+            result = coupling(
+                w_ref,
+                [tall(block_buffer.at[j], 4 * k) for j in range(4)],
+                [base_buffer[j, k] for j in range(4)],
+            )
             flipped[k + 2] = jnp.where(count[z >> 1] > k + 1, result, 0.0).T
-        for i in range(total + 2):
-            deal(z, flipped, i, parts)
+            deal(z, flipped, k + 2, parts)
 
 
 def finish_kernel(place, *refs):
@@ -246,9 +266,10 @@
         deal(z, flipped, 0, (p0, p1, p2, p3))
 
 
-def call(kernel, outs, scalars, arrays, us=2, scratch=()):
+def call(kernel, outs, scalars, arrays, us=2, scratch=(), left=0):
     vmem = pl.BlockSpec(memory_space=pltpu.VMEM)
-    specs = [pl.BlockSpec(memory_space=pltpu.SMEM)] * len(scalars) + [vmem] * len(arrays)
+    specs = [pl.BlockSpec(memory_space=pltpu.SMEM)] * len(scalars) + [vmem] * (len(arrays) - left)
+    specs += [pl.BlockSpec(memory_space=pl.ANY)] * left
     shapes = [jax.ShapeDtypeStruct(shape, jnp.float32) for shape in outs]
     cost = pl.CostEstimate(flops=us * 10**9, bytes_accessed=us * 10**6, transcendentals=0)
     return pl.pallas_call(
@@ -256,7 +277,7 @@
         out_shape=shapes,
         in_specs=specs,
         out_specs=[vmem] * len(outs),
-        scratch_shapes=[pltpu.VMEM(shape, jnp.float32) for shape in scratch],
+        scratch_shapes=[pltpu.VMEM(x, jnp.float32) if isinstance(x, tuple) else x for x in scratch],
         cost_estimate=cost,
     )(*scalars, *arrays)
 
@@ -379,7 +400,13 @@
         [place, near_count],
         [w, schur, first, *n_rest, *named],
         7,
-        [(total, skeleton, skeleton)],
+        [
+            (total, skeleton, skeleton),
+            (4, rest_blocks, edge, edge),
+            (4, slots - 1, edge, skeleton),
+            pltpu.SemaphoreType.DMA((slots - 1, 4, 2)),
+        ],
+        8,
     )
     turned = call(
         finish_kernel,

time: 159 us -> 159 us (level)
  waiting for transfers between devices: 60.5 us -> 58.7 us
    ppermute x3, waiting for transfers between devices: 10.1 us -> 8.37 us  [from_head(): lax.ppermute(x, both, [(r * n_col + z, r * n_col + (z ^ j)) for r, z in h...]
where the time goes in v5:
time: 159 us; the launch traced here: 157 us
  waiting for transfers between devices  58.7 us (37%)
  Pallas kernels  46 us (29%)
  starting transfers between devices  45.9 us (29%)
  local copies, waits for them, and re-layouts  4.25 us (3%)
    ppermute x12, waiting for transfers between devices, to_owner(): lax.ppermute(x, both, [(r * n_col + (z ^ j), r * n_col + z) for r, z in o...  50.3 us
    pallas_call x9, Pallas kernels, call(): pl.pallas_call(kernel, out_shape=shapes, in_specs=specs, out_specs=[vmem]...  46 us
    ppermute x12, starting transfers between devices, to_owner(): lax.ppermute(x, both, [(r * n_col + (z ^ j), r * n_col + z) for r, z in o...  26.5 us
    ppermute x3, waiting for transfers between devices, from_head(): lax.ppermute(x, both, [(r * n_col + z, r * n_col + (z ^ j)) for r, z in h...  8.37 us
    ppermute x3, starting transfers between devices, from_owner(): lax.ppermute(x, both, [(r * n_col + z, r * n_col + (z ^ j)) for r, z in o...  5.27 us
    ppermute x4, starting transfers between devices, across(): return lax.ppermute(x, 'row', [(r, r ^ bit) for r in range(n_row)])  4.7 us
    unnamed x45, local copies, waits for them, and re-layouts  4.23 us
    ppermute x3, starting transfers between devices, from_neighbour(): lax.ppermute(x, both, [(r * n_col + (z ^ 1), r * n_col + z) for r, z in h...  4 us
  transfers between devices with their start and end apart: 27, of which 5 were waited for; matrix products, arithmetic and copies ran while one was open for 1% of the time, Pallas kernels for 26%

profile of v5, /device:TPU:0, one launch (start us, length us, event | category | flops | bytes accessed | tf_op | source)
XLA Modules:
  0.0 156.7 jit_solution(3348017503631877561)
XLA Ops:
  0.6 0.6 pad_add_fusion.place
  1.3 2.3 %shard_map.85 = (f32[8,128,128]{2,1,0:T(8,128)}, f32[6,128,128]{2,1,0:T(8,128)}, f32[2,128,256]{2,1,0:T(8,128)}) custom-call(s32[2]{0:T(128)} %pad_add_fusion.place, f32[2,512,128]{2,1,0:T(8,128)} %diag.1, f32[2,128,512]{2,1,0:T(8,128)} %bases.1), custom_call_target="tpu_custom_call" | custom-call | flops 2000000000 | bytes 2000000 | tf_op jit(solution)/shard_map/pallas_call | solution.py:275
  3.6 3.0 %collective-permute-start.10 = (f32[2,128,256]{2,1,0:T(8,128)}, f32[2,128,256]{2,1,0:T(8,128)S(1)}, u32[]{:S(2)}, u32[]{:S(2)}) collective-permute-start(f32[2,128,256]{2,1,0:T(8,128)} %get-tuple-element.49), channel_id=1, source_target_pairs={{0,8},{4,12},{8,0},{12,4},{16,24},{20,28},{24,16},{28,20},{1,9},{5... | collective-permute-start | bytes 786440 | tf_op jit(solution)/shard_map/ppermute | solution.py:321
  6.5 1.3 collective-permute-start
  7.8 4.5 %collective-permute-start.1 = (f32[6,128,128]{2,1,0:T(8,128)}, f32[6,128,128]{2,1,0:T(8,128)S(1)}, u32[]{:S(2)}, u32[]{:S(2)}) collective-permute-start(f32[6,128,128]{2,1,0:T(8,128)} %get-tuple-element.37), channel_id=1, source_target_pairs={{2,0},{0,2},{7,5},{5,7},{10,8},{8,10},{15,13},{13,15},{18,16},{16,... | collective-permute-start | bytes 1179656 | tf_op jit(solution)/shard_map/ppermute | solution.py:303
  12.3 1.3 collective-permute-start.2
  13.6 1.0 constant_dynamic-update-slice_fusion.1
  14.6 1.6 %collective-permute-start.11 = (f32[4,128,256]{2,1,0:T(8,128)S(1)}, f32[4,128,256]{2,1,0:T(8,128)}, u32[]{:S(2)}, u32[]{:S(2)}) collective-permute-start(f32[4,128,256]{2,1,0:T(8,128)S(1)} %constant_dynamic-update-slice_fusion.low0), channel_id=1, source_target_pairs={{0,16},{4,20},{8,24},{12,28},{16,0},{20,4},{24,8},{28,12},{1,17},{... | collective-permute-start | bytes 1572872 | tf_op jit(solution)/shard_map/ppermute | solution.py:321
  16.2 3.8 %shard_map.88 = (f32[4,128,128]{2,1,0:T(8,128)}, f32[4,128,128]{2,1,0:T(8,128)}, f32[12,128,128]{2,1,0:T(8,128)}, f32[12,128,128]{2,1,0:T(8,128)}, f32[512,512]{1,0:T(8,128)}) custom-call(s32[2]{0:T(128)} %pad_add_fusion.place, f32[2,16,128,128]{3,2,1,0:T(8,128)} %bitcast.7, f32[512,512]{1,0:T(8,128)} %bitcast.8), custom_call_target="tpu_custom_call" | custom-call | flops 2000000000 | bytes 2000000 | tf_op jit(solution)/shard_map/pallas_call | solution.py:275
  20.0 9.4 %collective-permute-done.1.far2 = f32[6,128,128]{2,1,0:T(8,128)S(1)} collective-permute-done((f32[6,128,128]{2,1,0:T(8,128)}, f32[6,128,128]{2,1,0:T(8,128)S(1)}, u32[]{:S(2)}, u32[]{:S(2)}) %collective-permute-start.1) | collective-permute-done | bytes 393248 | tf_op jit(solution)/shard_map/ppermute | solution.py:303
  29.5 1.3 collective-permute-start.4
  30.8 5.0 %collective-permute-start.5 = (f32[4,128,128]{2,1,0:T(8,128)}, f32[4,128,128]{2,1,0:T(8,128)}, u32[]{:S(2)}, u32[]{:S(2)}) collective-permute-start(f32[4,128,128]{2,1,0:T(8,128)} %get-tuple-element.43), channel_id=1, source_target_pairs={{2,0},{0,2},{7,5},{5,7},{10,8},{8,10},{15,13},{13,15},{18,16},{16,... | collective-permute-start | bytes 786440 | tf_op jit(solution)/shard_map/ppermute | solution.py:303
  35.9 1.3 collective-permute-start.6
  37.2 2.4 %shard_map.87 = f32[4,128,256]{2,1,0:T(8,128)} custom-call(s32[2]{0:T(128)} %pad_add_fusion.place, f32[8,128,128]{2,1,0:T(8,128)} %get-tuple-element.36.own, f32[8,128,128]{2,1,0:T(8,128)} %copy-done.5, f32[6,128,128]{2,1,0:T(8,128)} %copy-done.8, f32[6,128,128]{2,1,0:T(8,128)} %copy-done.9), custom_call_target="tpu_custom_call" | custom-call | flops 2000000000 | bytes 2000000 | tf_op jit(solution)/shard_map/pallas_call | solution.py:275
  39.6 2.1 %collective-permute-start.3 = (f32[4,128,256]{2,1,0:T(8,128)}, f32[4,128,256]{2,1,0:T(8,128)S(1)}, u32[]{:S(2)}, u32[]{:S(2)}) collective-permute-start(f32[4,128,256]{2,1,0:T(8,128)} %shard_map.87), channel_id=1, source_target_pairs={{5,0},{7,2},{0,5},{2,7},{13,8},{15,10},{8,13},{10,15},{21,16},{23,... | collective-permute-start | bytes 1572872 | tf_op jit(solution)/shard_map/ppermute | solution.py:309
  41.7 6.2 %collective-permute-done.5.n2 = f32[4,128,128]{2,1,0:T(8,128)} collective-permute-done((f32[4,128,128]{2,1,0:T(8,128)}, f32[4,128,128]{2,1,0:T(8,128)}, u32[]{:S(2)}, u32[]{:S(2)}) %collective-permute-start.5) | collective-permute-done | bytes 262176 | tf_op jit(solution)/shard_map/ppermute | solution.py:303
  47.9 1.3 collective-permute-start.7
  49.2 18.0 %shard_map.86 = (f32[4,256,128]{2,1,0:T(8,128)}, f32[256,256]{1,0:T(8,128)}) custom-call(s32[2]{0:T(128)} %pad_add_fusion.place, f32[8,128,128]{2,1,0:T(8,128)} %get-tuple-element.36.own, f32[8,128,128]{2,1,0:T(8,128)} %copy-done.5, f32[6,128,128]{2,1,0:T(8,128)} %copy-done.8, f32[6,128,128]{2,1,0:T(8,128)} %copy-done.9), custom_call_target="tpu_custom_call" | custom-call | flops 22000001024 | bytes 22000000 | tf_op jit(solution)/shard_map/pallas_call | solution.py:275
  67.3 2.3 %collective-permute-start.8 = (f32[12,128,128]{2,1,0:T(8,128)S(1)}, f32[12,128,128]{2,1,0:T(8,128)}, u32[]{:S(2)}, u32[]{:S(2)}) collective-permute-start(f32[12,128,128]{2,1,0:T(8,128)S(1)} %copy-done.2), channel_id=1, source_target_pairs={{2,0},{0,2},{7,5},{5,7},{10,8},{8,10},{15,13},{13,15},{18,16},{16,... | collective-permute-start | bytes 2359304 | tf_op jit(solution)/shard_map/ppermute | solution.py:303
  69.6 1.3 collective-permute-start.9
  70.9 3.7 %shard_map.89 = (f32[128,256]{1,0:T(8,128)}, f32[128,256]{1,0:T(8,128)}, f32[256,256]{1,0:T(8,128)}, f32[2,256,256]{2,1,0:T(8,128)}) custom-call(s32[2]{0:T(128)} %pad_add_fusion.place, s32[2]{0:T(128)} %count.3, f32[4,256,128]{2,1,0:T(8,128)} %get-tuple-element.38.w_ref, f32[4,128,256]{2,1,0:T(8,128)} %copy-done.7, f32[4,128,128]{2,1,0:T(8,128)} %get-tuple-element.42.n0, ...), custom_call_target="tpu_custom_call" | custom-call | flops 4000000000 | bytes 4000000 | tf_op jit(solution)/shard_map/pallas_call | solution.py:275
  74.7 2.6 %shard_map.90 = (f32[3,128,256]{2,1,0:T(8,128)}, f32[3,128,256]{2,1,0:T(8,128)}) custom-call(s32[2]{0:T(128)} %pad_add_fusion.place, s32[2,4]{1,0:T(2,128)} %ids.1, f32[4,128,256]{2,1,0:T(8,128)} %copy-done, f32[4,128,256]{2,1,0:T(8,128)} %collective-permute-done.11.low1, f32[4,128,256]{2,1,0:T(8,128)} %collective-permute-done.12.high0, ...), custom_call_target="tpu_custom_call" | custom-call | flops 2000000000 | bytes 2000000 | tf_op jit(solution)/shard_map/pallas_call | solution.py:275
  77.3 1.3 collective-permute-start.14
  78.6 4.4 %collective-permute-start.15 = (f32[3,128,256]{2,1,0:T(8,128)}, f32[3,128,256]{2,1,0:T(8,128)}, u32[]{:S(2)}, u32[]{:S(2)}) collective-permute-start(f32[3,128,256]{2,1,0:T(8,128)} %get-tuple-element.53), channel_id=1, source_target_pairs={{2,0},{0,2},{7,5},{5,7},{10,8},{8,10},{15,13},{13,15},{18,16},{16,... | collective-permute-start | bytes 1179656 | tf_op jit(solution)/shard_map/ppermute | solution.py:303
  83.1 1.3 collective-permute-start.16
  84.4 29.7 %collective-permute-done.8.refs_2_ = f32[12,128,128]{2,1,0:T(8,128)} collective-permute-done((f32[12,128,128]{2,1,0:T(8,128)S(1)}, f32[12,128,128]{2,1,0:T(8,128)}, u32[]{:S(2)}, u32[]{:S(2)}) %collective-permute-start.8) | collective-permute-done | bytes 786464 | tf_op jit(solution)/shard_map/ppermute | solution.py:303
  114.1 1.3 collective-permute-start.20
  115.4 0.7 collective-permute-start.23
  116.1 1.4 collective-permute-start.21
  117.6 5.0 %collective-permute-done.15.refs_6_ = f32[3,128,256]{2,1,0:T(8,128)} collective-permute-done((f32[3,128,256]{2,1,0:T(8,128)}, f32[3,128,256]{2,1,0:T(8,128)}, u32[]{:S(2)}, u32[]{:S(2)}) %collective-permute-start.15) | collective-permute-done | bytes 393248 | tf_op jit(solution)/shard_map/ppermute | solution.py:303
  122.5 1.3 collective-permute-start.22
  123.9 0.8 copy-done.10
  124.6 8.1 %shard_map.91 = (f32[5,64,256]{2,1,0:T(8,128)}, f32[5,64,256]{2,1,0:T(8,128)}, f32[5,64,256]{2,1,0:T(8,128)}, f32[5,64,256]{2,1,0:T(8,128)}) custom-call(s32[2]{0:T(128)} %pad_add_fusion.place, s32[2]{0:T(128)} %count.3, f32[4,256,128]{2,1,0:T(8,128)} %get-tuple-element.38.w_ref, f32[256,256]{1,0:T(8,128)} %get-tuple-element.39.schur, ...), custom_call_target="tpu_custom_call" | custom-call | flops 7000000000 | bytes 7000000 | tf_op jit(solution)/shard_map/pallas_call | solution.py:275
  132.8 1.3 collective-permute-start.17
  134.1 0.7 copy-done.14
  134.8 2.6 %collective-permute-start.18 = (f32[5,64,256]{2,1,0:T(8,128)}, f32[5,64,256]{2,1,0:T(8,128)S(1)}, u32[]{:S(2)}, u32[]{:S(2)}) collective-permute-start(f32[5,64,256]{2,1,0:T(8,128)} %get-tuple-element.56), channel_id=1, source_target_pairs={{0,2},{2,0},{5,7},{7,5},{8,10},{10,8},{13,15},{15,13},{16,18},{18,... | collective-permute-start | bytes 983048 | tf_op jit(solution)/shard_map/ppermute | solution.py:306
  137.5 1.3 collective-permute-start.19
  138.9 0.6 copy-done.18
  139.5 0.2 copy-done.6
  139.7 2.8 %shard_map.92 = (f32[1,64,256]{2,1,0:T(8,128)}, f32[1,64,256]{2,1,0:T(8,128)}, f32[1,64,256]{2,1,0:T(8,128)}, f32[1,64,256]{2,1,0:T(8,128)}) custom-call(s32[2]{0:T(128)} %pad_add_fusion.place, f32[256,256]{1,0:T(8,128)} %copy-done.14, f32[128,256]{1,0:T(8,128)} %copy-done.17, f32[128,256]{1,0:T(8,128)} %copy-done.18, f32[2,256,256]{2,1,0:T(8,128)} %copy-done.6, ...), custom_call_target="tpu_custom_call" | custom-call | flops 20000000000 | bytes 20000000 | tf_op jit(solution)/shard_map/pallas_call | solution.py:275
  142.5 1.3 collective-permute-start.24
  143.7 0.7 collective-permute-start.25
  144.4 8.4 %collective-permute-done.24.refs_5_ = f32[1,64,256]{2,1,0:T(8,128)S(1)} collective-permute-done((f32[1,64,256]{2,1,0:T(8,128)}, f32[1,64,256]{2,1,0:T(8,128)S(1)}, u32[]{:S(2)}, u32[]{:S(2)}) %collective-permute-start.24) | collective-permute-done | bytes 65568 | tf_op jit(solution)/shard_map/ppermute | solution.py:318
  152.8 0.7 collective-permute-start.26
  153.5 0.5 copy-done.20
  154.2 0.1 copy-done.12
  154.4 0.1 copy-done.13
  154.5 2.2 %shard_map.93 = (f32[2,64,256]{2,1,0:T(8,128)}, f32[2,4,64,256]{3,2,1,0:T(8,128)}, f32[1,64,256]{2,1,0:T(8,128)}) custom-call(s32[2]{0:T(128)} %pad_add_fusion.place, f32[5,64,256]{2,1,0:T(8,128)} %get-tuple-element.54.refs_0_, f32[5,64,256]{2,1,0:T(8,128)} %copy-done.11, f32[5,64,256]{2,1,0:T(8,128)} %copy-done.12, f32[5,64,256]{2,1,0:T(8,128)} %copy-done.13, ...), custom_call_target="tpu_custom_call" | custom-call | flops 2000000000 | bytes 2000000 | tf_op jit(solution)/shard_map/pallas_call | solution.py:275
  (62 shorter events, 0.4 us)
Async XLA Ops:
  3.6 11.0 %collective-permute-start.10 = (f32[2,128,256]{2,1,0:T(8,128)}, f32[2,128,256]{2,1,0:T(8,128)S(1)}, u32[]{:S(2)}, u32[]{:S(2)}) collective-permute-start(f32[2,128,256]{2,1,0:T(8,128)} %get-tuple-element.49), channel_id=1, source_target_pairs={{0,8},{4,12},{8,0},{12,4},{16,24},{20,28},{24,16},{28,20},{1,9},{5... | collective-permute-start | bytes 786440 | tf_op jit(solution)/shard_map/ppermute | solution.py:321
  6.5 22.9 %collective-permute-start = (f32[8,128,128]{2,1,0:T(8,128)}, f32[8,128,128]{2,1,0:T(8,128)S(1)}, u32[]{:S(2)}, u32[]{:S(2)}) collective-permute-start(f32[8,128,128]{2,1,0:T(8,128)} %get-tuple-element.36.own), channel_id=1, source_target_pairs={{1,0},{3,2},{4,5},{6,7},{9,8},{11,10},{12,13},{14,15},{17,16},{19,... | collective-permute-start | bytes 1572872 | tf_op jit(solution)/shard_map/ppermute | solution.py:303
  7.8 21.6 %collective-permute-start.1 = (f32[6,128,128]{2,1,0:T(8,128)}, f32[6,128,128]{2,1,0:T(8,128)S(1)}, u32[]{:S(2)}, u32[]{:S(2)}) collective-permute-start(f32[6,128,128]{2,1,0:T(8,128)} %get-tuple-element.37), channel_id=1, source_target_pairs={{2,0},{0,2},{7,5},{5,7},{10,8},{8,10},{15,13},{13,15},{18,16},{16,... | collective-permute-start | bytes 1179656 | tf_op jit(solution)/shard_map/ppermute | solution.py:303
  12.3 17.1 %collective-permute-start.2 = (f32[6,128,128]{2,1,0:T(8,128)}, f32[6,128,128]{2,1,0:T(8,128)S(1)}, u32[]{:S(2)}, u32[]{:S(2)}) collective-permute-start(f32[6,128,128]{2,1,0:T(8,128)} %get-tuple-element.37), channel_id=1, source_target_pairs={{3,0},{1,2},{6,5},{4,7},{11,8},{9,10},{14,13},{12,15},{19,16},{17,... | collective-permute-start | bytes 1179656 | tf_op jit(solution)/shard_map/ppermute | solution.py:303
  14.6 21.2 %copy-start = (f32[4,128,256]{2,1,0:T(8,128)}, f32[4,128,256]{2,1,0:T(8,128)S(1)}, u32[]{:S(2)}) copy-start(f32[4,128,256]{2,1,0:T(8,128)S(1)} %constant_dynamic-update-slice_fusion.low0) | copy-start | bytes 1572868
  14.6 34.5 %collective-permute-start.11 = (f32[4,128,256]{2,1,0:T(8,128)S(1)}, f32[4,128,256]{2,1,0:T(8,128)}, u32[]{:S(2)}, u32[]{:S(2)}) collective-permute-start(f32[4,128,256]{2,1,0:T(8,128)S(1)} %constant_dynamic-update-slice_fusion.low0), channel_id=1, source_target_pairs={{0,16},{4,20},{8,24},{12,28},{16,0},{20,4},{24,8},{28,12},{1,17},{... | collective-permute-start | bytes 1572872 | tf_op jit(solution)/shard_map/ppermute | solution.py:321
  29.4 7.7 %copy-start.8 = (f32[6,128,128]{2,1,0:T(8,128)}, f32[6,128,128]{2,1,0:T(8,128)S(1)}, u32[]{:S(2)}) copy-start(f32[6,128,128]{2,1,0:T(8,128)S(1)} %collective-permute-done.1.far2) | copy-start | bytes 1179652
  29.5 7.7 %copy-start.9 = (f32[6,128,128]{2,1,0:T(8,128)}, f32[6,128,128]{2,1,0:T(8,128)S(1)}, u32[]{:S(2)}) copy-start(f32[6,128,128]{2,1,0:T(8,128)S(1)} %collective-permute-done.2.far3) | copy-start | bytes 1179652
  29.5 7.7 %copy-start.5 = (f32[8,128,128]{2,1,0:T(8,128)}, f32[8,128,128]{2,1,0:T(8,128)S(1)}, u32[]{:S(2)}) copy-start(f32[8,128,128]{2,1,0:T(8,128)S(1)} %collective-permute-done.near) | copy-start | bytes 1572868
  29.5 10.1 %collective-permute-start.4 = (f32[4,128,128]{2,1,0:T(8,128)}, f32[4,128,128]{2,1,0:T(8,128)S(1)}, u32[]{:S(2)}, u32[]{:S(2)}) collective-permute-start(f32[4,128,128]{2,1,0:T(8,128)} %get-tuple-element.42.n0), channel_id=1, source_target_pairs={{1,0},{3,2},{4,5},{6,7},{9,8},{11,10},{12,13},{14,15},{17,16},{19,... | collective-permute-start | bytes 786440 | tf_op jit(solution)/shard_map/ppermute | solution.py:303
  30.8 17.1 %collective-permute-start.5 = (f32[4,128,128]{2,1,0:T(8,128)}, f32[4,128,128]{2,1,0:T(8,128)}, u32[]{:S(2)}, u32[]{:S(2)}) collective-permute-start(f32[4,128,128]{2,1,0:T(8,128)} %get-tuple-element.43), channel_id=1, source_target_pairs={{2,0},{0,2},{7,5},{5,7},{10,8},{8,10},{15,13},{13,15},{18,16},{16,... | collective-permute-start | bytes 786440 | tf_op jit(solution)/shard_map/ppermute | solution.py:303
  35.8 38.9 %collective-permute-start.12 = (f32[4,128,256]{2,1,0:T(8,128)S(1)}, f32[4,128,256]{2,1,0:T(8,128)}, u32[]{:S(2)}, u32[]{:S(2)}) collective-permute-start(f32[4,128,256]{2,1,0:T(8,128)S(1)} %constant_dynamic-update-slice_fusion.low0), channel_id=1, source_target_pairs={{0,4},{4,0},{8,12},{12,8},{16,20},{20,16},{24,28},{28,24},{1,5},{5... | collective-permute-start | bytes 1572872 | tf_op jit(solution)/shard_map/ppermute | solution.py:321
  35.9 31.4 %collective-permute-start.6 = (f32[4,128,128]{2,1,0:T(8,128)}, f32[4,128,128]{2,1,0:T(8,128)}, u32[]{:S(2)}, u32[]{:S(2)}) collective-permute-start(f32[4,128,128]{2,1,0:T(8,128)} %get-tuple-element.43), channel_id=1, source_target_pairs={{3,0},{1,2},{6,5},{4,7},{11,8},{9,10},{14,13},{12,15},{19,16},{17,... | collective-permute-start | bytes 786440 | tf_op jit(solution)/shard_map/ppermute | solution.py:303
  37.2 10.7 %copy-start.1 = (f32[12,128,128]{2,1,0:T(8,128)S(1)}, f32[12,128,128]{2,1,0:T(8,128)}, u32[]{:S(2)}) copy-start(f32[12,128,128]{2,1,0:T(8,128)} %get-tuple-element.47.refs_0_) | copy-start | bytes 2359300
  39.6 27.7 %copy-start.2 = (f32[12,128,128]{2,1,0:T(8,128)S(1)}, f32[12,128,128]{2,1,0:T(8,128)}, u32[]{:S(2)}) copy-start(f32[12,128,128]{2,1,0:T(8,128)} %get-tuple-element.48) | copy-start | bytes 2359300
  39.6 2.1 %copy-start.15 = (f32[4,128,128]{2,1,0:T(8,128)}, f32[4,128,128]{2,1,0:T(8,128)S(1)}, u32[]{:S(2)}) copy-start(f32[4,128,128]{2,1,0:T(8,128)S(1)} %collective-permute-done.4.n1) | copy-start | bytes 786436
  39.6 30.0 %collective-permute-start.3 = (f32[4,128,256]{2,1,0:T(8,128)}, f32[4,128,256]{2,1,0:T(8,128)S(1)}, u32[]{:S(2)}, u32[]{:S(2)}) collective-permute-start(f32[4,128,256]{2,1,0:T(8,128)} %shard_map.87), channel_id=1, source_target_pairs={{5,0},{7,2},{0,5},{2,7},{13,8},{15,10},{8,13},{10,15},{21,16},{23,... | collective-permute-start | bytes 1572872 | tf_op jit(solution)/shard_map/ppermute | solution.py:309
  47.9 35.2 %collective-permute-start.7 = (f32[12,128,128]{2,1,0:T(8,128)S(1)}, f32[12,128,128]{2,1,0:T(8,128)S(1)}, u32[]{:S(2)}, u32[]{:S(2)}) collective-permute-start(f32[12,128,128]{2,1,0:T(8,128)S(1)} %copy-done.1), channel_id=1, source_target_pairs={{1,0},{3,2},{4,5},{6,7},{9,8},{11,10},{12,13},{14,15},{17,16},{19,... | collective-permute-start | bytes 2359304 | tf_op jit(solution)/shard_map/ppermute | solution.py:303
  49.2 25.5 %collective-permute-start.13 = (f32[4,128,256]{2,1,0:T(8,128)}, f32[4,128,256]{2,1,0:T(8,128)}, u32[]{:S(2)}, u32[]{:S(2)}) collective-permute-start(f32[4,128,256]{2,1,0:T(8,128)} %collective-permute-done.11.low1), channel_id=1, source_target_pairs={{0,4},{4,0},{8,12},{12,8},{16,20},{20,16},{24,28},{28,24},{1,5},{5... | collective-permute-start | bytes 1572872 | tf_op jit(solution)/shard_map/ppermute | solution.py:321
  67.3 46.9 %collective-permute-start.8 = (f32[12,128,128]{2,1,0:T(8,128)S(1)}, f32[12,128,128]{2,1,0:T(8,128)}, u32[]{:S(2)}, u32[]{:S(2)}) collective-permute-start(f32[12,128,128]{2,1,0:T(8,128)S(1)} %copy-done.2), channel_id=1, source_target_pairs={{2,0},{0,2},{7,5},{5,7},{10,8},{8,10},{15,13},{13,15},{18,16},{16,... | collective-permute-start | bytes 2359304 | tf_op jit(solution)/shard_map/ppermute | solution.py:303
  69.6 1.3 copy-start.7
  69.6 45.8 %collective-permute-start.9 = (f32[12,128,128]{2,1,0:T(8,128)S(1)}, f32[12,128,128]{2,1,0:T(8,128)}, u32[]{:S(2)}, u32[]{:S(2)}) collective-permute-start(f32[12,128,128]{2,1,0:T(8,128)S(1)} %copy-done.2), channel_id=1, source_target_pairs={{3,0},{1,2},{6,5},{4,7},{11,8},{9,10},{14,13},{12,15},{19,16},{17,... | collective-permute-start | bytes 2359304 | tf_op jit(solution)/shard_map/ppermute | solution.py:303
  74.7 40.8 %copy-start.4 = (f32[2,256,256]{2,1,0:T(8,128)S(1)}, f32[2,256,256]{2,1,0:T(8,128)}, u32[]{:S(2)}) copy-start(f32[2,256,256]{2,1,0:T(8,128)} %get-tuple-element.60) | copy-start | bytes 1572868
  74.7 47.9 %copy-start.16 = (f32[128,256]{1,0:T(8,128)S(1)}, f32[128,256]{1,0:T(8,128)}, u32[]{:S(2)}) copy-start(f32[128,256]{1,0:T(8,128)} %get-tuple-element.59) | copy-start | bytes 393220
  77.3 38.8 %collective-permute-start.14 = (f32[3,128,256]{2,1,0:T(8,128)}, f32[3,128,256]{2,1,0:T(8,128)}, u32[]{:S(2)}, u32[]{:S(2)}) collective-permute-start(f32[3,128,256]{2,1,0:T(8,128)} %get-tuple-element.52.refs_4_), channel_id=1, source_target_pairs={{1,0},{3,2},{4,5},{6,7},{9,8},{11,10},{12,13},{14,15},{17,16},{19,... | collective-permute-start | bytes 1179656 | tf_op jit(solution)/shard_map/ppermute | solution.py:303
  78.6 43.9 %collective-permute-start.15 = (f32[3,128,256]{2,1,0:T(8,128)}, f32[3,128,256]{2,1,0:T(8,128)}, u32[]{:S(2)}, u32[]{:S(2)}) collective-permute-start(f32[3,128,256]{2,1,0:T(8,128)} %get-tuple-element.53), channel_id=1, source_target_pairs={{2,0},{0,2},{7,5},{5,7},{10,8},{8,10},{15,13},{13,15},{18,16},{16,... | collective-permute-start | bytes 1179656 | tf_op jit(solution)/shard_map/ppermute | solution.py:303
  83.1 40.8 %copy-start.3 = (f32[12,128,128]{2,1,0:T(8,128)}, f32[12,128,128]{2,1,0:T(8,128)S(1)}, u32[]{:S(2)}) copy-start(f32[12,128,128]{2,1,0:T(8,128)S(1)} %collective-permute-done.7.refs_1_) | copy-start | bytes 2359300
  83.1 40.8 %collective-permute-start.16 = (f32[3,128,256]{2,1,0:T(8,128)}, f32[3,128,256]{2,1,0:T(8,128)S(1)}, u32[]{:S(2)}, u32[]{:S(2)}) collective-permute-start(f32[3,128,256]{2,1,0:T(8,128)} %get-tuple-element.53), channel_id=1, source_target_pairs={{3,0},{1,2},{6,5},{4,7},{11,8},{9,10},{14,13},{12,15},{19,16},{17,... | collective-permute-start | bytes 1179656 | tf_op jit(solution)/shard_map/ppermute | solution.py:303
  114.1 20.0 %collective-permute-start.20 = (f32[256,256]{1,0:T(8,128)}, f32[256,256]{1,0:T(8,128)S(1)}, u32[]{:S(2)}, u32[]{:S(2)}) collective-permute-start(f32[256,256]{1,0:T(8,128)} %get-tuple-element.39.schur), channel_id=1, source_target_pairs={{0,1},{7,6},{8,9},{15,14},{16,17},{23,22},{24,25},{31,30}} | collective-permute-start | bytes 786440 | tf_op jit(solution)/shard_map/ppermute | solution.py:312
  115.4 23.4 %collective-permute-start.23 = (f32[2,256,256]{2,1,0:T(8,128)S(1)}, f32[2,256,256]{2,1,0:T(8,128)S(1)}, u32[]{:S(2)}, u32[]{:S(2)}) collective-permute-start(f32[2,256,256]{2,1,0:T(8,128)S(1)} %copy-done.4), channel_id=1, source_target_pairs={{5,1},{2,6},{13,9},{10,14},{21,17},{18,22},{29,25},{26,30}} | collective-permute-start | bytes 1572872 | tf_op jit(solution)/shard_map/ppermute | solution.py:315
  116.1 21.4 %collective-permute-start.21 = (f32[128,256]{1,0:T(8,128)}, f32[128,256]{1,0:T(8,128)S(1)}, u32[]{:S(2)}, u32[]{:S(2)}) collective-permute-start(f32[128,256]{1,0:T(8,128)} %get-tuple-element.58), channel_id=1, source_target_pairs={{0,1},{7,6},{8,9},{15,14},{16,17},{23,22},{24,25},{31,30}} | collective-permute-start | bytes 393224 | tf_op jit(solution)/shard_map/ppermute | solution.py:312
  122.5 16.3 %collective-permute-start.22 = (f32[128,256]{1,0:T(8,128)S(1)}, f32[128,256]{1,0:T(8,128)S(1)}, u32[]{:S(2)}, u32[]{:S(2)}) collective-permute-start(f32[128,256]{1,0:T(8,128)S(1)} %copy-done.16), channel_id=1, source_target_pairs={{0,1},{7,6},{8,9},{15,14},{16,17},{23,22},{24,25},{31,30}} | collective-permute-start | bytes 393224 | tf_op jit(solution)/shard_map/ppermute | solution.py:312
  123.8 0.8 copy-start.10
  132.8 20.7 %collective-permute-start.17 = (f32[5,64,256]{2,1,0:T(8,128)}, f32[5,64,256]{2,1,0:T(8,128)S(1)}, u32[]{:S(2)}, u32[]{:S(2)}) collective-permute-start(f32[5,64,256]{2,1,0:T(8,128)} %get-tuple-element.55), channel_id=1, source_target_pairs={{0,1},{2,3},{5,4},{7,6},{8,9},{10,11},{13,12},{15,14},{16,17},{18,... | collective-permute-start | bytes 983048 | tf_op jit(solution)/shard_map/ppermute | solution.py:306
  134.1 0.7 copy-start.14
  134.8 18.7 %collective-permute-start.18 = (f32[5,64,256]{2,1,0:T(8,128)}, f32[5,64,256]{2,1,0:T(8,128)S(1)}, u32[]{:S(2)}, u32[]{:S(2)}) collective-permute-start(f32[5,64,256]{2,1,0:T(8,128)} %get-tuple-element.56), channel_id=1, source_target_pairs={{0,2},{2,0},{5,7},{7,5},{8,10},{10,8},{13,15},{15,13},{16,18},{18,... | collective-permute-start | bytes 983048 | tf_op jit(solution)/shard_map/ppermute | solution.py:306
  137.5 1.4 copy-start.17
  137.5 16.0 %collective-permute-start.19 = (f32[5,64,256]{2,1,0:T(8,128)}, f32[5,64,256]{2,1,0:T(8,128)S(1)}, u32[]{:S(2)}, u32[]{:S(2)}) collective-permute-start(f32[5,64,256]{2,1,0:T(8,128)} %get-tuple-element.57), channel_id=1, source_target_pairs={{0,3},{2,1},{5,6},{7,4},{8,11},{10,9},{13,14},{15,12},{16,19},{18,... | collective-permute-start | bytes 983048 | tf_op jit(solution)/shard_map/ppermute | solution.py:306
  138.8 0.7 copy-start.18
  138.9 0.8 copy-start.6
  142.5 10.3 %collective-permute-start.24 = (f32[1,64,256]{2,1,0:T(8,128)}, f32[1,64,256]{2,1,0:T(8,128)S(1)}, u32[]{:S(2)}, u32[]{:S(2)}) collective-permute-start(f32[1,64,256]{2,1,0:T(8,128)} %get-tuple-element.63), channel_id=1, source_target_pairs={{1,0},{6,7},{9,8},{14,15},{17,16},{22,23},{25,24},{30,31}} | collective-permute-start | bytes 196616 | tf_op jit(solution)/shard_map/ppermute | solution.py:318
  143.7 9.7 %collective-permute-start.25 = (f32[1,64,256]{2,1,0:T(8,128)}, f32[1,64,256]{2,1,0:T(8,128)S(1)}, u32[]{:S(2)}, u32[]{:S(2)}) collective-permute-start(f32[1,64,256]{2,1,0:T(8,128)} %get-tuple-element.64), channel_id=1, source_target_pairs={{1,3},{6,4},{9,11},{14,12},{17,19},{22,20},{25,27},{30,28}} | collective-permute-start | bytes 196616 | tf_op jit(solution)/shard_map/ppermute | solution.py:318
  152.8 0.8 copy-start.19
  152.8 0.7 collective-permute-start.26
  153.5 0.6 copy-start.21
  153.5 0.7 copy-start.11
  153.5 0.8 copy-start.12
  153.5 0.9 copy-start.13
  (1 other events, 0.6 us)

commit v6 on v5

--- a/solution.py
+++ b/solution.py
@@ -183,7 +183,7 @@
 
 
 def near_first_kernel(place, count, w_ref, bases, n0, n1, n2, n3, schur, top, low, flipped, pair):
-    result = coupling(w_ref, [tall(n, 0) for n in (n0, n1, n2, n3)], [bases[j ^ 1] for j in range(4)])
+    result = coupling(w_ref, [tall(n, 0) for n in (n0, n1, n2, n3)], [bases[j] for j in range(4)])
     result = jnp.where(count[place[1] >> 1] > 0, result, 0.0)
     half = top.shape[0]
     top[...], low[...] = result[:half], result[half:]
@@ -191,13 +191,17 @@
     flipped[...] = result.T
 
 
+def owns(column):
+    return ((column ^ (column >> 1)) & 1) == 1
+
+
 def near_rest_kernel(place, count, w_ref, schur, first, *refs):
-    row, z = place[0], place[1]
+    z = place[1]
     blocks, named, parts = refs[:4], refs[4:8], refs[8:12]
     flipped, block_buffer, base_buffer, sems = refs[12:]
     total = named[0].shape[0]
 
-    @pl.when((z & 1) == (row & 1))
+    @pl.when(owns(z))
     def _():
         copies = []
         for k in range(total):
@@ -230,7 +234,7 @@
 def finish_kernel(place, *refs):
     row, z = place[0], place[1]
     parts, crown, (diag, near, final) = refs[:4], refs[4:8], refs[8:]
-    owner = (z & 1) == (row & 1)
+    owner = owns(z)
     swap = z >> 1
     for i in range(parts[0].shape[0]):
         here = jnp.where(owner, parts[0][i], parts[1][i])
@@ -241,14 +245,14 @@
             else:
                 near[side, i - 1] = value
     arrived = crown[1][0] + (crown[2][0] + crown[3][0])
-    final[0] = jnp.where(z == 1 + (row & 1), crown[0][0], arrived)
+    final[0] = jnp.where(z == 3 * (row & 1), crown[0][0], arrived)
 
 
 def parent_kernel(place, diag, near0, near1, pair, vt_ref, v_ref, p0, p1, p2, p3, flipped):
     row, z = place[0], place[1]
     size = diag.shape[0]
 
-    @pl.when(z == 1 + (row & 1))
+    @pl.when(z == 3 * (row & 1))
     def _():
         swap = (row & 1) > 0
         near = jnp.concatenate([near0[...], near1[...]], axis=0)
@@ -296,8 +300,8 @@
     row, column = lax.axis_index("row"), lax.axis_index("col")
     place = jnp.stack([row, column]).astype(jnp.int32)
     both = ("row", "col")
-    owned = [(r, z) for r in range(n_row) for z in range(n_col) if z % 2 == r % 2]
-    heads = [(r, 1 + r % 2) for r in range(n_row)]
+    owned = [(r, z) for r in range(n_row) for z in range(1, n_col - 1)]
+    heads = [(r, (n_col - 1) * (r % 2)) for r in range(n_row)]
 
     def to_owner(x, j):
         return lax.ppermute(x, both, [(r * n_col + (z ^ j), r * n_col + z) for r, z in owned])
@@ -306,13 +310,13 @@
         return lax.ppermute(x, both, [(r * n_col + z, r * n_col + (z ^ j)) for r, z in owned])
 
     def from_sibling(x):
-        return lax.ppermute(x, both, [((r ^ 1) * n_col + (z ^ 1), r * n_col + z) for r, z in owned])
+        return lax.ppermute(x, both, [((r ^ 1) * n_col + z, r * n_col + z) for r, z in owned])
 
     def from_neighbour(x):
         return lax.ppermute(x, both, [(r * n_col + (z ^ 1), r * n_col + z) for r, z in heads])
 
-    def from_chip(x):
-        return lax.ppermute(x, both, [((r ^ 1) * n_col + z, r * n_col + z) for r, z in heads])
+    def from_beside(x):
+        return lax.ppermute(x, both, [((r ^ 1) * n_col + (z ^ 1), r * n_col + z) for r, z in heads])
 
     def from_head(x, j):
         return lax.ppermute(x, both, [(r * n_col + z, r * n_col + (z ^ j)) for r, z in heads])
@@ -377,7 +381,7 @@
     )
     top_got = from_neighbour(top)
     low_got = from_neighbour(low)
-    pair_got = from_chip(pair)
+    pair_got = from_beside(pair)
     chosen = call(
         name_kernel,
         [(slots - 1, edge, skeleton)] * 2,

time: 159 us -> 157 us (0.987)
  waiting for transfers between devices: 58.7 us -> 47.2 us
  Pallas kernels: 46 us -> 55.7 us
    ppermute x12, waiting for transfers between devices: 50.3 us -> 30.9 us  [to_owner(): lax.ppermute(x, both, [(r * n_col + (z ^ j), r * n_col + z) for r, z in o...]
    ppermute x3, waiting for transfers between devices: 0.01 us -> 12 us  [from_neighbour(): lax.ppermute(x, both, [(r * n_col + (z ^ 1), r * n_col + z) for r, z in h...]
    pallas_call x9, Pallas kernels: 46 us -> 55.7 us  [call(): pl.pallas_call(kernel, out_shape=shapes, in_specs=specs, out_specs=[vmem]...]
    ppermute x3, waiting for transfers between devices: 8.37 us -> 3.09 us  [from_head(): lax.ppermute(x, both, [(r * n_col + z, r * n_col + (z ^ j)) for r, z in h...]
    ppermute x12, starting transfers between devices: 26.5 us -> 29 us  [to_owner(): lax.ppermute(x, both, [(r * n_col + (z ^ j), r * n_col + z) for r, z in o...]
    ppermute x3, starting transfers between devices: 5.27 us -> 3.24 us  [from_owner(): lax.ppermute(x, both, [(r * n_col + z, r * n_col + (z ^ j)) for r, z in o...]
  transfers between devices with their start and end apart: 27 -> 27, of which waited for: 5 -> 11; matrix products, arithmetic and copies ran while one was open for 1% -> 1% of each run, Pallas kernels for 26% -> 33%
where the time goes in v6:
time: 157 us; the launch traced here: 155 us
  Pallas kernels  55.7 us (35%)
  waiting for transfers between devices  47.2 us (30%)
  starting transfers between devices  46.6 us (30%)
  local copies, waits for them, and re-layouts  4.3 us (3%)
    pallas_call x9, Pallas kernels, call(): pl.pallas_call(kernel, out_shape=shapes, in_specs=specs, out_specs=[vmem]...  55.7 us
    ppermute x12, waiting for transfers between devices, to_owner(): lax.ppermute(x, both, [(r * n_col + (z ^ j), r * n_col + z) for r, z in o...  30.9 us
    ppermute x12, starting transfers between devices, to_owner(): lax.ppermute(x, both, [(r * n_col + (z ^ j), r * n_col + z) for r, z in o...  29 us
    ppermute x3, waiting for transfers between devices, from_neighbour(): lax.ppermute(x, both, [(r * n_col + (z ^ 1), r * n_col + z) for r, z in h...  12 us
    ppermute x4, starting transfers between devices, across(): return lax.ppermute(x, 'row', [(r, r ^ bit) for r in range(n_row)])  4.63 us
    unnamed x45, local copies, waits for them, and re-layouts  4.28 us
    ppermute x3, starting transfers between devices, from_head(): lax.ppermute(x, both, [(r * n_col + z, r * n_col + (z ^ j)) for r, z in h...  3.85 us
    ppermute x3, starting transfers between devices, from_neighbour(): lax.ppermute(x, both, [(r * n_col + (z ^ 1), r * n_col + z) for r, z in h...  3.84 us
  transfers between devices with their start and end apart: 27, of which 11 were waited for; matrix products, arithmetic and copies ran while one was open for 1% of the time, Pallas kernels for 33%

profile of v6, /device:TPU:0, one launch (start us, length us, event | category | flops | bytes accessed | tf_op | source)
XLA Modules:
  0.0 155.4 jit_solution(17433118243587385320)
XLA Ops:
  1.3 2.3 %shard_map.85 = (f32[8,128,128]{2,1,0:T(8,128)}, f32[6,128,128]{2,1,0:T(8,128)}, f32[2,128,256]{2,1,0:T(8,128)}) custom-call(s32[2]{0:T(128)} %pad_add_fusion.place, f32[2,512,128]{2,1,0:T(8,128)} %diag.1, f32[2,128,512]{2,1,0:T(8,128)} %bases.1), custom_call_target="tpu_custom_call" | custom-call | flops 2000000000 | bytes 2000000 | tf_op jit(solution)/shard_map/pallas_call | solution.py:279
  3.6 3.0 %collective-permute-start.10 = (f32[2,128,256]{2,1,0:T(8,128)}, f32[2,128,256]{2,1,0:T(8,128)S(1)}, u32[]{:S(2)}, u32[]{:S(2)}) collective-permute-start(f32[2,128,256]{2,1,0:T(8,128)} %get-tuple-element.49), channel_id=1, source_target_pairs={{0,8},{4,12},{8,0},{12,4},{16,24},{20,28},{24,16},{28,20},{1,9},{5... | collective-permute-start | bytes 786440 | tf_op jit(solution)/shard_map/ppermute | solution.py:325
  6.5 3.5 %collective-permute-start = (f32[8,128,128]{2,1,0:T(8,128)}, f32[8,128,128]{2,1,0:T(8,128)S(1)}, u32[]{:S(2)}, u32[]{:S(2)}) collective-permute-start(f32[8,128,128]{2,1,0:T(8,128)} %get-tuple-element.36.own), channel_id=1, source_target_pairs={{0,1},{3,2},{4,5},{7,6},{8,9},{11,10},{12,13},{15,14},{16,17},{19,... | collective-permute-start | bytes 1572872 | tf_op jit(solution)/shard_map/ppermute | solution.py:307
  10.0 2.3 %collective-permute-start.1 = (f32[6,128,128]{2,1,0:T(8,128)}, f32[6,128,128]{2,1,0:T(8,128)S(1)}, u32[]{:S(2)}, u32[]{:S(2)}) collective-permute-start(f32[6,128,128]{2,1,0:T(8,128)} %get-tuple-element.37), channel_id=1, source_target_pairs={{3,1},{0,2},{7,5},{4,6},{11,9},{8,10},{15,13},{12,14},{19,17},{16,... | collective-permute-start | bytes 1179656 | tf_op jit(solution)/shard_map/ppermute | solution.py:307
  12.3 0.7 collective-permute-start.2
  13.0 1.0 constant_dynamic-update-slice_fusion.1
  14.0 1.6 %collective-permute-start.11 = (f32[4,128,256]{2,1,0:T(8,128)S(1)}, f32[4,128,256]{2,1,0:T(8,128)}, u32[]{:S(2)}, u32[]{:S(2)}) collective-permute-start(f32[4,128,256]{2,1,0:T(8,128)S(1)} %constant_dynamic-update-slice_fusion.low0), channel_id=1, source_target_pairs={{0,16},{4,20},{8,24},{12,28},{16,0},{20,4},{24,8},{28,12},{1,17},{... | collective-permute-start | bytes 1572872 | tf_op jit(solution)/shard_map/ppermute | solution.py:325
  15.6 3.8 %shard_map.88 = (f32[4,128,128]{2,1,0:T(8,128)}, f32[4,128,128]{2,1,0:T(8,128)}, f32[12,128,128]{2,1,0:T(8,128)}, f32[12,128,128]{2,1,0:T(8,128)}, f32[512,512]{1,0:T(8,128)}) custom-call(s32[2]{0:T(128)} %pad_add_fusion.place, f32[2,16,128,128]{3,2,1,0:T(8,128)} %bitcast.7, f32[512,512]{1,0:T(8,128)} %bitcast.8), custom_call_target="tpu_custom_call" | custom-call | flops 2000000000 | bytes 2000000 | tf_op jit(solution)/shard_map/pallas_call | solution.py:279
  19.5 10.2 %collective-permute-done.1.far2 = f32[6,128,128]{2,1,0:T(8,128)S(1)} collective-permute-done((f32[6,128,128]{2,1,0:T(8,128)}, f32[6,128,128]{2,1,0:T(8,128)S(1)}, u32[]{:S(2)}, u32[]{:S(2)}) %collective-permute-start.1) | collective-permute-done | bytes 393248 | tf_op jit(solution)/shard_map/ppermute | solution.py:307
  29.6 5.3 %collective-permute-start.4 = (f32[4,128,128]{2,1,0:T(8,128)}, f32[4,128,128]{2,1,0:T(8,128)S(1)}, u32[]{:S(2)}, u32[]{:S(2)}) collective-permute-start(f32[4,128,128]{2,1,0:T(8,128)} %get-tuple-element.42.n0), channel_id=1, source_target_pairs={{0,1},{3,2},{4,5},{7,6},{8,9},{11,10},{12,13},{15,14},{16,17},{19,... | collective-permute-start | bytes 786440 | tf_op jit(solution)/shard_map/ppermute | solution.py:307
  35.0 2.0 %collective-permute-start.5 = (f32[4,128,128]{2,1,0:T(8,128)}, f32[4,128,128]{2,1,0:T(8,128)}, u32[]{:S(2)}, u32[]{:S(2)}) collective-permute-start(f32[4,128,128]{2,1,0:T(8,128)} %get-tuple-element.43), channel_id=1, source_target_pairs={{3,1},{0,2},{7,5},{4,6},{11,9},{8,10},{15,13},{12,14},{19,17},{16,... | collective-permute-start | bytes 786440 | tf_op jit(solution)/shard_map/ppermute | solution.py:307
  37.0 1.4 collective-permute-start.6
  38.3 2.4 %shard_map.87 = f32[4,128,256]{2,1,0:T(8,128)} custom-call(s32[2]{0:T(128)} %pad_add_fusion.place, f32[8,128,128]{2,1,0:T(8,128)} %get-tuple-element.36.own, f32[8,128,128]{2,1,0:T(8,128)} %copy-done.5, f32[6,128,128]{2,1,0:T(8,128)} %copy-done.8, f32[6,128,128]{2,1,0:T(8,128)} %copy-done.9), custom_call_target="tpu_custom_call" | custom-call | flops 2000000000 | bytes 2000000 | tf_op jit(solution)/shard_map/pallas_call | solution.py:279
  40.7 1.2 collective-permute-done.4.n1
  41.9 0.7 collective-permute-start.3
  42.7 2.7 %collective-permute-done.5.n2 = f32[4,128,128]{2,1,0:T(8,128)} collective-permute-done((f32[4,128,128]{2,1,0:T(8,128)}, f32[4,128,128]{2,1,0:T(8,128)}, u32[]{:S(2)}, u32[]{:S(2)}) %collective-permute-start.5) | collective-permute-done | bytes 262176 | tf_op jit(solution)/shard_map/ppermute | solution.py:307
  45.3 4.4 %collective-permute-start.7 = (f32[12,128,128]{2,1,0:T(8,128)S(1)}, f32[12,128,128]{2,1,0:T(8,128)S(1)}, u32[]{:S(2)}, u32[]{:S(2)}) collective-permute-start(f32[12,128,128]{2,1,0:T(8,128)S(1)} %copy-done.1), channel_id=1, source_target_pairs={{0,1},{3,2},{4,5},{7,6},{8,9},{11,10},{12,13},{15,14},{16,17},{19,... | collective-permute-start | bytes 2359304 | tf_op jit(solution)/shard_map/ppermute | solution.py:307
  49.8 18.0 %shard_map.86 = (f32[4,256,128]{2,1,0:T(8,128)}, f32[256,256]{1,0:T(8,128)}) custom-call(s32[2]{0:T(128)} %pad_add_fusion.place, f32[8,128,128]{2,1,0:T(8,128)} %get-tuple-element.36.own, f32[8,128,128]{2,1,0:T(8,128)} %copy-done.5, f32[6,128,128]{2,1,0:T(8,128)} %copy-done.8, f32[6,128,128]{2,1,0:T(8,128)} %copy-done.9), custom_call_target="tpu_custom_call" | custom-call | flops 22000001024 | bytes 22000000 | tf_op jit(solution)/shard_map/pallas_call | solution.py:279
  67.8 3.1 %collective-permute-start.8 = (f32[12,128,128]{2,1,0:T(8,128)S(1)}, f32[12,128,128]{2,1,0:T(8,128)}, u32[]{:S(2)}, u32[]{:S(2)}) collective-permute-start(f32[12,128,128]{2,1,0:T(8,128)S(1)} %copy-done.2), channel_id=1, source_target_pairs={{3,1},{0,2},{7,5},{4,6},{11,9},{8,10},{15,13},{12,14},{19,17},{16,... | collective-permute-start | bytes 2359304 | tf_op jit(solution)/shard_map/ppermute | solution.py:307
  71.0 1.6 %collective-permute-start.9 = (f32[12,128,128]{2,1,0:T(8,128)S(1)}, f32[12,128,128]{2,1,0:T(8,128)}, u32[]{:S(2)}, u32[]{:S(2)}) collective-permute-start(f32[12,128,128]{2,1,0:T(8,128)S(1)} %copy-done.2), channel_id=1, source_target_pairs={{2,1},{1,2},{6,5},{5,6},{10,9},{9,10},{14,13},{13,14},{18,17},{17,... | collective-permute-start | bytes 2359304 | tf_op jit(solution)/shard_map/ppermute | solution.py:307
  72.5 3.7 %shard_map.89 = (f32[128,256]{1,0:T(8,128)}, f32[128,256]{1,0:T(8,128)}, f32[256,256]{1,0:T(8,128)}, f32[2,256,256]{2,1,0:T(8,128)}) custom-call(s32[2]{0:T(128)} %pad_add_fusion.place, s32[2]{0:T(128)} %count.3, f32[4,256,128]{2,1,0:T(8,128)} %get-tuple-element.38.w_ref, f32[4,128,256]{2,1,0:T(8,128)} %copy-done.7, f32[4,128,128]{2,1,0:T(8,128)} %get-tuple-element.42.n0, ...), custom_call_target="tpu_custom_call" | custom-call | flops 4000000000 | bytes 4000000 | tf_op jit(solution)/shard_map/pallas_call | solution.py:279
  76.3 2.6 %shard_map.90 = (f32[3,128,256]{2,1,0:T(8,128)}, f32[3,128,256]{2,1,0:T(8,128)}) custom-call(s32[2]{0:T(128)} %pad_add_fusion.place, s32[2,4]{1,0:T(2,128)} %ids.1, f32[4,128,256]{2,1,0:T(8,128)} %copy-done, f32[4,128,256]{2,1,0:T(8,128)} %collective-permute-done.11.low1, f32[4,128,256]{2,1,0:T(8,128)} %collective-permute-done.12.high0, ...), custom_call_target="tpu_custom_call" | custom-call | flops 2000000000 | bytes 2000000 | tf_op jit(solution)/shard_map/pallas_call | solution.py:279
  78.9 2.1 %collective-permute-start.14 = (f32[3,128,256]{2,1,0:T(8,128)}, f32[3,128,256]{2,1,0:T(8,128)}, u32[]{:S(2)}, u32[]{:S(2)}) collective-permute-start(f32[3,128,256]{2,1,0:T(8,128)} %get-tuple-element.52.refs_4_), channel_id=1, source_target_pairs={{0,1},{3,2},{4,5},{7,6},{8,9},{11,10},{12,13},{15,14},{16,17},{19,... | collective-permute-start | bytes 1179656 | tf_op jit(solution)/shard_map/ppermute | solution.py:307
  81.1 2.1 %collective-permute-start.15 = (f32[3,128,256]{2,1,0:T(8,128)}, f32[3,128,256]{2,1,0:T(8,128)}, u32[]{:S(2)}, u32[]{:S(2)}) collective-permute-start(f32[3,128,256]{2,1,0:T(8,128)} %get-tuple-element.53), channel_id=1, source_target_pairs={{3,1},{0,2},{7,5},{4,6},{11,9},{8,10},{15,13},{12,14},{19,17},{16,... | collective-permute-start | bytes 1179656 | tf_op jit(solution)/shard_map/ppermute | solution.py:307
  83.1 0.7 collective-permute-start.16
  83.8 4.2 %collective-permute-done.8.refs_2_ = f32[12,128,128]{2,1,0:T(8,128)} collective-permute-done((f32[12,128,128]{2,1,0:T(8,128)S(1)}, f32[12,128,128]{2,1,0:T(8,128)}, u32[]{:S(2)}, u32[]{:S(2)}) %collective-permute-start.8) | collective-permute-done | bytes 786464 | tf_op jit(solution)/shard_map/ppermute | solution.py:307
  88.0 1.3 collective-permute-start.20
  89.3 1.3 collective-permute-start.23
  90.6 5.9 %collective-permute-done.14.refs_5_ = f32[3,128,256]{2,1,0:T(8,128)} collective-permute-done((f32[3,128,256]{2,1,0:T(8,128)}, f32[3,128,256]{2,1,0:T(8,128)}, u32[]{:S(2)}, u32[]{:S(2)}) %collective-permute-start.14) | collective-permute-done | bytes 393248 | tf_op jit(solution)/shard_map/ppermute | solution.py:307
  96.6 1.3 collective-permute-start.21
  97.9 6.7 %collective-permute-done.15.refs_6_ = f32[3,128,256]{2,1,0:T(8,128)} collective-permute-done((f32[3,128,256]{2,1,0:T(8,128)}, f32[3,128,256]{2,1,0:T(8,128)}, u32[]{:S(2)}, u32[]{:S(2)}) %collective-permute-start.15) | collective-permute-done | bytes 393248 | tf_op jit(solution)/shard_map/ppermute | solution.py:307
  104.6 1.3 collective-permute-start.22
  105.9 0.8 copy-done.10
  106.7 2.5 %shard_map.91 = (f32[5,64,256]{2,1,0:T(8,128)}, f32[5,64,256]{2,1,0:T(8,128)}, f32[5,64,256]{2,1,0:T(8,128)}, f32[5,64,256]{2,1,0:T(8,128)}) custom-call(s32[2]{0:T(128)} %pad_add_fusion.place, s32[2]{0:T(128)} %count.3, f32[4,256,128]{2,1,0:T(8,128)} %get-tuple-element.38.w_ref, f32[256,256]{1,0:T(8,128)} %get-tuple-element.39.schur, ...), custom_call_target="tpu_custom_call" | custom-call | flops 7000000000 | bytes 7000000 | tf_op jit(solution)/shard_map/pallas_call | solution.py:279
  109.1 1.3 collective-permute-start.17
  110.5 0.7 copy-done.14
  111.2 1.3 collective-permute-start.18
  112.4 9.9 %collective-permute-done.21.near0 = f32[128,256]{1,0:T(8,128)S(1)} collective-permute-done((f32[128,256]{1,0:T(8,128)}, f32[128,256]{1,0:T(8,128)S(1)}, u32[]{:S(2)}, u32[]{:S(2)}) %collective-permute-start.21) | collective-permute-done | bytes 131104 | tf_op jit(solution)/shard_map/ppermute | solution.py:316
  123.0 2.1 %collective-permute-done.22.near1 = f32[128,256]{1,0:T(8,128)S(1)} collective-permute-done((f32[128,256]{1,0:T(8,128)S(1)}, f32[128,256]{1,0:T(8,128)S(1)}, u32[]{:S(2)}, u32[]{:S(2)}) %collective-permute-start.22) | collective-permute-done | bytes 131104 | tf_op jit(solution)/shard_map/ppermute | solution.py:316
  125.2 1.1 collective-permute-done.23.pair
  126.3 0.8 copy-done.6
  127.0 18.1 %shard_map.92 = (f32[1,64,256]{2,1,0:T(8,128)}, f32[1,64,256]{2,1,0:T(8,128)}, f32[1,64,256]{2,1,0:T(8,128)}, f32[1,64,256]{2,1,0:T(8,128)}) custom-call(s32[2]{0:T(128)} %pad_add_fusion.place, f32[256,256]{1,0:T(8,128)} %copy-done.14, f32[128,256]{1,0:T(8,128)} %copy-done.17, f32[128,256]{1,0:T(8,128)} %copy-done.18, f32[2,256,256]{2,1,0:T(8,128)} %copy-done.6, ...), custom_call_target="tpu_custom_call" | custom-call | flops 20000000000 | bytes 20000000 | tf_op jit(solution)/shard_map/pallas_call | solution.py:279
  145.2 1.3 collective-permute-start.24
  146.5 1.3 collective-permute-start.25
  147.8 0.9 collective-permute-done.24.refs_5_
  148.7 1.3 collective-permute-start.26
  150.0 2.2 %collective-permute-done.26.refs_7_ = f32[1,64,256]{2,1,0:T(8,128)S(1)} collective-permute-done((f32[1,64,256]{2,1,0:T(8,128)}, f32[1,64,256]{2,1,0:T(8,128)S(1)}, u32[]{:S(2)}, u32[]{:S(2)}) %collective-permute-start.26) | collective-permute-done | bytes 65568 | tf_op jit(solution)/shard_map/ppermute | solution.py:322
  153.1 2.2 %shard_map.93 = (f32[2,64,256]{2,1,0:T(8,128)}, f32[2,4,64,256]{3,2,1,0:T(8,128)}, f32[1,64,256]{2,1,0:T(8,128)}) custom-call(s32[2]{0:T(128)} %pad_add_fusion.place, f32[5,64,256]{2,1,0:T(8,128)} %get-tuple-element.54.refs_0_, f32[5,64,256]{2,1,0:T(8,128)} %copy-done.11, f32[5,64,256]{2,1,0:T(8,128)} %copy-done.12, f32[5,64,256]{2,1,0:T(8,128)} %copy-done.13, ...), custom_call_target="tpu_custom_call" | custom-call | flops 2000000000 | bytes 2000000 | tf_op jit(solution)/shard_map/pallas_call | solution.py:279
  (62 shorter events, 2.5 us)
Async XLA Ops:
  3.6 10.4 %collective-permute-start.10 = (f32[2,128,256]{2,1,0:T(8,128)}, f32[2,128,256]{2,1,0:T(8,128)S(1)}, u32[]{:S(2)}, u32[]{:S(2)}) collective-permute-start(f32[2,128,256]{2,1,0:T(8,128)} %get-tuple-element.49), channel_id=1, source_target_pairs={{0,8},{4,12},{8,0},{12,4},{16,24},{20,28},{24,16},{28,20},{1,9},{5... | collective-permute-start | bytes 786440 | tf_op jit(solution)/shard_map/ppermute | solution.py:325
  6.5 23.1 %collective-permute-start = (f32[8,128,128]{2,1,0:T(8,128)}, f32[8,128,128]{2,1,0:T(8,128)S(1)}, u32[]{:S(2)}, u32[]{:S(2)}) collective-permute-start(f32[8,128,128]{2,1,0:T(8,128)} %get-tuple-element.36.own), channel_id=1, source_target_pairs={{0,1},{3,2},{4,5},{7,6},{8,9},{11,10},{12,13},{15,14},{16,17},{19,... | collective-permute-start | bytes 1572872 | tf_op jit(solution)/shard_map/ppermute | solution.py:307
  10.0 19.6 %collective-permute-start.1 = (f32[6,128,128]{2,1,0:T(8,128)}, f32[6,128,128]{2,1,0:T(8,128)S(1)}, u32[]{:S(2)}, u32[]{:S(2)}) collective-permute-start(f32[6,128,128]{2,1,0:T(8,128)} %get-tuple-element.37), channel_id=1, source_target_pairs={{3,1},{0,2},{7,5},{4,6},{11,9},{8,10},{15,13},{12,14},{19,17},{16,... | collective-permute-start | bytes 1179656 | tf_op jit(solution)/shard_map/ppermute | solution.py:307
  12.3 17.3 %collective-permute-start.2 = (f32[6,128,128]{2,1,0:T(8,128)}, f32[6,128,128]{2,1,0:T(8,128)S(1)}, u32[]{:S(2)}, u32[]{:S(2)}) collective-permute-start(f32[6,128,128]{2,1,0:T(8,128)} %get-tuple-element.37), channel_id=1, source_target_pairs={{2,1},{1,2},{6,5},{5,6},{10,9},{9,10},{14,13},{13,14},{18,17},{17,... | collective-permute-start | bytes 1179656 | tf_op jit(solution)/shard_map/ppermute | solution.py:307
  14.0 22.9 %copy-start = (f32[4,128,256]{2,1,0:T(8,128)}, f32[4,128,256]{2,1,0:T(8,128)S(1)}, u32[]{:S(2)}) copy-start(f32[4,128,256]{2,1,0:T(8,128)S(1)} %constant_dynamic-update-slice_fusion.low0) | copy-start | bytes 1572868
  14.0 35.7 %collective-permute-start.11 = (f32[4,128,256]{2,1,0:T(8,128)S(1)}, f32[4,128,256]{2,1,0:T(8,128)}, u32[]{:S(2)}, u32[]{:S(2)}) collective-permute-start(f32[4,128,256]{2,1,0:T(8,128)S(1)} %constant_dynamic-update-slice_fusion.low0), channel_id=1, source_target_pairs={{0,16},{4,20},{8,24},{12,28},{16,0},{20,4},{24,8},{28,12},{1,17},{... | collective-permute-start | bytes 1572872 | tf_op jit(solution)/shard_map/ppermute | solution.py:325
  29.6 8.7 %copy-start.8 = (f32[6,128,128]{2,1,0:T(8,128)}, f32[6,128,128]{2,1,0:T(8,128)S(1)}, u32[]{:S(2)}) copy-start(f32[6,128,128]{2,1,0:T(8,128)S(1)} %collective-permute-done.1.far2) | copy-start | bytes 1179652
  29.6 8.7 %copy-start.9 = (f32[6,128,128]{2,1,0:T(8,128)}, f32[6,128,128]{2,1,0:T(8,128)S(1)}, u32[]{:S(2)}) copy-start(f32[6,128,128]{2,1,0:T(8,128)S(1)} %collective-permute-done.2.far3) | copy-start | bytes 1179652
  29.6 8.7 %copy-start.5 = (f32[8,128,128]{2,1,0:T(8,128)}, f32[8,128,128]{2,1,0:T(8,128)S(1)}, u32[]{:S(2)}) copy-start(f32[8,128,128]{2,1,0:T(8,128)S(1)} %collective-permute-done.near) | copy-start | bytes 1572868
  29.6 12.3 %collective-permute-start.4 = (f32[4,128,128]{2,1,0:T(8,128)}, f32[4,128,128]{2,1,0:T(8,128)S(1)}, u32[]{:S(2)}, u32[]{:S(2)}) collective-permute-start(f32[4,128,128]{2,1,0:T(8,128)} %get-tuple-element.42.n0), channel_id=1, source_target_pairs={{0,1},{3,2},{4,5},{7,6},{8,9},{11,10},{12,13},{15,14},{16,17},{19,... | collective-permute-start | bytes 786440 | tf_op jit(solution)/shard_map/ppermute | solution.py:307
  35.0 10.4 %collective-permute-start.5 = (f32[4,128,128]{2,1,0:T(8,128)}, f32[4,128,128]{2,1,0:T(8,128)}, u32[]{:S(2)}, u32[]{:S(2)}) collective-permute-start(f32[4,128,128]{2,1,0:T(8,128)} %get-tuple-element.43), channel_id=1, source_target_pairs={{3,1},{0,2},{7,5},{4,6},{11,9},{8,10},{15,13},{12,14},{19,17},{16,... | collective-permute-start | bytes 786440 | tf_op jit(solution)/shard_map/ppermute | solution.py:307
  37.0 39.3 %collective-permute-start.12 = (f32[4,128,256]{2,1,0:T(8,128)S(1)}, f32[4,128,256]{2,1,0:T(8,128)}, u32[]{:S(2)}, u32[]{:S(2)}) collective-permute-start(f32[4,128,256]{2,1,0:T(8,128)S(1)} %constant_dynamic-update-slice_fusion.low0), channel_id=1, source_target_pairs={{0,4},{4,0},{8,12},{12,8},{16,20},{20,16},{24,28},{28,24},{1,5},{5... | collective-permute-start | bytes 1572872 | tf_op jit(solution)/shard_map/ppermute | solution.py:325
  37.0 30.8 %collective-permute-start.6 = (f32[4,128,128]{2,1,0:T(8,128)}, f32[4,128,128]{2,1,0:T(8,128)}, u32[]{:S(2)}, u32[]{:S(2)}) collective-permute-start(f32[4,128,128]{2,1,0:T(8,128)} %get-tuple-element.43), channel_id=1, source_target_pairs={{2,1},{1,2},{6,5},{5,6},{10,9},{9,10},{14,13},{13,14},{18,17},{17,... | collective-permute-start | bytes 786440 | tf_op jit(solution)/shard_map/ppermute | solution.py:307
  38.3 7.0 %copy-start.1 = (f32[12,128,128]{2,1,0:T(8,128)S(1)}, f32[12,128,128]{2,1,0:T(8,128)}, u32[]{:S(2)}) copy-start(f32[12,128,128]{2,1,0:T(8,128)} %get-tuple-element.47.refs_0_) | copy-start | bytes 2359300
  40.7 27.1 %copy-start.2 = (f32[12,128,128]{2,1,0:T(8,128)S(1)}, f32[12,128,128]{2,1,0:T(8,128)}, u32[]{:S(2)}) copy-start(f32[12,128,128]{2,1,0:T(8,128)} %get-tuple-element.48) | copy-start | bytes 2359300
  41.9 0.7 copy-start.15
  41.9 29.0 %collective-permute-start.3 = (f32[4,128,256]{2,1,0:T(8,128)}, f32[4,128,256]{2,1,0:T(8,128)S(1)}, u32[]{:S(2)}, u32[]{:S(2)}) collective-permute-start(f32[4,128,256]{2,1,0:T(8,128)} %shard_map.87), channel_id=1, source_target_pairs={{5,1},{6,2},{1,5},{2,6},{13,9},{14,10},{9,13},{10,14},{21,17},{22,... | collective-permute-start | bytes 1572872 | tf_op jit(solution)/shard_map/ppermute | solution.py:313
  45.3 37.8 %collective-permute-start.7 = (f32[12,128,128]{2,1,0:T(8,128)S(1)}, f32[12,128,128]{2,1,0:T(8,128)S(1)}, u32[]{:S(2)}, u32[]{:S(2)}) collective-permute-start(f32[12,128,128]{2,1,0:T(8,128)S(1)} %copy-done.1), channel_id=1, source_target_pairs={{0,1},{3,2},{4,5},{7,6},{8,9},{11,10},{12,13},{15,14},{16,17},{19,... | collective-permute-start | bytes 2359304 | tf_op jit(solution)/shard_map/ppermute | solution.py:307
  49.7 26.6 %collective-permute-start.13 = (f32[4,128,256]{2,1,0:T(8,128)}, f32[4,128,256]{2,1,0:T(8,128)}, u32[]{:S(2)}, u32[]{:S(2)}) collective-permute-start(f32[4,128,256]{2,1,0:T(8,128)} %collective-permute-done.11.low1), channel_id=1, source_target_pairs={{0,4},{4,0},{8,12},{12,8},{16,20},{20,16},{24,28},{28,24},{1,5},{5... | collective-permute-start | bytes 1572872 | tf_op jit(solution)/shard_map/ppermute | solution.py:325
  67.8 20.2 %collective-permute-start.8 = (f32[12,128,128]{2,1,0:T(8,128)S(1)}, f32[12,128,128]{2,1,0:T(8,128)}, u32[]{:S(2)}, u32[]{:S(2)}) collective-permute-start(f32[12,128,128]{2,1,0:T(8,128)S(1)} %copy-done.2), channel_id=1, source_target_pairs={{3,1},{0,2},{7,5},{4,6},{11,9},{8,10},{15,13},{12,14},{19,17},{16,... | collective-permute-start | bytes 2359304 | tf_op jit(solution)/shard_map/ppermute | solution.py:307
  71.0 1.6 %copy-start.7 = (f32[4,128,256]{2,1,0:T(8,128)}, f32[4,128,256]{2,1,0:T(8,128)S(1)}, u32[]{:S(2)}) copy-start(f32[4,128,256]{2,1,0:T(8,128)S(1)} %collective-permute-done.3.bases) | copy-start | bytes 1572868
  71.0 18.4 %collective-permute-start.9 = (f32[12,128,128]{2,1,0:T(8,128)S(1)}, f32[12,128,128]{2,1,0:T(8,128)}, u32[]{:S(2)}, u32[]{:S(2)}) collective-permute-start(f32[12,128,128]{2,1,0:T(8,128)S(1)} %copy-done.2), channel_id=1, source_target_pairs={{2,1},{1,2},{6,5},{5,6},{10,9},{9,10},{14,13},{13,14},{18,17},{17,... | collective-permute-start | bytes 2359304 | tf_op jit(solution)/shard_map/ppermute | solution.py:307
  76.3 13.1 %copy-start.4 = (f32[2,256,256]{2,1,0:T(8,128)S(1)}, f32[2,256,256]{2,1,0:T(8,128)}, u32[]{:S(2)}) copy-start(f32[2,256,256]{2,1,0:T(8,128)} %get-tuple-element.60) | copy-start | bytes 1572868
  76.3 28.3 %copy-start.16 = (f32[128,256]{1,0:T(8,128)S(1)}, f32[128,256]{1,0:T(8,128)}, u32[]{:S(2)}) copy-start(f32[128,256]{1,0:T(8,128)} %get-tuple-element.59) | copy-start | bytes 393220
  78.9 17.6 %collective-permute-start.14 = (f32[3,128,256]{2,1,0:T(8,128)}, f32[3,128,256]{2,1,0:T(8,128)}, u32[]{:S(2)}, u32[]{:S(2)}) collective-permute-start(f32[3,128,256]{2,1,0:T(8,128)} %get-tuple-element.52.refs_4_), channel_id=1, source_target_pairs={{0,1},{3,2},{4,5},{7,6},{8,9},{11,10},{12,13},{15,14},{16,17},{19,... | collective-permute-start | bytes 1179656 | tf_op jit(solution)/shard_map/ppermute | solution.py:307
  81.1 23.5 %collective-permute-start.15 = (f32[3,128,256]{2,1,0:T(8,128)}, f32[3,128,256]{2,1,0:T(8,128)}, u32[]{:S(2)}, u32[]{:S(2)}) collective-permute-start(f32[3,128,256]{2,1,0:T(8,128)} %get-tuple-element.53), channel_id=1, source_target_pairs={{3,1},{0,2},{7,5},{4,6},{11,9},{8,10},{15,13},{12,14},{19,17},{16,... | collective-permute-start | bytes 1179656 | tf_op jit(solution)/shard_map/ppermute | solution.py:307
  83.1 22.8 %copy-start.3 = (f32[12,128,128]{2,1,0:T(8,128)}, f32[12,128,128]{2,1,0:T(8,128)S(1)}, u32[]{:S(2)}) copy-start(f32[12,128,128]{2,1,0:T(8,128)S(1)} %collective-permute-done.7.refs_1_) | copy-start | bytes 2359300
  83.1 22.7 %collective-permute-start.16 = (f32[3,128,256]{2,1,0:T(8,128)}, f32[3,128,256]{2,1,0:T(8,128)S(1)}, u32[]{:S(2)}, u32[]{:S(2)}) collective-permute-start(f32[3,128,256]{2,1,0:T(8,128)} %get-tuple-element.53), channel_id=1, source_target_pairs={{2,1},{1,2},{6,5},{5,6},{10,9},{9,10},{14,13},{13,14},{18,17},{17,... | collective-permute-start | bytes 1179656 | tf_op jit(solution)/shard_map/ppermute | solution.py:307
  88.0 22.4 %collective-permute-start.20 = (f32[256,256]{1,0:T(8,128)}, f32[256,256]{1,0:T(8,128)S(1)}, u32[]{:S(2)}, u32[]{:S(2)}) collective-permute-start(f32[256,256]{1,0:T(8,128)} %get-tuple-element.39.schur), channel_id=1, source_target_pairs={{1,0},{6,7},{9,8},{14,15},{17,16},{22,23},{25,24},{30,31}} | collective-permute-start | bytes 786440 | tf_op jit(solution)/shard_map/ppermute | solution.py:316
  89.3 36.9 %collective-permute-start.23 = (f32[2,256,256]{2,1,0:T(8,128)S(1)}, f32[2,256,256]{2,1,0:T(8,128)S(1)}, u32[]{:S(2)}, u32[]{:S(2)}) collective-permute-start(f32[2,256,256]{2,1,0:T(8,128)S(1)} %copy-done.4), channel_id=1, source_target_pairs={{5,0},{2,7},{13,8},{10,15},{21,16},{18,23},{29,24},{26,31}} | collective-permute-start | bytes 1572872 | tf_op jit(solution)/shard_map/ppermute | solution.py:319
  96.6 25.8 %collective-permute-start.21 = (f32[128,256]{1,0:T(8,128)}, f32[128,256]{1,0:T(8,128)S(1)}, u32[]{:S(2)}, u32[]{:S(2)}) collective-permute-start(f32[128,256]{1,0:T(8,128)} %get-tuple-element.58), channel_id=1, source_target_pairs={{1,0},{6,7},{9,8},{14,15},{17,16},{22,23},{25,24},{30,31}} | collective-permute-start | bytes 393224 | tf_op jit(solution)/shard_map/ppermute | solution.py:316
  104.6 20.6 %collective-permute-start.22 = (f32[128,256]{1,0:T(8,128)S(1)}, f32[128,256]{1,0:T(8,128)S(1)}, u32[]{:S(2)}, u32[]{:S(2)}) collective-permute-start(f32[128,256]{1,0:T(8,128)S(1)} %copy-done.16), channel_id=1, source_target_pairs={{1,0},{6,7},{9,8},{14,15},{17,16},{22,23},{25,24},{30,31}} | collective-permute-start | bytes 393224 | tf_op jit(solution)/shard_map/ppermute | solution.py:316
  105.9 0.8 copy-start.10
  109.1 43.0 %collective-permute-start.17 = (f32[5,64,256]{2,1,0:T(8,128)}, f32[5,64,256]{2,1,0:T(8,128)S(1)}, u32[]{:S(2)}, u32[]{:S(2)}) collective-permute-start(f32[5,64,256]{2,1,0:T(8,128)} %get-tuple-element.55), channel_id=1, source_target_pairs={{1,0},{2,3},{5,4},{6,7},{9,8},{10,11},{13,12},{14,15},{17,16},{18,... | collective-permute-start | bytes 983048 | tf_op jit(solution)/shard_map/ppermute | solution.py:310
  110.5 0.7 copy-start.14
  111.2 41.0 %collective-permute-start.18 = (f32[5,64,256]{2,1,0:T(8,128)}, f32[5,64,256]{2,1,0:T(8,128)S(1)}, u32[]{:S(2)}, u32[]{:S(2)}) collective-permute-start(f32[5,64,256]{2,1,0:T(8,128)} %get-tuple-element.56), channel_id=1, source_target_pairs={{1,3},{2,0},{5,7},{6,4},{9,11},{10,8},{13,15},{14,12},{17,19},{18,... | collective-permute-start | bytes 983048 | tf_op jit(solution)/shard_map/ppermute | solution.py:310
  122.3 3.9 %copy-start.17 = (f32[128,256]{1,0:T(8,128)}, f32[128,256]{1,0:T(8,128)S(1)}, u32[]{:S(2)}) copy-start(f32[128,256]{1,0:T(8,128)S(1)} %collective-permute-done.21.near0) | copy-start | bytes 393220
  122.3 29.8 %collective-permute-start.19 = (f32[5,64,256]{2,1,0:T(8,128)}, f32[5,64,256]{2,1,0:T(8,128)S(1)}, u32[]{:S(2)}, u32[]{:S(2)}) collective-permute-start(f32[5,64,256]{2,1,0:T(8,128)} %get-tuple-element.57), channel_id=1, source_target_pairs={{1,2},{2,1},{5,6},{6,5},{9,10},{10,9},{13,14},{14,13},{17,18},{18,... | collective-permute-start | bytes 983048 | tf_op jit(solution)/shard_map/ppermute | solution.py:310
  125.2 1.1 copy-start.18
  126.2 0.8 copy-start.6
  145.2 3.5 %collective-permute-start.24 = (f32[1,64,256]{2,1,0:T(8,128)}, f32[1,64,256]{2,1,0:T(8,128)S(1)}, u32[]{:S(2)}, u32[]{:S(2)}) collective-permute-start(f32[1,64,256]{2,1,0:T(8,128)} %get-tuple-element.63), channel_id=1, source_target_pairs={{0,1},{7,6},{8,9},{15,14},{16,17},{23,22},{24,25},{31,30}} | collective-permute-start | bytes 196616 | tf_op jit(solution)/shard_map/ppermute | solution.py:322
  146.5 3.5 %collective-permute-start.25 = (f32[1,64,256]{2,1,0:T(8,128)}, f32[1,64,256]{2,1,0:T(8,128)S(1)}, u32[]{:S(2)}, u32[]{:S(2)}) collective-permute-start(f32[1,64,256]{2,1,0:T(8,128)} %get-tuple-element.64), channel_id=1, source_target_pairs={{0,2},{7,5},{8,10},{15,13},{16,18},{23,21},{24,26},{31,29}} | collective-permute-start | bytes 196616 | tf_op jit(solution)/shard_map/ppermute | solution.py:322
  148.7 3.5 %copy-start.19 = (f32[1,64,256]{2,1,0:T(8,128)}, f32[1,64,256]{2,1,0:T(8,128)S(1)}, u32[]{:S(2)}) copy-start(f32[1,64,256]{2,1,0:T(8,128)S(1)} %collective-permute-done.24.refs_5_) | copy-start | bytes 196612
  148.7 3.5 %collective-permute-start.26 = (f32[1,64,256]{2,1,0:T(8,128)}, f32[1,64,256]{2,1,0:T(8,128)S(1)}, u32[]{:S(2)}, u32[]{:S(2)}) collective-permute-start(f32[1,64,256]{2,1,0:T(8,128)} %get-tuple-element.65), channel_id=1, source_target_pairs={{0,3},{7,4},{8,11},{15,12},{16,19},{23,20},{24,27},{31,28}} | collective-permute-start | bytes 196616 | tf_op jit(solution)/shard_map/ppermute | solution.py:322
  150.0 2.2 %copy-start.20 = (f32[1,64,256]{2,1,0:T(8,128)}, f32[1,64,256]{2,1,0:T(8,128)S(1)}, u32[]{:S(2)}) copy-start(f32[1,64,256]{2,1,0:T(8,128)S(1)} %collective-permute-done.25.refs_6_) | copy-start | bytes 196612
  152.2 0.7 copy-start.11
  152.2 0.9 copy-start.12
  152.2 1.0 copy-start.13
  (1 other events, 0.6 us)

commit v7 on v6

--- a/solution.py
+++ b/solution.py
@@ -152,10 +152,12 @@
                 rest[i - count] = near[which, i]
 
 
-def name_kernel(place, ids, low0, low1, high0, high1, mine_ref, other_ref):
+def name_kernel(place, ids, low0, low1, high0, high1, _, __, rest_mine, rest_other, found, sems):
     row, mine = place[0], place[1] >> 1
     clusters, slots = ids.shape
-    for which, out in ((mine, mine_ref), (1 - mine, other_ref)):
+    edge, count = found.shape[2], found.shape[1]
+    copies = []
+    for side, (which, rest) in enumerate(((mine, rest_mine), (1 - mine, rest_other))):
         for k in range(1, slots):
             name = ids[which, k]
             apart = lax.div(name, clusters) ^ row
@@ -164,7 +166,18 @@
             late = spot >= low0.shape[0]
             low = jnp.where(late, low1[inner], low0[inner])
             high = jnp.where(late, high1[inner], high0[inner])
-            out[k - 1] = jnp.where((apart & 1) > 0, high, low)
+            base = jnp.where((apart & 1) > 0, high, low)
+            for b in range(2):
+                found[side, 2 * (k - 1) + b] = base[:, b * edge : (b + 1) * edge]
+        copies.append(
+            pltpu.make_async_copy(
+                found.at[side], rest.at[pl.ds(rest.shape[0] - count, count)], sems.at[side]
+            )
+        )
+    for copy in copies:
+        copy.start()
+    for copy in copies:
+        copy.wait()
 
 
 def coupling(w_ref, blocks, bases):
@@ -197,9 +210,9 @@
 
 def near_rest_kernel(place, count, w_ref, schur, first, *refs):
     z = place[1]
-    blocks, named, parts = refs[:4], refs[4:8], refs[8:12]
-    flipped, block_buffer, base_buffer, sems = refs[12:]
-    total = named[0].shape[0]
+    blocks, parts = refs[:4], refs[4:8]
+    flipped, block_buffer, base_buffer, sems = refs[8:]
+    total = blocks[0].shape[0] // 6
 
     @pl.when(owns(z))
     def _():
@@ -210,8 +223,10 @@
                 copies.append(
                     pltpu.make_async_copy(blocks[j].at[tile], block_buffer.at[j, tile], sems.at[k, j, 0])
                 )
+                pair = pl.ds(2 * k, 2)
+                base = blocks[j].at[pl.ds(4 * total + 2 * k, 2)]
                 copies.append(
-                    pltpu.make_async_copy(named[j].at[k], base_buffer.at[j, k], sems.at[k, j, 1])
+                    pltpu.make_async_copy(base, base_buffer.at[j, pair], sems.at[k, j, 1])
                 )
         for copy in copies:
             copy.start()
@@ -225,7 +240,7 @@
             result = coupling(
                 w_ref,
                 [tall(block_buffer.at[j], 4 * k) for j in range(4)],
-                [base_buffer[j, k] for j in range(4)],
+                [wide(base_buffer.at[j], 2 * k, 2) for j in range(4)],
             )
             flipped[k + 2] = jnp.where(count[z >> 1] > k + 1, result, 0.0).T
             deal(z, flipped, k + 2, parts)
@@ -351,7 +366,7 @@
         pieces.append(across(pieces[0], bit))
 
     near = near_blocks.reshape(clusters, slots * 4, edge, edge)
-    rest_blocks = (slots - 1) * 4
+    rest_blocks = (slots - 1) * 6
     v = parent_bases[0]
     split = call(
         split_kernel,
@@ -363,7 +378,20 @@
     for piece in pieces:
         swapped.append(across(piece, 1))
     n_early = gather(*after((split[0], split[1]), leaf[1:]))
-    n_rest = gather(*after((split[2], split[3]), leaf[1:]))
+    scalar, vmem = pl.BlockSpec(memory_space=pltpu.SMEM), pl.BlockSpec(memory_space=pltpu.VMEM)
+    anywhere = pl.BlockSpec(memory_space=pl.ANY)
+    rest = pl.pallas_call(
+        name_kernel,
+        out_shape=[jax.ShapeDtypeStruct((rest_blocks, edge, edge), jnp.float32)] * 2,
+        in_specs=[scalar] * 2 + [vmem] * 4 + [anywhere] * 2,
+        out_specs=[anywhere] * 2,
+        scratch_shapes=[
+            pltpu.VMEM((2, (slots - 1) * 2, edge, edge), jnp.float32),
+            pltpu.SemaphoreType.DMA((2,)),
+        ],
+        input_output_aliases={6: 0, 7: 1},
+    )(place, near_ids, *pieces, *swapped, split[2], split[3])
+    n_rest = gather(*after(rest, leaf[1:]))
     (skeletons,) = call(skeleton_kernel, [(4, edge, skeleton)], [place], leaf)
     sibling = from_sibling(skeletons)
 
@@ -382,13 +410,6 @@
     top_got = from_neighbour(top)
     low_got = from_neighbour(low)
     pair_got = from_beside(pair)
-    chosen = call(
-        name_kernel,
-        [(slots - 1, edge, skeleton)] * 2,
-        [place, near_ids],
-        [*after(pieces, first), *swapped],
-    )
-    named = gather(*chosen)
     crown = call(
         parent_kernel,
         [(1, quarter, skeleton)] * 4,
@@ -402,15 +423,15 @@
         near_rest_kernel,
         [(total, quarter, skeleton)] * 4,
         [place, near_count],
-        [w, schur, first, *n_rest, *named],
+        [w, schur, first, *n_rest],
         7,
         [
             (total, skeleton, skeleton),
-            (4, rest_blocks, edge, edge),
-            (4, slots - 1, edge, skeleton),
+            (4, (slots - 1) * 4, edge, edge),
+            (4, (slots - 1) * 2, edge, edge),
             pltpu.SemaphoreType.DMA((slots - 1, 4, 2)),
         ],
-        8,
+        4,
     )
     turned = call(
         finish_kernel,

time: 157 us -> 146 us (0.930)
  starting transfers between devices: 46.6 us -> 40.7 us
  waiting for transfers between devices: 47.2 us -> 43.4 us
    ppermute x3, waiting for transfers between devices: 12 us -> 0.01 us  [from_neighbour(): lax.ppermute(x, both, [(r * n_col + (z ^ 1), r * n_col + z) for r, z in h...]
    ppermute x4, waiting for transfers between devices: 0.01 us -> 10.2 us  [across(): return lax.ppermute(x, 'row', [(r, r ^ bit) for r in range(n_row)])]
    ppermute x12 -> x9, starting transfers between devices: 29 us -> 22.1 us  [to_owner(): lax.ppermute(x, both, [(r * n_col + (z ^ j), r * n_col + z) for r, z in o...]
    pallas_call x0 -> x1, Pallas kernels: none -> 2.63 us  [levels(): pl.pallas_call(name_kernel, out_shape=[jax.ShapeDtypeStruct((rest_blocks,...]
    pallas_call x9 -> x8, Pallas kernels: 55.7 us -> 53.4 us  [call(): pl.pallas_call(kernel, out_shape=shapes, in_specs=specs, out_specs=[vmem]...]
    ppermute x12 -> x9, waiting for transfers between devices: 30.9 us -> 30 us  [to_owner(): lax.ppermute(x, both, [(r * n_col + (z ^ j), r * n_col + z) for r, z in o...]
    unnamed x45 -> x33, local copies, waits for them, and re-layouts: 4.28 us -> 3.76 us
  transfers between devices with their start and end apart: 27 -> 24, of which waited for: 11 -> 6; matrix products, arithmetic and copies ran while one was open for 1% -> 1% of each run, Pallas kernels for 33% -> 35%
where the time goes in v7:
time: 146 us
  Pallas kernels  56.1 us (38%)
  waiting for transfers between devices  43.4 us (30%)
  starting transfers between devices  40.7 us (28%)
  local copies, waits for them, and re-layouts  3.78 us (3%)
    pallas_call x8, Pallas kernels, call(): pl.pallas_call(kernel, out_shape=shapes, in_specs=specs, out_specs=[vmem]...  53.4 us
    ppermute x9, waiting for transfers between devices, to_owner(): lax.ppermute(x, both, [(r * n_col + (z ^ j), r * n_col + z) for r, z in o...  30 us
    ppermute x9, starting transfers between devices, to_owner(): lax.ppermute(x, both, [(r * n_col + (z ^ j), r * n_col + z) for r, z in o...  22.1 us
    ppermute x4, waiting for transfers between devices, across(): return lax.ppermute(x, 'row', [(r, r ^ bit) for r in range(n_row)])  10.2 us
    ppermute x4, starting transfers between devices, across(): return lax.ppermute(x, 'row', [(r, r ^ bit) for r in range(n_row)])  4.88 us
    ppermute x3, starting transfers between devices, from_head(): lax.ppermute(x, both, [(r * n_col + z, r * n_col + (z ^ j)) for r, z in h...  3.85 us
    ppermute x3, starting transfers between devices, from_neighbour(): lax.ppermute(x, both, [(r * n_col + (z ^ 1), r * n_col + z) for r, z in h...  3.85 us
    unnamed x33, local copies, waits for them, and re-layouts  3.76 us
  transfers between devices with their start and end apart: 24, of which 6 were waited for; matrix products, arithmetic and copies ran while one was open for 1% of the time, Pallas kernels for 35%

profile of v7, /device:TPU:0, one launch (start us, length us, event | category | flops | bytes accessed | tf_op | source)
XLA Modules:
  0.0 145.5 jit_solution(4339637523035690554)
XLA Ops:
  0.6 0.7 pad_add_fusion.place
  1.3 2.3 %shard_map.85 = (f32[8,128,128]{2,1,0:T(8,128)}, f32[6,128,128]{2,1,0:T(8,128)}, f32[2,128,256]{2,1,0:T(8,128)}) custom-call(s32[2]{0:T(128)} %pad_add_fusion.place, f32[2,512,128]{2,1,0:T(8,128)} %diag.1, f32[2,128,512]{2,1,0:T(8,128)} %bases.1), custom_call_target="tpu_custom_call" | custom-call | flops 2000000000 | bytes 2000000 | tf_op jit(solution)/shard_map/pallas_call | solution.py:294
  3.6 3.0 %collective-permute-start.7 = (f32[2,128,256]{2,1,0:T(8,128)}, f32[2,128,256]{2,1,0:T(8,128)S(1)}, u32[]{:S(2)}, u32[]{:S(2)}) collective-permute-start(f32[2,128,256]{2,1,0:T(8,128)} %get-tuple-element.43), channel_id=1, source_target_pairs={{0,8},{4,12},{8,0},{12,4},{16,24},{20,28},{24,16},{28,20},{1,9},{5... | collective-permute-start | bytes 786440 | tf_op jit(solution)/shard_map/ppermute | solution.py:340
  6.6 1.0 constant_dynamic-update-slice_fusion.1
  7.6 5.5 %collective-permute-done.7 = f32[2,128,256]{2,1,0:T(8,128)S(1)} collective-permute-done((f32[2,128,256]{2,1,0:T(8,128)}, f32[2,128,256]{2,1,0:T(8,128)S(1)}, u32[]{:S(2)}, u32[]{:S(2)}) %collective-permute-start.7) | collective-permute-done | bytes 262176 | tf_op jit(solution)/shard_map/ppermute | solution.py:340
  13.1 1.8 %collective-permute-start.8 = (f32[4,128,256]{2,1,0:T(8,128)S(1)}, f32[4,128,256]{2,1,0:T(8,128)S(1)}, u32[]{:S(2)}, u32[]{:S(2)}) collective-permute-start(f32[4,128,256]{2,1,0:T(8,128)S(1)} %constant_dynamic-update-slice_fusion.low0), channel_id=1, source_target_pairs={{0,16},{4,20},{8,24},{12,28},{16,0},{20,4},{24,8},{28,12},{1,17},{... | collective-permute-start | bytes 1572872 | tf_op jit(solution)/shard_map/ppermute | solution.py:340
  14.9 3.5 %collective-permute-start = (f32[8,128,128]{2,1,0:T(8,128)}, f32[8,128,128]{2,1,0:T(8,128)S(1)}, u32[]{:S(2)}, u32[]{:S(2)}) collective-permute-start(f32[8,128,128]{2,1,0:T(8,128)} %get-tuple-element.34.own), channel_id=1, source_target_pairs={{0,1},{3,2},{4,5},{7,6},{8,9},{11,10},{12,13},{15,14},{16,17},{19,... | collective-permute-start | bytes 1572872 | tf_op jit(solution)/shard_map/ppermute | solution.py:322
  18.4 2.3 %collective-permute-start.1 = (f32[6,128,128]{2,1,0:T(8,128)}, f32[6,128,128]{2,1,0:T(8,128)S(1)}, u32[]{:S(2)}, u32[]{:S(2)}) collective-permute-start(f32[6,128,128]{2,1,0:T(8,128)} %get-tuple-element.35), channel_id=1, source_target_pairs={{3,1},{0,2},{7,5},{4,6},{11,9},{8,10},{15,13},{12,14},{19,17},{16,... | collective-permute-start | bytes 1179656 | tf_op jit(solution)/shard_map/ppermute | solution.py:322
  20.8 0.7 collective-permute-start.2
  21.4 0.1 collective-permute-start.9
  21.5 4.7 %collective-permute-done.8.low1 = f32[4,128,256]{2,1,0:T(8,128)S(1)} collective-permute-done((f32[4,128,256]{2,1,0:T(8,128)S(1)}, f32[4,128,256]{2,1,0:T(8,128)S(1)}, u32[]{:S(2)}, u32[]{:S(2)}) %collective-permute-start.8) | collective-permute-done | bytes 524320 | tf_op jit(solution)/shard_map/ppermute | solution.py:340
  26.3 0.0 collective-permute-start.10
  26.3 4.2 %shard_map.88 = (f32[4,128,128]{2,1,0:T(8,128)}, f32[4,128,128]{2,1,0:T(8,128)}, f32[18,128,128]{2,1,0:T(8,128)}, f32[18,128,128]{2,1,0:T(8,128)}, f32[512,512]{1,0:T(8,128)}) custom-call(s32[2]{0:T(128)} %pad_add_fusion.place, f32[2,16,128,128]{3,2,1,0:T(8,128)} %bitcast.7, f32[512,512]{1,0:T(8,128)} %bitcast.8), custom_call_target="tpu_custom_call" | custom-call | flops 2000000000 | bytes 2000000 | tf_op jit(solution)/shard_map/pallas_call | solution.py:294
  30.5 6.7 %collective-permute-done.1.far2 = f32[6,128,128]{2,1,0:T(8,128)S(1)} collective-permute-done((f32[6,128,128]{2,1,0:T(8,128)}, f32[6,128,128]{2,1,0:T(8,128)S(1)}, u32[]{:S(2)}, u32[]{:S(2)}) %collective-permute-start.1) | collective-permute-done | bytes 393248 | tf_op jit(solution)/shard_map/ppermute | solution.py:322
  37.2 6.0 %collective-permute-start.4 = (f32[4,128,128]{2,1,0:T(8,128)}, f32[4,128,128]{2,1,0:T(8,128)}, u32[]{:S(2)}, u32[]{:S(2)}) collective-permute-start(f32[4,128,128]{2,1,0:T(8,128)} %get-tuple-element.40.n0), channel_id=1, source_target_pairs={{0,1},{3,2},{4,5},{7,6},{8,9},{11,10},{12,13},{15,14},{16,17},{19,... | collective-permute-start | bytes 786440 | tf_op jit(solution)/shard_map/ppermute | solution.py:322
  43.2 2.0 %collective-permute-start.5 = (f32[4,128,128]{2,1,0:T(8,128)}, f32[4,128,128]{2,1,0:T(8,128)}, u32[]{:S(2)}, u32[]{:S(2)}) collective-permute-start(f32[4,128,128]{2,1,0:T(8,128)} %get-tuple-element.41), channel_id=1, source_target_pairs={{3,1},{0,2},{7,5},{4,6},{11,9},{8,10},{15,13},{12,14},{19,17},{16,... | collective-permute-start | bytes 786440 | tf_op jit(solution)/shard_map/ppermute | solution.py:322
  45.2 1.4 collective-permute-start.6
  46.6 2.3 %shard_map.87 = f32[4,128,256]{2,1,0:T(8,128)} custom-call(s32[2]{0:T(128)} %pad_add_fusion.place, f32[8,128,128]{2,1,0:T(8,128)} %get-tuple-element.34.own, f32[8,128,128]{2,1,0:T(8,128)} %copy-done.7, f32[6,128,128]{2,1,0:T(8,128)} %copy-done.8, f32[6,128,128]{2,1,0:T(8,128)} %copy-done.9), custom_call_target="tpu_custom_call" | custom-call | flops 2000000000 | bytes 2000000 | tf_op jit(solution)/shard_map/pallas_call | solution.py:294
  48.9 1.4 collective-permute-start.3
  50.3 0.8 copy-done.3
  51.1 2.6 %shard_map.90 = (f32[18,128,128]{2,1,0:T(8,128)}, f32[18,128,128]{2,1,0:T(8,128)}) custom-call(s32[2]{0:T(128)} %pad_add_fusion.place, s32[2,4]{1,0:T(2,128)} %ids.1, f32[4,128,256]{2,1,0:T(8,128)} %copy-done, f32[4,128,256]{2,1,0:T(8,128)} %copy-done.1, f32[4,128,256]{2,1,0:T(8,128)} %copy-done.2, ...), custom_call_target="tpu_custom_call", output_to_operand_aliasing={{0}: (6, {}), {1}: (7, {})} | custom-call | tf_op jit(solution)/shard_map/pallas_call | solution.py:383
  53.8 2.5 %collective-permute-start.12 = (f32[18,128,128]{2,1,0:T(8,128)}, f32[18,128,128]{2,1,0:T(8,128)S(1)}, u32[]{:S(2)}, u32[]{:S(2)}) collective-permute-start(f32[18,128,128]{2,1,0:T(8,128)} %get-tuple-element.49), channel_id=1, source_target_pairs={{3,1},{0,2},{7,5},{4,6},{11,9},{8,10},{15,13},{12,14},{19,17},{16,... | collective-permute-start | bytes 3538952 | tf_op jit(solution)/shard_map/ppermute | solution.py:322
  56.2 0.7 collective-permute-start.13
  57.0 3.0 %collective-permute-start.11 = (f32[18,128,128]{2,1,0:T(8,128)}, f32[18,128,128]{2,1,0:T(8,128)S(1)}, u32[]{:S(2)}, u32[]{:S(2)}) collective-permute-start(f32[18,128,128]{2,1,0:T(8,128)} %get-tuple-element.48.refs_0_), channel_id=1, source_target_pairs={{0,1},{3,2},{4,5},{7,6},{8,9},{11,10},{12,13},{15,14},{16,17},{19,... | collective-permute-start | bytes 3538952 | tf_op jit(solution)/shard_map/ppermute | solution.py:322
  60.0 18.0 %shard_map.86 = (f32[4,256,128]{2,1,0:T(8,128)}, f32[256,256]{1,0:T(8,128)}) custom-call(s32[2]{0:T(128)} %pad_add_fusion.place, f32[8,128,128]{2,1,0:T(8,128)} %get-tuple-element.34.own, f32[8,128,128]{2,1,0:T(8,128)} %copy-done.7, f32[6,128,128]{2,1,0:T(8,128)} %copy-done.8, f32[6,128,128]{2,1,0:T(8,128)} %copy-done.9), custom_call_target="tpu_custom_call" | custom-call | flops 22000001024 | bytes 22000000 | tf_op jit(solution)/shard_map/pallas_call | solution.py:294
  78.1 1.3 collective-permute-start.17
  79.4 3.8 %shard_map.89 = (f32[128,256]{1,0:T(8,128)}, f32[128,256]{1,0:T(8,128)}, f32[256,256]{1,0:T(8,128)}, f32[2,256,256]{2,1,0:T(8,128)}) custom-call(s32[2]{0:T(128)} %pad_add_fusion.place, s32[2]{0:T(128)} %count.3, f32[4,256,128]{2,1,0:T(8,128)} %get-tuple-element.36.w_ref, f32[4,128,256]{2,1,0:T(8,128)} %collective-permute-done.3.bases, ...), custom_call_target="tpu_custom_call" | custom-call | flops 4000000000 | bytes 4000000 | tf_op jit(solution)/shard_map/pallas_call | solution.py:294
  83.1 1.3 collective-permute-start.20
  84.4 23.3 %collective-permute-done.11.refs_1_ = f32[18,128,128]{2,1,0:T(8,128)S(1)} collective-permute-done((f32[18,128,128]{2,1,0:T(8,128)}, f32[18,128,128]{2,1,0:T(8,128)S(1)}, u32[]{:S(2)}, u32[]{:S(2)}) %collective-permute-start.11) | collective-permute-done | bytes 1179680 | tf_op jit(solution)/shard_map/ppermute | solution.py:322
  107.7 1.3 collective-permute-start.18
  109.0 1.3 collective-permute-start.19
  110.3 1.0 copy-done.5
  111.3 2.5 %shard_map.91 = (f32[5,64,256]{2,1,0:T(8,128)}, f32[5,64,256]{2,1,0:T(8,128)}, f32[5,64,256]{2,1,0:T(8,128)}, f32[5,64,256]{2,1,0:T(8,128)}) custom-call(s32[2]{0:T(128)} %pad_add_fusion.place, s32[2]{0:T(128)} %count.3, f32[4,256,128]{2,1,0:T(8,128)} %get-tuple-element.36.w_ref, f32[256,256]{1,0:T(8,128)} %get-tuple-element.37.schur, ...), custom_call_target="tpu_custom_call" | custom-call | flops 7000000000 | bytes 7000000 | tf_op jit(solution)/shard_map/pallas_call | solution.py:294
  113.9 1.3 collective-permute-start.14
  115.2 1.3 collective-permute-start.15
  116.5 0.7 collective-permute-start.16
  117.2 18.1 %shard_map.92 = (f32[1,64,256]{2,1,0:T(8,128)}, f32[1,64,256]{2,1,0:T(8,128)}, f32[1,64,256]{2,1,0:T(8,128)}, f32[1,64,256]{2,1,0:T(8,128)}) custom-call(s32[2]{0:T(128)} %pad_add_fusion.place, f32[256,256]{1,0:T(8,128)} %collective-permute-done.17.diag, f32[128,256]{1,0:T(8,128)} %collective-permute-done.18.near0, ...), custom_call_target="tpu_custom_call" | custom-call | flops 20000000000 | bytes 20000000 | tf_op jit(solution)/shard_map/pallas_call | solution.py:294
  135.3 1.3 collective-permute-start.21
  136.6 1.3 collective-permute-start.22
  137.9 0.9 collective-permute-done.21.refs_5_
  138.8 1.3 collective-permute-start.23
  140.1 0.0 collective-permute-done.22.refs_6_
  140.1 2.2 %collective-permute-done.23.refs_7_ = f32[1,64,256]{2,1,0:T(8,128)S(1)} collective-permute-done((f32[1,64,256]{2,1,0:T(8,128)}, f32[1,64,256]{2,1,0:T(8,128)S(1)}, u32[]{:S(2)}, u32[]{:S(2)}) %collective-permute-start.23) | collective-permute-done | bytes 65568 | tf_op jit(solution)/shard_map/ppermute | solution.py:337
  142.4 0.6 copy-done.15
  142.9 0.1 copy-done.10
  143.1 0.1 copy-done.11
  143.2 0.1 copy-done.12
  143.3 2.2 %shard_map.93 = (f32[2,64,256]{2,1,0:T(8,128)}, f32[2,4,64,256]{3,2,1,0:T(8,128)}, f32[1,64,256]{2,1,0:T(8,128)}) custom-call(s32[2]{0:T(128)} %pad_add_fusion.place, f32[5,64,256]{2,1,0:T(8,128)} %get-tuple-element.50.refs_0_, f32[5,64,256]{2,1,0:T(8,128)} %copy-done.10, f32[5,64,256]{2,1,0:T(8,128)} %copy-done.11, f32[5,64,256]{2,1,0:T(8,128)} %copy-done.12, ...), custom_call_target="tpu_custom_call" | custom-call | flops 2000000000 | bytes 2000000 | tf_op jit(solution)/shard_map/pallas_call | solution.py:294
  (44 shorter events, 0.1 us)
Async XLA Ops:
  3.6 9.5 %collective-permute-start.7 = (f32[2,128,256]{2,1,0:T(8,128)}, f32[2,128,256]{2,1,0:T(8,128)S(1)}, u32[]{:S(2)}, u32[]{:S(2)}) collective-permute-start(f32[2,128,256]{2,1,0:T(8,128)} %get-tuple-element.43), channel_id=1, source_target_pairs={{0,8},{4,12},{8,0},{12,4},{16,24},{20,28},{24,16},{28,20},{1,9},{5... | collective-permute-start | bytes 786440 | tf_op jit(solution)/shard_map/ppermute | solution.py:340
  13.1 17.4 %copy-start = (f32[4,128,256]{2,1,0:T(8,128)}, f32[4,128,256]{2,1,0:T(8,128)S(1)}, u32[]{:S(2)}) copy-start(f32[4,128,256]{2,1,0:T(8,128)S(1)} %constant_dynamic-update-slice_fusion.low0) | copy-start | bytes 1572868
  13.1 13.2 %collective-permute-start.8 = (f32[4,128,256]{2,1,0:T(8,128)S(1)}, f32[4,128,256]{2,1,0:T(8,128)S(1)}, u32[]{:S(2)}, u32[]{:S(2)}) collective-permute-start(f32[4,128,256]{2,1,0:T(8,128)S(1)} %constant_dynamic-update-slice_fusion.low0), channel_id=1, source_target_pairs={{0,16},{4,20},{8,24},{12,28},{16,0},{20,4},{24,8},{28,12},{1,17},{... | collective-permute-start | bytes 1572872 | tf_op jit(solution)/shard_map/ppermute | solution.py:340
  14.9 22.3 %collective-permute-start = (f32[8,128,128]{2,1,0:T(8,128)}, f32[8,128,128]{2,1,0:T(8,128)S(1)}, u32[]{:S(2)}, u32[]{:S(2)}) collective-permute-start(f32[8,128,128]{2,1,0:T(8,128)} %get-tuple-element.34.own), channel_id=1, source_target_pairs={{0,1},{3,2},{4,5},{7,6},{8,9},{11,10},{12,13},{15,14},{16,17},{19,... | collective-permute-start | bytes 1572872 | tf_op jit(solution)/shard_map/ppermute | solution.py:322
  18.4 18.7 %collective-permute-start.1 = (f32[6,128,128]{2,1,0:T(8,128)}, f32[6,128,128]{2,1,0:T(8,128)S(1)}, u32[]{:S(2)}, u32[]{:S(2)}) collective-permute-start(f32[6,128,128]{2,1,0:T(8,128)} %get-tuple-element.35), channel_id=1, source_target_pairs={{3,1},{0,2},{7,5},{4,6},{11,9},{8,10},{15,13},{12,14},{19,17},{16,... | collective-permute-start | bytes 1179656 | tf_op jit(solution)/shard_map/ppermute | solution.py:322
  20.8 16.4 %collective-permute-start.2 = (f32[6,128,128]{2,1,0:T(8,128)}, f32[6,128,128]{2,1,0:T(8,128)S(1)}, u32[]{:S(2)}, u32[]{:S(2)}) collective-permute-start(f32[6,128,128]{2,1,0:T(8,128)} %get-tuple-element.35), channel_id=1, source_target_pairs={{2,1},{1,2},{6,5},{5,6},{10,9},{9,10},{14,13},{13,14},{18,17},{17,... | collective-permute-start | bytes 1179656 | tf_op jit(solution)/shard_map/ppermute | solution.py:322
  21.4 27.4 %collective-permute-start.9 = (f32[4,128,256]{2,1,0:T(8,128)S(1)}, f32[4,128,256]{2,1,0:T(8,128)S(1)}, u32[]{:S(2)}, u32[]{:S(2)}) collective-permute-start(f32[4,128,256]{2,1,0:T(8,128)S(1)} %constant_dynamic-update-slice_fusion.low0), channel_id=1, source_target_pairs={{0,4},{4,0},{8,12},{12,8},{16,20},{20,16},{24,28},{28,24},{1,5},{5... | collective-permute-start | bytes 1572872 | tf_op jit(solution)/shard_map/ppermute | solution.py:340
  26.3 4.2 %copy-start.1 = (f32[4,128,256]{2,1,0:T(8,128)}, f32[4,128,256]{2,1,0:T(8,128)S(1)}, u32[]{:S(2)}) copy-start(f32[4,128,256]{2,1,0:T(8,128)S(1)} %collective-permute-done.8.low1) | copy-start | bytes 1572868
  26.3 24.1 %collective-permute-start.10 = (f32[4,128,256]{2,1,0:T(8,128)S(1)}, f32[4,128,256]{2,1,0:T(8,128)S(1)}, u32[]{:S(2)}, u32[]{:S(2)}) collective-permute-start(f32[4,128,256]{2,1,0:T(8,128)S(1)} %collective-permute-done.8.low1), channel_id=1, source_target_pairs={{0,4},{4,0},{8,12},{12,8},{16,20},{20,16},{24,28},{28,24},{1,5},{5... | collective-permute-start | bytes 1572872 | tf_op jit(solution)/shard_map/ppermute | solution.py:340
  37.2 9.4 %copy-start.8 = (f32[6,128,128]{2,1,0:T(8,128)}, f32[6,128,128]{2,1,0:T(8,128)S(1)}, u32[]{:S(2)}) copy-start(f32[6,128,128]{2,1,0:T(8,128)S(1)} %collective-permute-done.1.far2) | copy-start | bytes 1179652
  37.2 9.4 %copy-start.9 = (f32[6,128,128]{2,1,0:T(8,128)}, f32[6,128,128]{2,1,0:T(8,128)S(1)}, u32[]{:S(2)}) copy-start(f32[6,128,128]{2,1,0:T(8,128)S(1)} %collective-permute-done.2.far3) | copy-start | bytes 1179652
  37.2 9.4 %copy-start.7 = (f32[8,128,128]{2,1,0:T(8,128)}, f32[8,128,128]{2,1,0:T(8,128)S(1)}, u32[]{:S(2)}) copy-start(f32[8,128,128]{2,1,0:T(8,128)S(1)} %collective-permute-done.near) | copy-start | bytes 1572868
  37.2 19.0 %collective-permute-start.4 = (f32[4,128,128]{2,1,0:T(8,128)}, f32[4,128,128]{2,1,0:T(8,128)}, u32[]{:S(2)}, u32[]{:S(2)}) collective-permute-start(f32[4,128,128]{2,1,0:T(8,128)} %get-tuple-element.40.n0), channel_id=1, source_target_pairs={{0,1},{3,2},{4,5},{7,6},{8,9},{11,10},{12,13},{15,14},{16,17},{19,... | collective-permute-start | bytes 786440 | tf_op jit(solution)/shard_map/ppermute | solution.py:322
  43.2 13.8 %collective-permute-start.5 = (f32[4,128,128]{2,1,0:T(8,128)}, f32[4,128,128]{2,1,0:T(8,128)}, u32[]{:S(2)}, u32[]{:S(2)}) collective-permute-start(f32[4,128,128]{2,1,0:T(8,128)} %get-tuple-element.41), channel_id=1, source_target_pairs={{3,1},{0,2},{7,5},{4,6},{11,9},{8,10},{15,13},{12,14},{19,17},{16,... | collective-permute-start | bytes 786440 | tf_op jit(solution)/shard_map/ppermute | solution.py:322
  45.2 32.8 %collective-permute-start.6 = (f32[4,128,128]{2,1,0:T(8,128)}, f32[4,128,128]{2,1,0:T(8,128)}, u32[]{:S(2)}, u32[]{:S(2)}) collective-permute-start(f32[4,128,128]{2,1,0:T(8,128)} %get-tuple-element.41), channel_id=1, source_target_pairs={{2,1},{1,2},{6,5},{5,6},{10,9},{9,10},{14,13},{13,14},{18,17},{17,... | collective-permute-start | bytes 786440 | tf_op jit(solution)/shard_map/ppermute | solution.py:322
  48.9 1.5 %copy-start.2 = (f32[4,128,256]{2,1,0:T(8,128)}, f32[4,128,256]{2,1,0:T(8,128)S(1)}, u32[]{:S(2)}) copy-start(f32[4,128,256]{2,1,0:T(8,128)S(1)} %collective-permute-done.9.high0) | copy-start | bytes 1572868
  48.9 30.5 %collective-permute-start.3 = (f32[4,128,256]{2,1,0:T(8,128)}, f32[4,128,256]{2,1,0:T(8,128)}, u32[]{:S(2)}, u32[]{:S(2)}) collective-permute-start(f32[4,128,256]{2,1,0:T(8,128)} %shard_map.87), channel_id=1, source_target_pairs={{5,1},{6,2},{1,5},{2,6},{13,9},{14,10},{9,13},{10,14},{21,17},{22,... | collective-permute-start | bytes 1572872 | tf_op jit(solution)/shard_map/ppermute | solution.py:328
  50.3 0.8 copy-start.3
  53.8 55.2 %collective-permute-start.12 = (f32[18,128,128]{2,1,0:T(8,128)}, f32[18,128,128]{2,1,0:T(8,128)S(1)}, u32[]{:S(2)}, u32[]{:S(2)}) collective-permute-start(f32[18,128,128]{2,1,0:T(8,128)} %get-tuple-element.49), channel_id=1, source_target_pairs={{3,1},{0,2},{7,5},{4,6},{11,9},{8,10},{15,13},{12,14},{19,17},{16,... | collective-permute-start | bytes 3538952 | tf_op jit(solution)/shard_map/ppermute | solution.py:322
  56.2 54.0 %collective-permute-start.13 = (f32[18,128,128]{2,1,0:T(8,128)}, f32[18,128,128]{2,1,0:T(8,128)S(1)}, u32[]{:S(2)}, u32[]{:S(2)}) collective-permute-start(f32[18,128,128]{2,1,0:T(8,128)} %get-tuple-element.49), channel_id=1, source_target_pairs={{2,1},{1,2},{6,5},{5,6},{10,9},{9,10},{14,13},{13,14},{18,17},{17,... | collective-permute-start | bytes 3538952 | tf_op jit(solution)/shard_map/ppermute | solution.py:322
  57.0 50.7 %collective-permute-start.11 = (f32[18,128,128]{2,1,0:T(8,128)}, f32[18,128,128]{2,1,0:T(8,128)S(1)}, u32[]{:S(2)}, u32[]{:S(2)}) collective-permute-start(f32[18,128,128]{2,1,0:T(8,128)} %get-tuple-element.48.refs_0_), channel_id=1, source_target_pairs={{0,1},{3,2},{4,5},{7,6},{8,9},{11,10},{12,13},{15,14},{16,17},{19,... | collective-permute-start | bytes 3538952 | tf_op jit(solution)/shard_map/ppermute | solution.py:322
  78.1 37.1 %collective-permute-start.17 = (f32[256,256]{1,0:T(8,128)}, f32[256,256]{1,0:T(8,128)}, u32[]{:S(2)}, u32[]{:S(2)}) collective-permute-start(f32[256,256]{1,0:T(8,128)} %get-tuple-element.37.schur), channel_id=1, source_target_pairs={{1,0},{6,7},{9,8},{14,15},{17,16},{22,23},{25,24},{30,31}} | collective-permute-start | bytes 786440 | tf_op jit(solution)/shard_map/ppermute | solution.py:331
  83.1 34.1 %collective-permute-start.20 = (f32[2,256,256]{2,1,0:T(8,128)}, f32[2,256,256]{2,1,0:T(8,128)}, u32[]{:S(2)}, u32[]{:S(2)}) collective-permute-start(f32[2,256,256]{2,1,0:T(8,128)} %get-tuple-element.56), channel_id=1, source_target_pairs={{5,0},{2,7},{13,8},{10,15},{21,16},{18,23},{29,24},{26,31}} | collective-permute-start | bytes 1572872 | tf_op jit(solution)/shard_map/ppermute | solution.py:334
  107.7 2.6 %copy-start.6 = (f32[18,128,128]{2,1,0:T(8,128)}, f32[18,128,128]{2,1,0:T(8,128)S(1)}, u32[]{:S(2)}) copy-start(f32[18,128,128]{2,1,0:T(8,128)S(1)} %collective-permute-done.11.refs_1_) | copy-start | bytes 3538948
  107.7 8.8 %collective-permute-start.18 = (f32[128,256]{1,0:T(8,128)}, f32[128,256]{1,0:T(8,128)}, u32[]{:S(2)}, u32[]{:S(2)}) collective-permute-start(f32[128,256]{1,0:T(8,128)} %get-tuple-element.54), channel_id=1, source_target_pairs={{1,0},{6,7},{9,8},{14,15},{17,16},{22,23},{25,24},{30,31}} | collective-permute-start | bytes 393224 | tf_op jit(solution)/shard_map/ppermute | solution.py:331
  109.0 1.3 copy-start.4
  109.0 8.2 %collective-permute-start.19 = (f32[128,256]{1,0:T(8,128)}, f32[128,256]{1,0:T(8,128)}, u32[]{:S(2)}, u32[]{:S(2)}) collective-permute-start(f32[128,256]{1,0:T(8,128)} %get-tuple-element.55), channel_id=1, source_target_pairs={{1,0},{6,7},{9,8},{14,15},{17,16},{22,23},{25,24},{30,31}} | collective-permute-start | bytes 393224 | tf_op jit(solution)/shard_map/ppermute | solution.py:331
  110.3 1.0 copy-start.5
  113.9 28.5 %collective-permute-start.14 = (f32[5,64,256]{2,1,0:T(8,128)}, f32[5,64,256]{2,1,0:T(8,128)S(1)}, u32[]{:S(2)}, u32[]{:S(2)}) collective-permute-start(f32[5,64,256]{2,1,0:T(8,128)} %get-tuple-element.51), channel_id=1, source_target_pairs={{1,0},{2,3},{5,4},{6,7},{9,8},{10,11},{13,12},{14,15},{17,16},{18,... | collective-permute-start | bytes 983048 | tf_op jit(solution)/shard_map/ppermute | solution.py:325
  115.2 27.2 %collective-permute-start.15 = (f32[5,64,256]{2,1,0:T(8,128)}, f32[5,64,256]{2,1,0:T(8,128)S(1)}, u32[]{:S(2)}, u32[]{:S(2)}) collective-permute-start(f32[5,64,256]{2,1,0:T(8,128)} %get-tuple-element.52), channel_id=1, source_target_pairs={{1,3},{2,0},{5,7},{6,4},{9,11},{10,8},{13,15},{14,12},{17,19},{18,... | collective-permute-start | bytes 983048 | tf_op jit(solution)/shard_map/ppermute | solution.py:325
  116.5 25.9 %collective-permute-start.16 = (f32[5,64,256]{2,1,0:T(8,128)}, f32[5,64,256]{2,1,0:T(8,128)S(1)}, u32[]{:S(2)}, u32[]{:S(2)}) collective-permute-start(f32[5,64,256]{2,1,0:T(8,128)} %get-tuple-element.53), channel_id=1, source_target_pairs={{1,2},{2,1},{5,6},{6,5},{9,10},{10,9},{13,14},{14,13},{17,18},{18,... | collective-permute-start | bytes 983048 | tf_op jit(solution)/shard_map/ppermute | solution.py:325
  135.3 3.5 %collective-permute-start.21 = (f32[1,64,256]{2,1,0:T(8,128)}, f32[1,64,256]{2,1,0:T(8,128)S(1)}, u32[]{:S(2)}, u32[]{:S(2)}) collective-permute-start(f32[1,64,256]{2,1,0:T(8,128)} %get-tuple-element.59), channel_id=1, source_target_pairs={{0,1},{7,6},{8,9},{15,14},{16,17},{23,22},{24,25},{31,30}} | collective-permute-start | bytes 196616 | tf_op jit(solution)/shard_map/ppermute | solution.py:337
  136.6 3.5 %collective-permute-start.22 = (f32[1,64,256]{2,1,0:T(8,128)}, f32[1,64,256]{2,1,0:T(8,128)S(1)}, u32[]{:S(2)}, u32[]{:S(2)}) collective-permute-start(f32[1,64,256]{2,1,0:T(8,128)} %get-tuple-element.60), channel_id=1, source_target_pairs={{0,2},{7,5},{8,10},{15,13},{16,18},{23,21},{24,26},{31,29}} | collective-permute-start | bytes 196616 | tf_op jit(solution)/shard_map/ppermute | solution.py:337
  138.8 3.5 %copy-start.13 = (f32[1,64,256]{2,1,0:T(8,128)}, f32[1,64,256]{2,1,0:T(8,128)S(1)}, u32[]{:S(2)}) copy-start(f32[1,64,256]{2,1,0:T(8,128)S(1)} %collective-permute-done.21.refs_5_) | copy-start | bytes 196612
  138.8 3.5 %collective-permute-start.23 = (f32[1,64,256]{2,1,0:T(8,128)}, f32[1,64,256]{2,1,0:T(8,128)S(1)}, u32[]{:S(2)}, u32[]{:S(2)}) collective-permute-start(f32[1,64,256]{2,1,0:T(8,128)} %get-tuple-element.61), channel_id=1, source_target_pairs={{0,3},{7,4},{8,11},{15,12},{16,19},{23,20},{24,27},{31,28}} | collective-permute-start | bytes 196616 | tf_op jit(solution)/shard_map/ppermute | solution.py:337
  140.1 2.2 %copy-start.14 = (f32[1,64,256]{2,1,0:T(8,128)}, f32[1,64,256]{2,1,0:T(8,128)S(1)}, u32[]{:S(2)}) copy-start(f32[1,64,256]{2,1,0:T(8,128)S(1)} %collective-permute-done.22.refs_6_) | copy-start | bytes 196612
  142.3 0.6 copy-start.15
  142.3 0.7 copy-start.10
  142.3 0.8 copy-start.11
  142.4 1.0 copy-start.12

commit v8 on v7

--- a/solution.py
+++ b/solution.py
@@ -90,7 +90,7 @@
 def eliminate(dense, redundant):
     rr = dense[:redundant, :redundant]
     solved = solve((rr + rr.T) * 0.5, dense[:redundant, redundant:])
-    return solved, dense[redundant:, redundant:] - dot(dense[redundant:, :redundant], solved)
+    return solved, dense[redundant:, redundant:] - dot3(dense[redundant:, :redundant], solved)
 
 
 def wide(ref, start, count):
@@ -98,26 +98,28 @@
 
 
 def leaf_kernel(place, own, near, far2, far3, w_ref, schur_ref):
-    z = place[1]
-    inner = z & 1
-    edge = own.shape[1]
-    redundant = 4 * edge - w_ref.shape[1]
-    pairs = [jnp.concatenate([own[z ^ m], near[z ^ m]], axis=1) for m in range(4)]
-    corner = jnp.concatenate(pairs[:2], axis=0)
-    side = jnp.concatenate(pairs[2:], axis=0)
-    far = [jnp.concatenate([far2[i], far3[i]], axis=1) for i in (inner, 1 - inner)]
-    far = jnp.concatenate(far, axis=0)
-    bases = [wide(own, 4, 4), wide(near, 4, 4), wide(far2, 2, 4), wide(far3, 2, 4)]
-    u = jnp.concatenate(bases, axis=0)
-    ut = u.T
-    left = jnp.concatenate([corner, side], axis=0)
-    right = jnp.concatenate([side.T, far], axis=0)
-    dense = dot3(dot3(ut, jnp.concatenate([left, right], axis=1)), u)
-    solved, schur = eliminate(dense, redundant)
-    schur_ref[...] = schur
-    wt = ut[redundant:] - dot(solved.T, ut[:redundant])
-    for m in range(4):
-        w_ref[z ^ m] = wt[:, m * edge : (m + 1) * edge]
+    @pl.when(owns(place[1]))
+    def _():
+        z = place[1]
+        inner = z & 1
+        edge = own.shape[1]
+        redundant = 4 * edge - w_ref.shape[1]
+        pairs = [jnp.concatenate([own[z ^ m], near[z ^ m]], axis=1) for m in range(4)]
+        corner = jnp.concatenate(pairs[:2], axis=0)
+        side = jnp.concatenate(pairs[2:], axis=0)
+        far = [jnp.concatenate([far2[i], far3[i]], axis=1) for i in (inner, 1 - inner)]
+        far = jnp.concatenate(far, axis=0)
+        bases = [wide(own, 4, 4), wide(near, 4, 4), wide(far2, 2, 4), wide(far3, 2, 4)]
+        u = jnp.concatenate(bases, axis=0)
+        ut = u.T
+        left = jnp.concatenate([corner, side], axis=0)
+        right = jnp.concatenate([side.T, far], axis=0)
+        dense = dot3(dot3(ut, jnp.concatenate([left, right], axis=1)), u)
+        solved, schur = eliminate(dense, redundant)
+        schur_ref[...] = schur
+        wt = ut[redundant:] - dot3(solved.T, ut[:redundant])
+        for m in range(4):
+            w_ref[z ^ m] = wt[:, m * edge : (m + 1) * edge]
 
 
 def pack_kernel(place, diag, bases, full, half, shard):
@@ -196,12 +198,14 @@
 
 
 def near_first_kernel(place, count, w_ref, bases, n0, n1, n2, n3, schur, top, low, flipped, pair):
-    result = coupling(w_ref, [tall(n, 0) for n in (n0, n1, n2, n3)], [bases[j] for j in range(4)])
-    result = jnp.where(count[place[1] >> 1] > 0, result, 0.0)
-    half = top.shape[0]
-    top[...], low[...] = result[:half], result[half:]
-    pair[0], pair[1] = schur[...], result
-    flipped[...] = result.T
+    @pl.when(owns(place[1]))
+    def _():
+        result = coupling(w_ref, [tall(n, 0) for n in (n0, n1, n2, n3)], [bases[j] for j in range(4)])
+        result = jnp.where(count[place[1] >> 1] > 0, result, 0.0)
+        half = top.shape[0]
+        top[...], low[...] = result[:half], result[half:]
+        pair[0], pair[1] = schur[...], result
+        flipped[...] = result.T
 
 
 def owns(column):

time: 146 us -> 146 us (level)
  Pallas kernels: 56.1 us -> 39 us
  waiting for transfers between devices: 43.4 us -> 60.2 us
    pallas_call x8, Pallas kernels: 53.4 us -> 36.3 us  [call(): pl.pallas_call(kernel, out_shape=shapes, in_specs=specs, out_specs=[vmem]...]
    ppermute x9, waiting for transfers between devices: 30 us -> 46.8 us  [to_owner(): lax.ppermute(x, both, [(r * n_col + (z ^ j), r * n_col + z) for r, z in o...]
  transfers between devices with their start and end apart: 24 -> 24, of which waited for: 6 -> 6; matrix products, arithmetic and copies ran while one was open for 1% -> 1% of each run, Pallas kernels for 35% -> 24%
where the time goes in v8:
time: 146 us; the launch traced here: 145 us
  waiting for transfers between devices  60.2 us (41%)
  starting transfers between devices  40.7 us (28%)
  Pallas kernels  39 us (27%)
  local copies, waits for them, and re-layouts  3.78 us (3%)
    ppermute x9, waiting for transfers between devices, to_owner(): lax.ppermute(x, both, [(r * n_col + (z ^ j), r * n_col + z) for r, z in o...  46.8 us
    pallas_call x8, Pallas kernels, call(): pl.pallas_call(kernel, out_shape=shapes, in_specs=specs, out_specs=[vmem]...  36.3 us
    ppermute x9, starting transfers between devices, to_owner(): lax.ppermute(x, both, [(r * n_col + (z ^ j), r * n_col + z) for r, z in o...  22.1 us
    ppermute x4, waiting for transfers between devices, across(): return lax.ppermute(x, 'row', [(r, r ^ bit) for r in range(n_row)])  10.2 us
    ppermute x4, starting transfers between devices, across(): return lax.ppermute(x, 'row', [(r, r ^ bit) for r in range(n_row)])  4.88 us
    ppermute x3, starting transfers between devices, from_head(): lax.ppermute(x, both, [(r * n_col + z, r * n_col + (z ^ j)) for r, z in h...  3.85 us
    ppermute x3, starting transfers between devices, from_neighbour(): lax.ppermute(x, both, [(r * n_col + (z ^ 1), r * n_col + z) for r, z in h...  3.85 us
    unnamed x33, local copies, waits for them, and re-layouts  3.76 us
  transfers between devices with their start and end apart: 24, of which 6 were waited for; matrix products, arithmetic and copies ran while one was open for 1% of the time, Pallas kernels for 24%

profile of v8, /device:TPU:0, one launch (start us, length us, event | category | flops | bytes accessed | tf_op | source)
XLA Modules:
  0.0 145.2 jit_solution(2231938925932437455)
XLA Ops:
  0.6 0.7 pad_add_fusion.place
  1.3 2.3 %shard_map.85 = (f32[8,128,128]{2,1,0:T(8,128)}, f32[6,128,128]{2,1,0:T(8,128)}, f32[2,128,256]{2,1,0:T(8,128)}) custom-call(s32[2]{0:T(128)} %pad_add_fusion.place, f32[2,512,128]{2,1,0:T(8,128)} %diag.1, f32[2,128,512]{2,1,0:T(8,128)} %bases.1), custom_call_target="tpu_custom_call" | custom-call | flops 2000000000 | bytes 2000000 | tf_op jit(solution)/shard_map/pallas_call | solution.py:298
  3.6 3.0 %collective-permute-start.7 = (f32[2,128,256]{2,1,0:T(8,128)}, f32[2,128,256]{2,1,0:T(8,128)S(1)}, u32[]{:S(2)}, u32[]{:S(2)}) collective-permute-start(f32[2,128,256]{2,1,0:T(8,128)} %get-tuple-element.43), channel_id=1, source_target_pairs={{0,8},{4,12},{8,0},{12,4},{16,24},{20,28},{24,16},{28,20},{1,9},{5... | collective-permute-start | bytes 786440 | tf_op jit(solution)/shard_map/ppermute | solution.py:344
  6.6 1.0 constant_dynamic-update-slice_fusion.1
  7.6 5.5 %collective-permute-done.7 = f32[2,128,256]{2,1,0:T(8,128)S(1)} collective-permute-done((f32[2,128,256]{2,1,0:T(8,128)}, f32[2,128,256]{2,1,0:T(8,128)S(1)}, u32[]{:S(2)}, u32[]{:S(2)}) %collective-permute-start.7) | collective-permute-done | bytes 262176 | tf_op jit(solution)/shard_map/ppermute | solution.py:344
  13.1 1.8 %collective-permute-start.8 = (f32[4,128,256]{2,1,0:T(8,128)S(1)}, f32[4,128,256]{2,1,0:T(8,128)S(1)}, u32[]{:S(2)}, u32[]{:S(2)}) collective-permute-start(f32[4,128,256]{2,1,0:T(8,128)S(1)} %constant_dynamic-update-slice_fusion.low0), channel_id=1, source_target_pairs={{0,16},{4,20},{8,24},{12,28},{16,0},{20,4},{24,8},{28,12},{1,17},{... | collective-permute-start | bytes 1572872 | tf_op jit(solution)/shard_map/ppermute | solution.py:344
  14.9 3.5 %collective-permute-start = (f32[8,128,128]{2,1,0:T(8,128)}, f32[8,128,128]{2,1,0:T(8,128)S(1)}, u32[]{:S(2)}, u32[]{:S(2)}) collective-permute-start(f32[8,128,128]{2,1,0:T(8,128)} %get-tuple-element.34.own), channel_id=1, source_target_pairs={{0,1},{3,2},{4,5},{7,6},{8,9},{11,10},{12,13},{15,14},{16,17},{19,... | collective-permute-start | bytes 1572872 | tf_op jit(solution)/shard_map/ppermute | solution.py:326
  18.4 2.3 %collective-permute-start.1 = (f32[6,128,128]{2,1,0:T(8,128)}, f32[6,128,128]{2,1,0:T(8,128)S(1)}, u32[]{:S(2)}, u32[]{:S(2)}) collective-permute-start(f32[6,128,128]{2,1,0:T(8,128)} %get-tuple-element.35), channel_id=1, source_target_pairs={{3,1},{0,2},{7,5},{4,6},{11,9},{8,10},{15,13},{12,14},{19,17},{16,... | collective-permute-start | bytes 1179656 | tf_op jit(solution)/shard_map/ppermute | solution.py:326
  20.8 0.7 collective-permute-start.2
  21.4 0.1 collective-permute-start.9
  21.5 4.7 %collective-permute-done.8.low1 = f32[4,128,256]{2,1,0:T(8,128)S(1)} collective-permute-done((f32[4,128,256]{2,1,0:T(8,128)S(1)}, f32[4,128,256]{2,1,0:T(8,128)S(1)}, u32[]{:S(2)}, u32[]{:S(2)}) %collective-permute-start.8) | collective-permute-done | bytes 524320 | tf_op jit(solution)/shard_map/ppermute | solution.py:344
  26.3 0.0 collective-permute-start.10
  26.3 4.2 %shard_map.88 = (f32[4,128,128]{2,1,0:T(8,128)}, f32[4,128,128]{2,1,0:T(8,128)}, f32[18,128,128]{2,1,0:T(8,128)}, f32[18,128,128]{2,1,0:T(8,128)}, f32[512,512]{1,0:T(8,128)}) custom-call(s32[2]{0:T(128)} %pad_add_fusion.place, f32[2,16,128,128]{3,2,1,0:T(8,128)} %bitcast.7, f32[512,512]{1,0:T(8,128)} %bitcast.8), custom_call_target="tpu_custom_call" | custom-call | flops 2000000000 | bytes 2000000 | tf_op jit(solution)/shard_map/pallas_call | solution.py:298
  30.5 6.7 %collective-permute-done.1.far2 = f32[6,128,128]{2,1,0:T(8,128)S(1)} collective-permute-done((f32[6,128,128]{2,1,0:T(8,128)}, f32[6,128,128]{2,1,0:T(8,128)S(1)}, u32[]{:S(2)}, u32[]{:S(2)}) %collective-permute-start.1) | collective-permute-done | bytes 393248 | tf_op jit(solution)/shard_map/ppermute | solution.py:326
  37.2 6.0 %collective-permute-start.4 = (f32[4,128,128]{2,1,0:T(8,128)}, f32[4,128,128]{2,1,0:T(8,128)}, u32[]{:S(2)}, u32[]{:S(2)}) collective-permute-start(f32[4,128,128]{2,1,0:T(8,128)} %get-tuple-element.40.n0), channel_id=1, source_target_pairs={{0,1},{3,2},{4,5},{7,6},{8,9},{11,10},{12,13},{15,14},{16,17},{19,... | collective-permute-start | bytes 786440 | tf_op jit(solution)/shard_map/ppermute | solution.py:326
  43.2 2.0 %collective-permute-start.5 = (f32[4,128,128]{2,1,0:T(8,128)}, f32[4,128,128]{2,1,0:T(8,128)}, u32[]{:S(2)}, u32[]{:S(2)}) collective-permute-start(f32[4,128,128]{2,1,0:T(8,128)} %get-tuple-element.41), channel_id=1, source_target_pairs={{3,1},{0,2},{7,5},{4,6},{11,9},{8,10},{15,13},{12,14},{19,17},{16,... | collective-permute-start | bytes 786440 | tf_op jit(solution)/shard_map/ppermute | solution.py:326
  45.2 1.4 collective-permute-start.6
  46.6 2.3 %shard_map.87 = f32[4,128,256]{2,1,0:T(8,128)} custom-call(s32[2]{0:T(128)} %pad_add_fusion.place, f32[8,128,128]{2,1,0:T(8,128)} %get-tuple-element.34.own, f32[8,128,128]{2,1,0:T(8,128)} %copy-done.7, f32[6,128,128]{2,1,0:T(8,128)} %copy-done.8, f32[6,128,128]{2,1,0:T(8,128)} %copy-done.9), custom_call_target="tpu_custom_call" | custom-call | flops 2000000000 | bytes 2000000 | tf_op jit(solution)/shard_map/pallas_call | solution.py:298
  48.9 1.4 collective-permute-start.3
  50.3 0.8 copy-done.3
  51.1 2.6 %shard_map.90 = (f32[18,128,128]{2,1,0:T(8,128)}, f32[18,128,128]{2,1,0:T(8,128)}) custom-call(s32[2]{0:T(128)} %pad_add_fusion.place, s32[2,4]{1,0:T(2,128)} %ids.1, f32[4,128,256]{2,1,0:T(8,128)} %copy-done, f32[4,128,256]{2,1,0:T(8,128)} %copy-done.1, f32[4,128,256]{2,1,0:T(8,128)} %copy-done.2, ...), custom_call_target="tpu_custom_call", output_to_operand_aliasing={{0}: (6, {}), {1}: (7, {})} | custom-call | tf_op jit(solution)/shard_map/pallas_call | solution.py:387
  53.8 2.5 %collective-permute-start.12 = (f32[18,128,128]{2,1,0:T(8,128)}, f32[18,128,128]{2,1,0:T(8,128)S(1)}, u32[]{:S(2)}, u32[]{:S(2)}) collective-permute-start(f32[18,128,128]{2,1,0:T(8,128)} %get-tuple-element.49), channel_id=1, source_target_pairs={{3,1},{0,2},{7,5},{4,6},{11,9},{8,10},{15,13},{12,14},{19,17},{16,... | collective-permute-start | bytes 3538952 | tf_op jit(solution)/shard_map/ppermute | solution.py:326
  56.2 0.7 collective-permute-start.13
  57.0 3.0 %collective-permute-start.11 = (f32[18,128,128]{2,1,0:T(8,128)}, f32[18,128,128]{2,1,0:T(8,128)S(1)}, u32[]{:S(2)}, u32[]{:S(2)}) collective-permute-start(f32[18,128,128]{2,1,0:T(8,128)} %get-tuple-element.48.refs_0_), channel_id=1, source_target_pairs={{0,1},{3,2},{4,5},{7,6},{8,9},{11,10},{12,13},{15,14},{16,17},{19,... | collective-permute-start | bytes 3538952 | tf_op jit(solution)/shard_map/ppermute | solution.py:326
  60.0 2.4 %shard_map.86 = (f32[4,256,128]{2,1,0:T(8,128)}, f32[256,256]{1,0:T(8,128)}) custom-call(s32[2]{0:T(128)} %pad_add_fusion.place, f32[8,128,128]{2,1,0:T(8,128)} %get-tuple-element.34.own, f32[8,128,128]{2,1,0:T(8,128)} %copy-done.7, f32[6,128,128]{2,1,0:T(8,128)} %copy-done.8, f32[6,128,128]{2,1,0:T(8,128)} %copy-done.9), custom_call_target="tpu_custom_call" | custom-call | flops 22000001024 | bytes 22000000 | tf_op jit(solution)/shard_map/pallas_call | solution.py:298
  62.4 1.3 collective-permute-start.17
  63.7 2.6 %shard_map.89 = (f32[128,256]{1,0:T(8,128)}, f32[128,256]{1,0:T(8,128)}, f32[256,256]{1,0:T(8,128)}, f32[2,256,256]{2,1,0:T(8,128)}) custom-call(s32[2]{0:T(128)} %pad_add_fusion.place, s32[2]{0:T(128)} %count.3, f32[4,256,128]{2,1,0:T(8,128)} %get-tuple-element.36.w_ref, f32[4,128,256]{2,1,0:T(8,128)} %collective-permute-done.3.bases, ...), custom_call_target="tpu_custom_call" | custom-call | flops 4000000000 | bytes 4000000 | tf_op jit(solution)/shard_map/pallas_call | solution.py:298
  66.3 1.3 collective-permute-start.20
  67.6 40.1 %collective-permute-done.11.refs_1_ = f32[18,128,128]{2,1,0:T(8,128)S(1)} collective-permute-done((f32[18,128,128]{2,1,0:T(8,128)}, f32[18,128,128]{2,1,0:T(8,128)S(1)}, u32[]{:S(2)}, u32[]{:S(2)}) %collective-permute-start.11) | collective-permute-done | bytes 1179680 | tf_op jit(solution)/shard_map/ppermute | solution.py:326
  107.7 1.3 collective-permute-start.18
  109.0 1.3 collective-permute-start.19
  110.3 1.0 copy-done.5
  111.3 2.5 %shard_map.91 = (f32[5,64,256]{2,1,0:T(8,128)}, f32[5,64,256]{2,1,0:T(8,128)}, f32[5,64,256]{2,1,0:T(8,128)}, f32[5,64,256]{2,1,0:T(8,128)}) custom-call(s32[2]{0:T(128)} %pad_add_fusion.place, s32[2]{0:T(128)} %count.3, f32[4,256,128]{2,1,0:T(8,128)} %get-tuple-element.36.w_ref, f32[256,256]{1,0:T(8,128)} %get-tuple-element.37.schur, ...), custom_call_target="tpu_custom_call" | custom-call | flops 7000000000 | bytes 7000000 | tf_op jit(solution)/shard_map/pallas_call | solution.py:298
  113.9 1.3 collective-permute-start.14
  115.2 1.3 collective-permute-start.15
  116.5 0.7 collective-permute-start.16
  117.2 17.9 %shard_map.92 = (f32[1,64,256]{2,1,0:T(8,128)}, f32[1,64,256]{2,1,0:T(8,128)}, f32[1,64,256]{2,1,0:T(8,128)}, f32[1,64,256]{2,1,0:T(8,128)}) custom-call(s32[2]{0:T(128)} %pad_add_fusion.place, f32[256,256]{1,0:T(8,128)} %collective-permute-done.17.diag, f32[128,256]{1,0:T(8,128)} %collective-permute-done.18.near0, ...), custom_call_target="tpu_custom_call" | custom-call | flops 20000000000 | bytes 20000000 | tf_op jit(solution)/shard_map/pallas_call | solution.py:298
  135.1 1.3 collective-permute-start.21
  136.3 1.3 collective-permute-start.22
  137.6 0.9 collective-permute-done.21.refs_5_
  138.5 1.3 collective-permute-start.23
  139.8 0.0 collective-permute-done.22.refs_6_
  139.9 2.2 %collective-permute-done.23.refs_7_ = f32[1,64,256]{2,1,0:T(8,128)S(1)} collective-permute-done((f32[1,64,256]{2,1,0:T(8,128)}, f32[1,64,256]{2,1,0:T(8,128)S(1)}, u32[]{:S(2)}, u32[]{:S(2)}) %collective-permute-start.23) | collective-permute-done | bytes 65568 | tf_op jit(solution)/shard_map/ppermute | solution.py:341
  142.1 0.6 copy-done.15
  142.7 0.1 copy-done.10
  142.8 0.1 copy-done.11
  142.9 0.1 copy-done.12
  143.0 2.2 %shard_map.93 = (f32[2,64,256]{2,1,0:T(8,128)}, f32[2,4,64,256]{3,2,1,0:T(8,128)}, f32[1,64,256]{2,1,0:T(8,128)}) custom-call(s32[2]{0:T(128)} %pad_add_fusion.place, f32[5,64,256]{2,1,0:T(8,128)} %get-tuple-element.50.refs_0_, f32[5,64,256]{2,1,0:T(8,128)} %copy-done.10, f32[5,64,256]{2,1,0:T(8,128)} %copy-done.11, f32[5,64,256]{2,1,0:T(8,128)} %copy-done.12, ...), custom_call_target="tpu_custom_call" | custom-call | flops 2000000000 | bytes 2000000 | tf_op jit(solution)/shard_map/pallas_call | solution.py:298
  (44 shorter events, 0.1 us)
Async XLA Ops:
  3.6 9.5 %collective-permute-start.7 = (f32[2,128,256]{2,1,0:T(8,128)}, f32[2,128,256]{2,1,0:T(8,128)S(1)}, u32[]{:S(2)}, u32[]{:S(2)}) collective-permute-start(f32[2,128,256]{2,1,0:T(8,128)} %get-tuple-element.43), channel_id=1, source_target_pairs={{0,8},{4,12},{8,0},{12,4},{16,24},{20,28},{24,16},{28,20},{1,9},{5... | collective-permute-start | bytes 786440 | tf_op jit(solution)/shard_map/ppermute | solution.py:344
  13.1 17.4 %copy-start = (f32[4,128,256]{2,1,0:T(8,128)}, f32[4,128,256]{2,1,0:T(8,128)S(1)}, u32[]{:S(2)}) copy-start(f32[4,128,256]{2,1,0:T(8,128)S(1)} %constant_dynamic-update-slice_fusion.low0) | copy-start | bytes 1572868
  13.1 13.2 %collective-permute-start.8 = (f32[4,128,256]{2,1,0:T(8,128)S(1)}, f32[4,128,256]{2,1,0:T(8,128)S(1)}, u32[]{:S(2)}, u32[]{:S(2)}) collective-permute-start(f32[4,128,256]{2,1,0:T(8,128)S(1)} %constant_dynamic-update-slice_fusion.low0), channel_id=1, source_target_pairs={{0,16},{4,20},{8,24},{12,28},{16,0},{20,4},{24,8},{28,12},{1,17},{... | collective-permute-start | bytes 1572872 | tf_op jit(solution)/shard_map/ppermute | solution.py:344
  14.9 22.3 %collective-permute-start = (f32[8,128,128]{2,1,0:T(8,128)}, f32[8,128,128]{2,1,0:T(8,128)S(1)}, u32[]{:S(2)}, u32[]{:S(2)}) collective-permute-start(f32[8,128,128]{2,1,0:T(8,128)} %get-tuple-element.34.own), channel_id=1, source_target_pairs={{0,1},{3,2},{4,5},{7,6},{8,9},{11,10},{12,13},{15,14},{16,17},{19,... | collective-permute-start | bytes 1572872 | tf_op jit(solution)/shard_map/ppermute | solution.py:326
  18.4 18.7 %collective-permute-start.1 = (f32[6,128,128]{2,1,0:T(8,128)}, f32[6,128,128]{2,1,0:T(8,128)S(1)}, u32[]{:S(2)}, u32[]{:S(2)}) collective-permute-start(f32[6,128,128]{2,1,0:T(8,128)} %get-tuple-element.35), channel_id=1, source_target_pairs={{3,1},{0,2},{7,5},{4,6},{11,9},{8,10},{15,13},{12,14},{19,17},{16,... | collective-permute-start | bytes 1179656 | tf_op jit(solution)/shard_map/ppermute | solution.py:326
  20.8 16.4 %collective-permute-start.2 = (f32[6,128,128]{2,1,0:T(8,128)}, f32[6,128,128]{2,1,0:T(8,128)S(1)}, u32[]{:S(2)}, u32[]{:S(2)}) collective-permute-start(f32[6,128,128]{2,1,0:T(8,128)} %get-tuple-element.35), channel_id=1, source_target_pairs={{2,1},{1,2},{6,5},{5,6},{10,9},{9,10},{14,13},{13,14},{18,17},{17,... | collective-permute-start | bytes 1179656 | tf_op jit(solution)/shard_map/ppermute | solution.py:326
  21.4 27.4 %collective-permute-start.9 = (f32[4,128,256]{2,1,0:T(8,128)S(1)}, f32[4,128,256]{2,1,0:T(8,128)S(1)}, u32[]{:S(2)}, u32[]{:S(2)}) collective-permute-start(f32[4,128,256]{2,1,0:T(8,128)S(1)} %constant_dynamic-update-slice_fusion.low0), channel_id=1, source_target_pairs={{0,4},{4,0},{8,12},{12,8},{16,20},{20,16},{24,28},{28,24},{1,5},{5... | collective-permute-start | bytes 1572872 | tf_op jit(solution)/shard_map/ppermute | solution.py:344
  26.3 4.2 %copy-start.1 = (f32[4,128,256]{2,1,0:T(8,128)}, f32[4,128,256]{2,1,0:T(8,128)S(1)}, u32[]{:S(2)}) copy-start(f32[4,128,256]{2,1,0:T(8,128)S(1)} %collective-permute-done.8.low1) | copy-start | bytes 1572868
  26.3 24.1 %collective-permute-start.10 = (f32[4,128,256]{2,1,0:T(8,128)S(1)}, f32[4,128,256]{2,1,0:T(8,128)S(1)}, u32[]{:S(2)}, u32[]{:S(2)}) collective-permute-start(f32[4,128,256]{2,1,0:T(8,128)S(1)} %collective-permute-done.8.low1), channel_id=1, source_target_pairs={{0,4},{4,0},{8,12},{12,8},{16,20},{20,16},{24,28},{28,24},{1,5},{5... | collective-permute-start | bytes 1572872 | tf_op jit(solution)/shard_map/ppermute | solution.py:344
  37.2 9.4 %copy-start.8 = (f32[6,128,128]{2,1,0:T(8,128)}, f32[6,128,128]{2,1,0:T(8,128)S(1)}, u32[]{:S(2)}) copy-start(f32[6,128,128]{2,1,0:T(8,128)S(1)} %collective-permute-done.1.far2) | copy-start | bytes 1179652
  37.2 9.4 %copy-start.9 = (f32[6,128,128]{2,1,0:T(8,128)}, f32[6,128,128]{2,1,0:T(8,128)S(1)}, u32[]{:S(2)}) copy-start(f32[6,128,128]{2,1,0:T(8,128)S(1)} %collective-permute-done.2.far3) | copy-start | bytes 1179652
  37.2 9.4 %copy-start.7 = (f32[8,128,128]{2,1,0:T(8,128)}, f32[8,128,128]{2,1,0:T(8,128)S(1)}, u32[]{:S(2)}) copy-start(f32[8,128,128]{2,1,0:T(8,128)S(1)} %collective-permute-done.near) | copy-start | bytes 1572868
  37.2 19.0 %collective-permute-start.4 = (f32[4,128,128]{2,1,0:T(8,128)}, f32[4,128,128]{2,1,0:T(8,128)}, u32[]{:S(2)}, u32[]{:S(2)}) collective-permute-start(f32[4,128,128]{2,1,0:T(8,128)} %get-tuple-element.40.n0), channel_id=1, source_target_pairs={{0,1},{3,2},{4,5},{7,6},{8,9},{11,10},{12,13},{15,14},{16,17},{19,... | collective-permute-start | bytes 786440 | tf_op jit(solution)/shard_map/ppermute | solution.py:326
  43.2 13.8 %collective-permute-start.5 = (f32[4,128,128]{2,1,0:T(8,128)}, f32[4,128,128]{2,1,0:T(8,128)}, u32[]{:S(2)}, u32[]{:S(2)}) collective-permute-start(f32[4,128,128]{2,1,0:T(8,128)} %get-tuple-element.41), channel_id=1, source_target_pairs={{3,1},{0,2},{7,5},{4,6},{11,9},{8,10},{15,13},{12,14},{19,17},{16,... | collective-permute-start | bytes 786440 | tf_op jit(solution)/shard_map/ppermute | solution.py:326
  45.2 17.2 %collective-permute-start.6 = (f32[4,128,128]{2,1,0:T(8,128)}, f32[4,128,128]{2,1,0:T(8,128)}, u32[]{:S(2)}, u32[]{:S(2)}) collective-permute-start(f32[4,128,128]{2,1,0:T(8,128)} %get-tuple-element.41), channel_id=1, source_target_pairs={{2,1},{1,2},{6,5},{5,6},{10,9},{9,10},{14,13},{13,14},{18,17},{17,... | collective-permute-start | bytes 786440 | tf_op jit(solution)/shard_map/ppermute | solution.py:326
  48.9 1.5 %copy-start.2 = (f32[4,128,256]{2,1,0:T(8,128)}, f32[4,128,256]{2,1,0:T(8,128)S(1)}, u32[]{:S(2)}) copy-start(f32[4,128,256]{2,1,0:T(8,128)S(1)} %collective-permute-done.9.high0) | copy-start | bytes 1572868
  48.9 14.8 %collective-permute-start.3 = (f32[4,128,256]{2,1,0:T(8,128)}, f32[4,128,256]{2,1,0:T(8,128)}, u32[]{:S(2)}, u32[]{:S(2)}) collective-permute-start(f32[4,128,256]{2,1,0:T(8,128)} %shard_map.87), channel_id=1, source_target_pairs={{5,1},{6,2},{1,5},{2,6},{13,9},{14,10},{9,13},{10,14},{21,17},{22,... | collective-permute-start | bytes 1572872 | tf_op jit(solution)/shard_map/ppermute | solution.py:332
  50.3 0.8 copy-start.3
  53.8 55.2 %collective-permute-start.12 = (f32[18,128,128]{2,1,0:T(8,128)}, f32[18,128,128]{2,1,0:T(8,128)S(1)}, u32[]{:S(2)}, u32[]{:S(2)}) collective-permute-start(f32[18,128,128]{2,1,0:T(8,128)} %get-tuple-element.49), channel_id=1, source_target_pairs={{3,1},{0,2},{7,5},{4,6},{11,9},{8,10},{15,13},{12,14},{19,17},{16,... | collective-permute-start | bytes 3538952 | tf_op jit(solution)/shard_map/ppermute | solution.py:326
  56.2 54.0 %collective-permute-start.13 = (f32[18,128,128]{2,1,0:T(8,128)}, f32[18,128,128]{2,1,0:T(8,128)S(1)}, u32[]{:S(2)}, u32[]{:S(2)}) collective-permute-start(f32[18,128,128]{2,1,0:T(8,128)} %get-tuple-element.49), channel_id=1, source_target_pairs={{2,1},{1,2},{6,5},{5,6},{10,9},{9,10},{14,13},{13,14},{18,17},{17,... | collective-permute-start | bytes 3538952 | tf_op jit(solution)/shard_map/ppermute | solution.py:326
  57.0 50.7 %collective-permute-start.11 = (f32[18,128,128]{2,1,0:T(8,128)}, f32[18,128,128]{2,1,0:T(8,128)S(1)}, u32[]{:S(2)}, u32[]{:S(2)}) collective-permute-start(f32[18,128,128]{2,1,0:T(8,128)} %get-tuple-element.48.refs_0_), channel_id=1, source_target_pairs={{0,1},{3,2},{4,5},{7,6},{8,9},{11,10},{12,13},{15,14},{16,17},{19,... | collective-permute-start | bytes 3538952 | tf_op jit(solution)/shard_map/ppermute | solution.py:326
  62.4 52.7 %collective-permute-start.17 = (f32[256,256]{1,0:T(8,128)}, f32[256,256]{1,0:T(8,128)}, u32[]{:S(2)}, u32[]{:S(2)}) collective-permute-start(f32[256,256]{1,0:T(8,128)} %get-tuple-element.37.schur), channel_id=1, source_target_pairs={{1,0},{6,7},{9,8},{14,15},{17,16},{22,23},{25,24},{30,31}} | collective-permute-start | bytes 786440 | tf_op jit(solution)/shard_map/ppermute | solution.py:335
  66.3 50.9 %collective-permute-start.20 = (f32[2,256,256]{2,1,0:T(8,128)}, f32[2,256,256]{2,1,0:T(8,128)}, u32[]{:S(2)}, u32[]{:S(2)}) collective-permute-start(f32[2,256,256]{2,1,0:T(8,128)} %get-tuple-element.56), channel_id=1, source_target_pairs={{5,0},{2,7},{13,8},{10,15},{21,16},{18,23},{29,24},{26,31}} | collective-permute-start | bytes 1572872 | tf_op jit(solution)/shard_map/ppermute | solution.py:338
  107.7 2.6 %copy-start.6 = (f32[18,128,128]{2,1,0:T(8,128)}, f32[18,128,128]{2,1,0:T(8,128)S(1)}, u32[]{:S(2)}) copy-start(f32[18,128,128]{2,1,0:T(8,128)S(1)} %collective-permute-done.11.refs_1_) | copy-start | bytes 3538948
  107.7 8.8 %collective-permute-start.18 = (f32[128,256]{1,0:T(8,128)}, f32[128,256]{1,0:T(8,128)}, u32[]{:S(2)}, u32[]{:S(2)}) collective-permute-start(f32[128,256]{1,0:T(8,128)} %get-tuple-element.54), channel_id=1, source_target_pairs={{1,0},{6,7},{9,8},{14,15},{17,16},{22,23},{25,24},{30,31}} | collective-permute-start | bytes 393224 | tf_op jit(solution)/shard_map/ppermute | solution.py:335
  109.0 1.3 copy-start.4
  109.0 8.2 %collective-permute-start.19 = (f32[128,256]{1,0:T(8,128)}, f32[128,256]{1,0:T(8,128)}, u32[]{:S(2)}, u32[]{:S(2)}) collective-permute-start(f32[128,256]{1,0:T(8,128)} %get-tuple-element.55), channel_id=1, source_target_pairs={{1,0},{6,7},{9,8},{14,15},{17,16},{22,23},{25,24},{30,31}} | collective-permute-start | bytes 393224 | tf_op jit(solution)/shard_map/ppermute | solution.py:335
  110.3 1.0 copy-start.5
  113.9 28.2 %collective-permute-start.14 = (f32[5,64,256]{2,1,0:T(8,128)}, f32[5,64,256]{2,1,0:T(8,128)S(1)}, u32[]{:S(2)}, u32[]{:S(2)}) collective-permute-start(f32[5,64,256]{2,1,0:T(8,128)} %get-tuple-element.51), channel_id=1, source_target_pairs={{1,0},{2,3},{5,4},{6,7},{9,8},{10,11},{13,12},{14,15},{17,16},{18,... | collective-permute-start | bytes 983048 | tf_op jit(solution)/shard_map/ppermute | solution.py:329
  115.2 26.9 %collective-permute-start.15 = (f32[5,64,256]{2,1,0:T(8,128)}, f32[5,64,256]{2,1,0:T(8,128)S(1)}, u32[]{:S(2)}, u32[]{:S(2)}) collective-permute-start(f32[5,64,256]{2,1,0:T(8,128)} %get-tuple-element.52), channel_id=1, source_target_pairs={{1,3},{2,0},{5,7},{6,4},{9,11},{10,8},{13,15},{14,12},{17,19},{18,... | collective-permute-start | bytes 983048 | tf_op jit(solution)/shard_map/ppermute | solution.py:329
  116.5 25.6 %collective-permute-start.16 = (f32[5,64,256]{2,1,0:T(8,128)}, f32[5,64,256]{2,1,0:T(8,128)S(1)}, u32[]{:S(2)}, u32[]{:S(2)}) collective-permute-start(f32[5,64,256]{2,1,0:T(8,128)} %get-tuple-element.53), channel_id=1, source_target_pairs={{1,2},{2,1},{5,6},{6,5},{9,10},{10,9},{13,14},{14,13},{17,18},{18,... | collective-permute-start | bytes 983048 | tf_op jit(solution)/shard_map/ppermute | solution.py:329
  135.1 3.5 %collective-permute-start.21 = (f32[1,64,256]{2,1,0:T(8,128)}, f32[1,64,256]{2,1,0:T(8,128)S(1)}, u32[]{:S(2)}, u32[]{:S(2)}) collective-permute-start(f32[1,64,256]{2,1,0:T(8,128)} %get-tuple-element.59), channel_id=1, source_target_pairs={{0,1},{7,6},{8,9},{15,14},{16,17},{23,22},{24,25},{31,30}} | collective-permute-start | bytes 196616 | tf_op jit(solution)/shard_map/ppermute | solution.py:341
  136.3 3.5 %collective-permute-start.22 = (f32[1,64,256]{2,1,0:T(8,128)}, f32[1,64,256]{2,1,0:T(8,128)S(1)}, u32[]{:S(2)}, u32[]{:S(2)}) collective-permute-start(f32[1,64,256]{2,1,0:T(8,128)} %get-tuple-element.60), channel_id=1, source_target_pairs={{0,2},{7,5},{8,10},{15,13},{16,18},{23,21},{24,26},{31,29}} | collective-permute-start | bytes 196616 | tf_op jit(solution)/shard_map/ppermute | solution.py:341
  138.5 3.5 %copy-start.13 = (f32[1,64,256]{2,1,0:T(8,128)}, f32[1,64,256]{2,1,0:T(8,128)S(1)}, u32[]{:S(2)}) copy-start(f32[1,64,256]{2,1,0:T(8,128)S(1)} %collective-permute-done.21.refs_5_) | copy-start | bytes 196612
  138.5 3.5 %collective-permute-start.23 = (f32[1,64,256]{2,1,0:T(8,128)}, f32[1,64,256]{2,1,0:T(8,128)S(1)}, u32[]{:S(2)}, u32[]{:S(2)}) collective-permute-start(f32[1,64,256]{2,1,0:T(8,128)} %get-tuple-element.61), channel_id=1, source_target_pairs={{0,3},{7,4},{8,11},{15,12},{16,19},{23,20},{24,27},{31,28}} | collective-permute-start | bytes 196616 | tf_op jit(solution)/shard_map/ppermute | solution.py:341
  139.8 2.2 %copy-start.14 = (f32[1,64,256]{2,1,0:T(8,128)}, f32[1,64,256]{2,1,0:T(8,128)S(1)}, u32[]{:S(2)}) copy-start(f32[1,64,256]{2,1,0:T(8,128)S(1)} %collective-permute-done.22.refs_6_) | copy-start | bytes 196612
  142.0 0.6 copy-start.15
  142.0 0.7 copy-start.10
  142.1 0.8 copy-start.11
  142.1 1.0 copy-start.12
